TPU v7x, 128 devices: a whole 4x4x4 slice. The times are simulated.
128 devices in a mesh: dp: 8 (over y, x_lo), seq: 16 (over z, x_hi, core).
Axes of the slice: x: 4 (x_hi: 2, x_lo: 2; x = x_hi * 2 + x_lo), y: 4, z: 4, core: 2. Of those that a mesh axis runs over, the one named last changes fastest.
Arguments:
- hidden_in: bfloat16 [2, 8, 2048, 1024], P(None, 'dp', 'seq'), may hold values from -6 to 6
- seg_ids: int32 [2, 8, 2048], P(None, 'dp', 'seq'), may hold values from 0 to 11, never falling along the last dimension, each value on 1 to 1024 neighbouring positions
- decay_rates: float32 [8], replicated, may hold values from 0.00012207031 to 0.033
- grad_out: bfloat16 [2, 8, 2048, 1024], P(None, 'dp', 'seq'), may hold values from -6 to 6
- w_query: bfloat16 [1048576], P(('dp', 'seq')), may hold values from -0.1875 to 0.1875
- w_key: bfloat16 [1048576], P(('dp', 'seq')), may hold values from -0.1875 to 0.1875
- w_value: bfloat16 [1048576], P(('dp', 'seq')), may hold values from -0.1875 to 0.1875
- w_gate: bfloat16 [1048576], P(('dp', 'seq')), may hold values from -0.1875 to 0.1875
- w_output: bfloat16 [1048576], P(('dp', 'seq')), may hold values from -0.1875 to 0.1875
- w_left: bfloat16 [2883584], P(('dp', 'seq')), may hold values from -0.1875 to 0.1875
- w_right: bfloat16 [2883584], P(('dp', 'seq')), may hold values from -0.1875 to 0.1875
- w_down: bfloat16 [2883584], P(('dp', 'seq')), may hold values from -0.109375 to 0.109375
Outputs:
- activations: bfloat16 [2, 8, 2048, 1024], P(None, 'dp', 'seq')
- input_grad: float32 [2, 8, 2048, 1024], P(None, 'dp', 'seq')
- grad_query: float32 [1048576], P(('dp', 'seq'))
- grad_key: float32 [1048576], P(('dp', 'seq'))
- grad_value: float32 [1048576], P(('dp', 'seq'))
- grad_gate: float32 [1048576], P(('dp', 'seq'))
- grad_output: float32 [1048576], P(('dp', 'seq'))
- grad_left: float32 [2883584], P(('dp', 'seq'))
- grad_right: float32 [2883584], P(('dp', 'seq'))
- grad_down: float32 [2883584], P(('dp', 'seq'))
Inputs may be any that keep to these rules, and one draw needn't show every extreme that they name: `seg_ids`: along each sequence the document ids never fall; a document has 1 to 1024 tokens, and one of each sequence has exactly that many.
All inputs are finite; a program needn't handle non-finite values.
Results may differ from a plain program's by a relative error of at most 0.017.
Values may be sent and summed in bfloat16 or wider, within the bound.
A program may use at most 320 MiB of HBM per device.

v0:
```python
import jax
import jax.numpy as jnp
from jax import lax
from jax.sharding import PartitionSpec as P

D = 1024
H = 8
HD = 128
FF = 2816


EPSILON = 1e-06


def carried_in(shard, axis, join, neutral, backward):
    count = lax.axis_size(axis)
    place = lax.axis_index(axis)
    ahead = count - 1 - place if backward else place
    gathered = jax.tree.map(
        lambda a, kind: lax.all_gather(a.astype(kind), axis),
        shard,
        jax.tree.map(lambda a: jnp.bfloat16 if a.dtype == jnp.float32 else a.dtype, shard),
    )
    state = jax.tree.map(lambda a, e: jnp.zeros_like(a) + jnp.asarray(e, a.dtype), shard, neutral)

    def one(turn, state):
        source = count - 1 - turn if backward else turn
        return join(
            state,
            jax.tree.map(
                lambda a, own: lax.dynamic_index_in_dim(a, source, 0, False).astype(own.dtype),
                gathered,
                shard,
            ),
        )

    return lax.fori_loop(0, ahead, one, state)


def swish(values):
    return values * jax.nn.sigmoid(values)


def swish_slope(values):
    sigma = jax.nn.sigmoid(values)
    return sigma * (1.0 + values * (1.0 - sigma))


def rms_factor(values):
    return lax.rsqrt(jnp.mean(values * values, axis=-1, keepdims=True) + EPSILON)


def norm_back(upstream, normed, factor):
    return factor * (upstream - normed * jnp.mean(upstream * normed, axis=-1, keepdims=True))


def matmul(form, left_op, right_op):
    return jnp.einsum(form, left_op, right_op, preferred_element_type=jnp.float32)


def link(earlier, later):
    e_state, e_decay, e_near, e_far, e_whole = earlier
    l_state, l_decay, l_near, l_far, l_whole = later
    e_wild = e_near < 0.0
    l_wild = l_near < 0.0
    matching = (l_far == e_near) | e_wild | l_wild
    passes = jnp.where((l_whole > 0.5) & matching, 1.0, 0.0)
    merged = l_state + (passes[:, None] * l_decay)[:, :, None, None] * e_state
    near_tag = jnp.where(l_wild, e_near, l_near)
    far_tag = jnp.where(e_wild, l_far, e_far)
    whole_tag = jnp.where((e_whole > 0.5) & (l_whole > 0.5) & matching, 1.0, 0.0)
    return (merged, e_decay * l_decay, near_tag, far_tag, whole_tag)


def decay_tables(segments, decays, length):
    places = jnp.arange(length, dtype=jnp.float32)
    distance = places[:, None] - places[None, :]
    allowed = (distance >= 0.0)[None] & (segments[:, :, None] == segments[:, None, :])
    decay_mask = jnp.where(
        allowed[:, None],
        jnp.exp(-decays[None, :, None, None] * jnp.maximum(distance, 0.0)[None, None]),
        0.0,
    )
    return (places, decay_mask)


def chain_parts(segments, decays, length):
    first_tag = segments[:, 0].astype(jnp.float32)
    last_tag = segments[:, -1].astype(jnp.float32)
    whole_tag = jnp.where(segments[:, 0] == segments[:, -1], 1.0, 0.0)
    passing = jnp.exp(-length * decays)[None]
    neutral_tag = -jnp.ones_like(first_tag)
    return (first_tag, last_tag, whole_tag, passing, neutral_tag)


def mix_forward(queries, key_rows, value_rows, segments, decays):
    length = queries.shape[1]
    places, decay_mask = decay_tables(segments, decays, length)
    scores = matmul("sihd,sjhd->shij", queries, key_rows)
    weighted = (scores * decay_mask).astype(jnp.bfloat16)
    within = matmul("shij,sjhe->sihe", weighted, value_rows)
    keeping = (
        jnp.exp(-(length - 1.0 - places)[None, :, None] * decays[None, None, :])
        * jnp.where(segments == segments[:, -1:], 1.0, 0.0)[:, :, None]
    )
    local_state = jnp.einsum(
        "sjhd,sjhe->shde",
        key_rows.astype(jnp.float32) * keeping[..., None],
        value_rows.astype(jnp.float32),
        precision=lax.Precision.HIGHEST,
    )
    first_tag, last_tag, whole_tag, passing, neutral_tag = chain_parts(segments, decays, length)
    neutral = (
        jnp.zeros_like(local_state),
        jnp.ones_like(passing),
        neutral_tag,
        neutral_tag,
        jnp.ones_like(first_tag),
    )
    carried, carried_decay, boundary, far_seen, whole_seen = carried_in(
        (local_state, passing, last_tag, first_tag, whole_tag), "seq", link, neutral, False
    )
    reaching = (
        jnp.exp(-(places + 1.0)[None, :, None] * decays[None, None, :])
        * jnp.where(segments.astype(jnp.float32) == boundary[:, None], 1.0, 0.0)[:, :, None]
    )
    crossed = matmul("sihd,shde->sihe", queries, carried.astype(jnp.bfloat16)) * reaching[..., None]
    return (within + crossed, (weighted, decay_mask, carried, reaching))


def mix_backward(queries, key_rows, value_rows, d_mixed, saved, segments, decays):
    weighted, decay_mask, carried, reaching = saved
    length = queries.shape[1]
    places = jnp.arange(length, dtype=jnp.float32)
    d_weighted = matmul("sihe,sjhe->shij", d_mixed, value_rows)
    d_scores = (d_weighted * decay_mask).astype(jnp.bfloat16)
    d_query = matmul("shij,sjhd->sihd", d_scores, key_rows)
    d_query = (
        d_query
        + matmul("sihe,shde->sihd", d_mixed, carried.astype(jnp.bfloat16)) * reaching[..., None]
    )
    d_key = matmul("shij,sihd->sjhd", d_scores, queries)
    d_value = matmul("shij,sihe->sjhe", weighted, d_mixed)
    opening = (
        jnp.exp(-(places + 1.0)[None, :, None] * decays[None, None, :])
        * jnp.where(segments == segments[:, :1], 1.0, 0.0)[:, :, None]
    )
    back_local = jnp.einsum(
        "sihd,sihe->shde",
        queries.astype(jnp.float32) * opening[..., None],
        d_mixed.astype(jnp.float32),
        precision=lax.Precision.HIGHEST,
    )
    first_tag, last_tag, whole_tag, passing, neutral_tag = chain_parts(segments, decays, length)
    neutral = (
        jnp.zeros_like(back_local),
        jnp.ones_like(passing),
        neutral_tag,
        neutral_tag,
        jnp.ones_like(first_tag),
    )
    reverse, reverse_decay, reverse_tag, far_seen, whole_seen = carried_in(
        (back_local, passing, first_tag, last_tag, whole_tag), "seq", link, neutral, True
    )
    keeping = (
        jnp.exp(-(length - 1.0 - places)[None, :, None] * decays[None, None, :])
        * jnp.where(segments.astype(jnp.float32) == reverse_tag[:, None], 1.0, 0.0)[:, :, None]
    )
    reverse_low = reverse.astype(jnp.bfloat16)
    d_key = d_key + matmul("sjhe,shde->sjhd", value_rows, reverse_low) * keeping[..., None]
    d_value = d_value + matmul("sjhd,shde->sjhe", key_rows, reverse_low) * keeping[..., None]
    return (d_query, d_key, d_value)


def on_device(
    hidden_in,
    seg_ids,
    decay_rates,
    grad_out,
    w_query,
    w_key,
    w_value,
    w_gate,
    w_output,
    w_left,
    w_right,
    w_down,
):
    shapes = ((D, D), (D, D), (D, D), (D, D), (D, D), (D, FF), (D, FF), (FF, D))

    def unflatten(pieces):
        return tuple((piece.reshape(target) for piece, target in zip(pieces, shapes)))

    totals = tuple(
        (
            jnp.zeros(piece.shape, jnp.float32)
            for piece in (w_query, w_key, w_value, w_gate, w_output, w_left, w_right, w_down)
        )
    )
    seq_count = hidden_in.shape[1]
    length = hidden_in.shape[2]
    results = []
    input_grads = []
    for micro in range(hidden_in.shape[0]):
        forward_w = unflatten(
            (
                lax.all_gather(w_query, ("dp", "seq"), axis=0, tiled=True),
                lax.all_gather(w_key, ("dp", "seq"), axis=0, tiled=True),
                lax.all_gather(w_value, ("dp", "seq"), axis=0, tiled=True),
                lax.all_gather(w_gate, ("dp", "seq"), axis=0, tiled=True),
                lax.all_gather(w_output, ("dp", "seq"), axis=0, tiled=True),
                lax.all_gather(w_left, ("dp", "seq"), axis=0, tiled=True),
                lax.all_gather(w_right, ("dp", "seq"), axis=0, tiled=True),
                lax.all_gather(w_down, ("dp", "seq"), axis=0, tiled=True),
            )
        )
        m_query, m_key, m_value, m_gate, m_output, m_left, m_right, m_down = forward_w
        segments = seg_ids[micro]
        inputs = hidden_in[micro].reshape(-1, D).astype(jnp.float32)
        factor_in = rms_factor(inputs)
        normed_in = inputs * factor_in
        first_in = normed_in.astype(jnp.bfloat16)
        q_pre = matmul("rd,de->re", first_in, m_query)
        k_pre = matmul("rd,de->re", first_in, m_key)
        v_pre = matmul("rd,de->re", first_in, m_value)
        gate = matmul("rd,de->re", first_in, m_gate)
        queries = swish(q_pre).astype(jnp.bfloat16).reshape(seq_count, length, H, HD)
        key_rows = swish(k_pre).astype(jnp.bfloat16).reshape(seq_count, length, H, HD)
        value_rows = v_pre.astype(jnp.bfloat16).reshape(seq_count, length, H, HD)
        mixed, saved = mix_forward(queries, key_rows, value_rows, segments, decay_rates)
        mixed = mixed.reshape(-1, D)
        factor_mix = rms_factor(mixed)
        normed_mix = mixed * factor_mix
        gated = (normed_mix * gate).astype(jnp.bfloat16)
        resid = inputs + matmul("rd,de->re", gated, m_output)
        factor_res = rms_factor(resid)
        normed_res = resid * factor_res
        second = normed_res.astype(jnp.bfloat16)
        left_proj = matmul("rd,df->rf", second, m_left)
        right_proj = matmul("rd,df->rf", second, m_right)
        product = (left_proj * right_proj).astype(jnp.bfloat16)
        result = resid + matmul("rf,fd->rd", product, m_down)
        results.append(result.astype(jnp.bfloat16).reshape(seq_count, length, D))
        backward_w = unflatten(
            (
                lax.all_gather(w_query, ("dp", "seq"), axis=0, tiled=True),
                lax.all_gather(w_key, ("dp", "seq"), axis=0, tiled=True),
                lax.all_gather(w_value, ("dp", "seq"), axis=0, tiled=True),
                lax.all_gather(w_gate, ("dp", "seq"), axis=0, tiled=True),
                lax.all_gather(w_output, ("dp", "seq"), axis=0, tiled=True),
                lax.all_gather(w_left, ("dp", "seq"), axis=0, tiled=True),
                lax.all_gather(w_right, ("dp", "seq"), axis=0, tiled=True),
                lax.all_gather(w_down, ("dp", "seq"), axis=0, tiled=True),
            )
        )
        b_query, b_key, b_value, b_gate, b_output, b_left, b_right, b_down = backward_w
        cotangent = grad_out[micro].reshape(-1, D).astype(jnp.float32)
        d_branch = cotangent.astype(jnp.bfloat16)
        g_down = matmul("rf,rd->fd", product, d_branch)
        d_prod = matmul("rd,fd->rf", d_branch, b_down)
        d_left = (d_prod * right_proj).astype(jnp.bfloat16)
        d_right = (d_prod * left_proj).astype(jnp.bfloat16)
        g_left = matmul("rd,rf->df", second, d_left)
        g_right = matmul("rd,rf->df", second, d_right)
        d_second = matmul("rf,df->rd", d_left, b_left) + matmul("rf,df->rd", d_right, b_right)
        d_resid = cotangent + norm_back(d_second, normed_res, factor_res)
        d_attn = d_resid.astype(jnp.bfloat16)
        g_output = matmul("rd,re->de", gated, d_attn)
        d_gated = matmul("re,de->rd", d_attn, b_output)
        d_gate = (d_gated * normed_mix).astype(jnp.bfloat16)
        d_mixed = (
            norm_back(d_gated * gate, normed_mix, factor_mix)
            .astype(jnp.bfloat16)
            .reshape(seq_count, length, H, HD)
        )
        d_query, d_key, d_value = mix_backward(
            queries, key_rows, value_rows, d_mixed, saved, segments, decay_rates
        )
        d_qpre = (d_query.reshape(-1, D) * swish_slope(q_pre)).astype(jnp.bfloat16)
        d_kpre = (d_key.reshape(-1, D) * swish_slope(k_pre)).astype(jnp.bfloat16)
        d_vpre = d_value.reshape(-1, D).astype(jnp.bfloat16)
        g_query = matmul("rd,re->de", first_in, d_qpre)
        g_key = matmul("rd,re->de", first_in, d_kpre)
        g_value = matmul("rd,re->de", first_in, d_vpre)
        g_gate = matmul("rd,re->de", first_in, d_gate)
        d_first = matmul("re,de->rd", d_qpre, b_query) + matmul("re,de->rd", d_kpre, b_key)
        d_first = (
            d_first + matmul("re,de->rd", d_vpre, b_value) + matmul("re,de->rd", d_gate, b_gate)
        )
        d_inputs = d_resid + norm_back(d_first, normed_in, factor_in)
        input_grads.append(d_inputs.reshape(seq_count, length, D))
        shares = (
            lax.psum_scatter(g_query.reshape(-1), ("dp", "seq"), scatter_dimension=0, tiled=True),
            lax.psum_scatter(g_key.reshape(-1), ("dp", "seq"), scatter_dimension=0, tiled=True),
            lax.psum_scatter(g_value.reshape(-1), ("dp", "seq"), scatter_dimension=0, tiled=True),
            lax.psum_scatter(g_gate.reshape(-1), ("dp", "seq"), scatter_dimension=0, tiled=True),
            lax.psum_scatter(g_output.reshape(-1), ("dp", "seq"), scatter_dimension=0, tiled=True),
            lax.psum_scatter(g_left.reshape(-1), ("dp", "seq"), scatter_dimension=0, tiled=True),
            lax.psum_scatter(g_right.reshape(-1), ("dp", "seq"), scatter_dimension=0, tiled=True),
            lax.psum_scatter(g_down.reshape(-1), ("dp", "seq"), scatter_dimension=0, tiled=True),
        )
        totals = tuple((total + share for total, share in zip(totals, shares)))
    return (jnp.stack(results), jnp.stack(input_grads)) + tuple(totals)


def solution(mesh):
    in_specs = (
        P(None, "dp", "seq", None),
        P(None, "dp", "seq"),
        P(),
        P(None, "dp", "seq", None),
        P(("dp", "seq")),
        P(("dp", "seq")),
        P(("dp", "seq")),
        P(("dp", "seq")),
        P(("dp", "seq")),
        P(("dp", "seq")),
        P(("dp", "seq")),
        P(("dp", "seq")),
    )
    out_specs = (
        P(None, "dp", "seq", None),
        P(None, "dp", "seq", None),
        P(("dp", "seq")),
        P(("dp", "seq")),
        P(("dp", "seq")),
        P(("dp", "seq")),
        P(("dp", "seq")),
        P(("dp", "seq")),
        P(("dp", "seq")),
        P(("dp", "seq")),
    )
    return jax.shard_map(
        on_device, mesh=mesh, in_specs=in_specs, out_specs=out_specs, check_vma=False
    )
```

profile of v0, /device:TPU:1, one launch (start us, length us, event | category | flops | bytes accessed | tf_op | source)
XLA Modules:
  0.0 2589.6 jit_solution(2742279729521109118)
XLA Ops:
  19.1 187.9 %all-gather.22.cloned.1.call-done = bf16[1048576]{0:T(1024)(128)(2,1)} async-done(((bf16[8192]{0:T(1024)(128)(2,1)}), bf16[1048576]{0:T(1024)(128)(2,1)}) %all-gather.22.cloned.1.call-update) | async-done | bytes 2097168 | tf_op jit(solution)/shard_map/all_gather | solution.py:208
  211.6 189.9 %all-gather.18.cloned.1.call-done = bf16[1048576]{0:T(1024)(128)(2,1)} async-done(((bf16[8192]{0:T(1024)(128)(2,1)}), bf16[1048576]{0:T(1024)(128)(2,1)}) %all-gather.18.cloned.1.call-update) | async-done | bytes 2097168 | tf_op jit(solution)/shard_map/all_gather | solution.py:209
  424.5 34.2 %all-reduce.16 = (bf16[16]{0:T(256)(128)(2,1)S(1)}, bf16[16]{0:T(256)(128)(2,1)S(1)}, bf16[16]{0:T(256)(128)(2,1)S(1)}, bf16[128]{0:T(256)(128)(2,1)S(1)}, bf16[...) all-reduce(bf16[16]{0:T(256)(128)(2,1)S(1)} %dynamic-update-slice.4, ...), channel_id=1, replica_groups=mesh['dp'=8,'seq'=16] {'seq'}, use_global_device_ids=true, to_apply=%add.4 | all-reduce | flops 224 | bytes 896
  459.4 136.7 %all-gather.20.cloned.1.call-done = bf16[1048576]{0:T(1024)(128)(2,1)} async-done(((bf16[8192]{0:T(1024)(128)(2,1)}), bf16[1048576]{0:T(1024)(128)(2,1)}) %all-gather.20.cloned.1.call-update) | async-done | bytes 2097168 | tf_op jit(solution)/shard_map/all_gather | solution.py:207
  603.2 187.3 %all-gather.24.cloned.1.call-done = bf16[1048576]{0:T(1024)(128)(2,1)} async-done(((bf16[8192]{0:T(1024)(128)(2,1)}), bf16[1048576]{0:T(1024)(128)(2,1)}) %all-gather.24.cloned.1.call-update) | async-done | bytes 2097168 | tf_op jit(solution)/shard_map/all_gather | solution.py:210
  794.7 190.2 %all-gather.26.cloned.1.call-done = bf16[1048576]{0:T(1024)(128)(2,1)} async-done(((bf16[8192]{0:T(1024)(128)(2,1)}), bf16[1048576]{0:T(1024)(128)(2,1)}) %all-gather.26.cloned.1.call-update) | async-done | bytes 2097168 | tf_op jit(solution)/shard_map/all_gather | solution.py:211
  991.2 194.4 %all-gather.28.cloned.1.call-done = bf16[2883584]{0:T(1024)(128)(2,1)} async-done(((bf16[22528]{0:T(1024)(128)(2,1)}), bf16[2883584]{0:T(1024)(128)(2,1)}) %all-gather.28.cloned.1.call-update) | async-done | bytes 5767184 | tf_op jit(solution)/shard_map/all_gather | solution.py:212
  1185.6 11.5 reshape.1374
  1197.2 189.4 %all-gather.30.cloned.1.call-done = bf16[2883584]{0:T(1024)(128)(2,1)} async-done(((bf16[22528]{0:T(1024)(128)(2,1)}), bf16[2883584]{0:T(1024)(128)(2,1)}) %all-gather.30.cloned.1.call-update) | async-done | bytes 5767184 | tf_op jit(solution)/shard_map/all_gather | solution.py:213
  1386.6 11.5 reshape.1375
  1398.1 189.3 %all-gather.32.cloned.1.call-done = bf16[2883584]{0:T(1024)(128)(2,1)} async-done(((bf16[22528]{0:T(1024)(128)(2,1)}), bf16[2883584]{0:T(1024)(128)(2,1)}) %all-gather.32.cloned.1.call-update) | async-done | bytes 5767184 | tf_op jit(solution)/shard_map/all_gather | solution.py:214
  1587.4 9.7 reshape.1376
  1597.1 48.0 %all-gather.34.cloned.1.call-done = bf16[128,128,128]{2,1,0:T(8,128)(2,1)} async-done(((bf16[8,128,128]{2,1,0:T(8,128)(2,1)}), bf16[128,128,128]{2,1,0:T(8,128)(2,1)}) %all-gather.34.cloned.1.call-update) | async-done | bytes 4194320 | tf_op jit(solution)/shard_map/all_gather | solution.py:20
  1650.8 49.9 %all-gather.36.cloned.1.call-done = bf16[128,128,128]{2,1,0:T(8,128)(2,1)} async-done(((bf16[8,128,128]{2,1,0:T(8,128)(2,1)}), bf16[128,128,128]{2,1,0:T(8,128)(2,1)}) %all-gather.36.cloned.1.call-update) | async-done | bytes 4194320 | tf_op jit(solution)/shard_map/all_gather | solution.py:20
  1774.2 147.6 %all-gather.38.cloned.1.call-done = bf16[128,128,128]{2,1,0:T(8,128)(2,1)} async-done(((bf16[8,128,128]{2,1,0:T(8,128)(2,1)}), bf16[128,128,128]{2,1,0:T(8,128)(2,1)}) %all-gather.38.cloned.1.call-update) | async-done | bytes 4194320 | tf_op jit(solution)/shard_map/all_gather | solution.py:20
  1921.8 77.3 %while.70 = (s32[]{:T(128)}, f32[1,8,128,128]{3,2,1,0:T(8,128)S(1)}, f32[1]{0:T(128)}, s32[]{:T(128)}, bf16[16,1,8,128,128]{4,3,2,1,0:T(8,128)(2,1)}, /*index=5*...) while((s32[]{:T(128)}, ...), condition=%wide.region_13.14_spmd, body=%wide.region_12.13_spmd.sunk | while | flops 393248 | bytes 1311082 | solution.py:37
  2025.6 6.4 convolution_add_fusion.1
  2032.0 12.6 reshape.1430
  2047.5 5.9 convolution_add_fusion
  2053.4 12.8 reshape.1431
  2067.9 5.9 add_bitcast_fusion
  2073.9 11.4 copy.195
  2085.3 69.4 %while.71 = (s32[]{:T(128)}, f32[1,8,128,128]{3,2,1,0:T(8,128)S(1)}, f32[1]{0:T(128)}, s32[]{:T(128)}, bf16[16,1,8,128,128]{4,3,2,1,0:T(8,128)(2,1)}, /*index=5*...) while((s32[]{:T(128)}, ...), condition=%wide.region_18.19_spmd, body=%wide.region_17.18_spmd.sunk | while | flops 393248 | bytes 1311082 | solution.py:37
  2200.4 371.0 %all-reduce.19.cloned.1.call-done = (f32[1048576]{0:T(1024)}, f32[1048576]{0:T(1024)}, f32[1048576]{0:T(1024)}, f32[1048576]{0:T(1024)}, f32[1048576]{0:T(1024)}...) async-done(((f32[1048576]{0:T(1024)}, f32[1048576]{0:T(1024)}, f32[1048576]{0:T(1024)}, f32[1048576]{0:T(1024)}, f32[1048576]{0:T(1024)}, ...) | async-done | bytes 55574544
  (528 shorter events, 285.2 us)
Async XLA Ops:
  7.2 202.6 %copy-start.4 = (bf16[2,1,128,1024]{3,2,1,0:T(8,128)(2,1)S(1)}, bf16[2,1,128,1024]{3,2,1,0:T(8,128)(2,1)}, u32[]{:S(2)}) copy-start(bf16[2,1,128,1024]{3,2,1,0:T(8,128)(2,1)} %param.20) | copy-start | bytes 1572868
  7.2 199.8 %all-gather.22.cloned.1.call-start = ((), (), s32[]{:S(2)}) async-start(), calls=%async_computation.2 | async-start | bytes 2113536 | tf_op jit(solution)/shard_map/all_gather | solution.py:208
  7.9 393.6 %all-gather.18.cloned.1.call-start = ((), (), s32[]{:S(2)}) async-start(), calls=%async_computation | async-start | bytes 2113536 | tf_op jit(solution)/shard_map/all_gather | solution.py:209
  8.7 587.4 %all-gather.20.cloned.1.call-start = ((), (), s32[]{:S(2)}) async-start(), calls=%async_computation.1 | async-start | bytes 2113536 | tf_op jit(solution)/shard_map/all_gather | solution.py:207
  9.4 781.1 %all-gather.24.cloned.1.call-start = ((), (), s32[]{:S(2)}) async-start(), calls=%async_computation.3 | async-start | bytes 2113536 | tf_op jit(solution)/shard_map/all_gather | solution.py:210
  10.0 974.9 %all-gather.26.cloned.1.call-start = ((), (), s32[]{:S(2)}) async-start(), calls=%async_computation.4 | async-start | bytes 2113536 | tf_op jit(solution)/shard_map/all_gather | solution.py:211
  10.6 1175.1 %all-gather.28.cloned.1.call-start = ((), (), s32[]{:S(2)}) async-start(), calls=%async_computation.5 | async-start | bytes 5812224 | tf_op jit(solution)/shard_map/all_gather | solution.py:212
  11.1 1375.4 %all-gather.30.cloned.1.call-start = ((), (), s32[]{:S(2)}) async-start(), calls=%async_computation.6 | async-start | bytes 5812224 | tf_op jit(solution)/shard_map/all_gather | solution.py:213
  11.9 1575.6 %all-gather.32.cloned.1.call-start = ((), (), s32[]{:S(2)}) async-start(), calls=%async_computation.7 | async-start | bytes 5812224 | tf_op jit(solution)/shard_map/all_gather | solution.py:214
  12.6 1632.5 %all-gather.34.cloned.1.call-start = ((), (), s32[]{:S(2)}) async-start(), calls=%async_computation.8 | async-start | bytes 4456448 | tf_op jit(solution)/shard_map/all_gather | solution.py:20
  12.7 198.6 %copy-start.89 = (f32[128]{0:T(128)}, f32[128]{0:T(128)S(1)}, u32[]{:S(2)}) copy-start(f32[128]{0:T(128)S(1)} %subtract_negate_fusion) | copy-start | bytes 1540
  211.3 778.9 %copy-start.73 = (bf16[128,1024]{1,0:T(8,128)(2,1)}, bf16[128,1024]{1,0:T(8,128)(2,1)S(1)}, u32[]{:S(2)}) copy-start(bf16[128,1024]{1,0:T(8,128)(2,1)S(1)} %get-tuple-element.727) | copy-start | bytes 786436
  211.6 198.2 %copy-start.49 = (bf16[128,8,128]{0,2,1:T(8,128)(2,1)}, bf16[128,8,128]{0,2,1:T(8,128)(2,1)S(1)}, u32[]{:S(2)}) copy-start(bf16[128,8,128]{0,2,1:T(8,128)(2,1)S(1)} %copy.125) | copy-start | bytes 786436
  406.9 1293.8 %all-gather.36.cloned.1.call-start = ((), (), s32[]{:S(2)}) async-start(), calls=%async_computation.9 | async-start | bytes 4456448 | tf_op jit(solution)/shard_map/all_gather | solution.py:20
  413.2 1508.6 %all-gather.38.cloned.1.call-start = ((), (), s32[]{:S(2)}) async-start(), calls=%async_computation.10 | async-start | bytes 4456448 | tf_op jit(solution)/shard_map/all_gather | solution.py:20
  424.3 565.9 %copy-start.95 = (f32[8]{0:T(128)}, f32[8]{0:T(128)S(1)}, u32[]{:S(2)}) copy-start(f32[8]{0:T(128)S(1)} %get-tuple-element.719) | copy-start | bytes 100
  600.6 388.5 %copy-start.42 = (bf16[128,1024]{0,1:T(8,128)(2,1)}, bf16[128,1024]{0,1:T(8,128)(2,1)S(1)}, u32[]{:S(2)}) copy-start(bf16[128,1024]{0,1:T(8,128)(2,1)S(1)} %copy.181) | copy-start | bytes 786436
  603.2 1121.8 %copy-start.41 = (bf16[128,1024]{0,1:T(8,128)(2,1)}, bf16[128,1024]{0,1:T(8,128)(2,1)S(1)}, u32[]{:S(2)}) copy-start(bf16[128,1024]{0,1:T(8,128)(2,1)S(1)} %copy.180) | copy-start | bytes 786436
  603.2 385.9 %copy-start.75 = (bf16[128,1024]{1,0:T(8,128)(2,1)S(1)}, bf16[128,1024]{1,0:T(8,128)(2,1)}, u32[]{:S(2)}) copy-start(bf16[128,1024]{1,0:T(8,128)(2,1)} %copy-done.74) | copy-start | bytes 786436
  1770.0 315.2 %all-gather.40.cloned.1.call-start = ((), (), s32[]{:S(2)}) async-start(), calls=%async_computation.11 | async-start | bytes 4456448 | tf_op jit(solution)/shard_map/all_gather | solution.py:20
  1773.9 225.9 %copy-start.85 = (f32[8]{0:T(128)S(1)}, f32[8]{0:T(128)}, u32[]{:S(2)}) copy-start(f32[8]{0:T(128)} %param.22) | copy-start | bytes 100
  1774.0 226.7 %copy-start.43 = (bf16[128,1024]{0,1:T(8,128)(2,1)S(1)}, bf16[128,1024]{0,1:T(8,128)(2,1)}, u32[]{:S(2)}) copy-start(bf16[128,1024]{0,1:T(8,128)(2,1)} %copy-done.42) | copy-start | bytes 786436
  1774.1 229.2 %copy-start.39 = (bf16[128,1024]{0,1:T(8,128)(2,1)}, bf16[128,1024]{0,1:T(8,128)(2,1)S(1)}, u32[]{:S(2)}) copy-start(bf16[128,1024]{0,1:T(8,128)(2,1)S(1)} %copy.183) | copy-start | bytes 786436
  2002.0 569.4 %all-reduce.19.cloned.1.call-start = ((), (), s32[]{:S(2)}) async-start(), calls=%async_computation.12 | async-start | bytes 111149056
  (96 other events, 974.8 us)
Sparse Core Ops, SparseCore 0:
  9.7 197.1 all-gather.21
  208.7 192.7 all-gather.17
  403.2 192.8 all-gather.19
  597.7 192.8 all-gather.23
  792.1 192.7 all-gather.25
  986.5 199.0 all-gather.27
  1187.3 199.1 all-gather.29
  1388.3 199.1 all-gather.31
  1590.5 54.6 all-gather.33
  1647.5 53.1 all-gather.35
  1770.2 151.5 all-gather.37
  2002.1 57.2 all-gather.39
  2182.8 388.5 all-reduce.18
where the time goes:
time: 2600 us; the launch traced here: 2590 us
  waiting for transfers between devices  2090 us (80%)
  local copies, waits for them, and re-layouts  159 us (6%)
  matrix products  120 us (5%)
  loops' own time  78.5 us (3%)
  other arithmetic  77.6 us (3%)
  blocking collectives  34.2 us (1%)
  between operations  33.1 us (1%)
    unnamed x14, waiting for transfers between devices  376 us
    all_gather x4, waiting for transfers between devices, carried_in(): lax.all_gather(a.astype(kind), axis)  246 us
    all_gather x1, waiting for transfers between devices, on_device(): lax.all_gather(w_left, ('dp', 'seq'), axis=0, tiled=True)  194 us
    all_gather x1, waiting for transfers between devices, on_device(): lax.all_gather(w_output, ('dp', 'seq'), axis=0, tiled=True)  190 us
    all_gather x1, waiting for transfers between devices, on_device(): lax.all_gather(w_value, ('dp', 'seq'), axis=0, tiled=True)  190 us
    all_gather x1, waiting for transfers between devices, on_device(): lax.all_gather(w_right, ('dp', 'seq'), axis=0, tiled=True)  189 us
    all_gather x1, waiting for transfers between devices, on_device(): lax.all_gather(w_down, ('dp', 'seq'), axis=0, tiled=True)  189 us
    all_gather x1, waiting for transfers between devices, on_device(): lax.all_gather(w_key, ('dp', 'seq'), axis=0, tiled=True)  188 us
  transfers between devices with their start and end apart: 13, of which 12 were waited for; matrix products, arithmetic and copies ran while one was open for 7% of the time, Pallas kernels for 0%

commit v1 on v0

v1 whole, which is shorter than its diff:
```python
import functools
import jax, jax.numpy as jnp
from jax import lax
from jax.experimental import pallas as pl
from jax.experimental.pallas import tpu as pltpu
from jax.sharding import PartitionSpec as P

MESH = pl.DeviceIdType.MESH
RING = 4

UNITS = (
    (0, 0, 0, 13 * 128), (0, 1, 13 * 128, 26 * 128), (0, 2, 26 * 128, 32 * 128),
    (1, 2, 0, 8 * 128),
    (2, 0, 0, 22 * 128), (2, 1, 22 * 128, 44 * 128),
    (3, 2, 0, 176),
)
ORDERS = (("x", "y", "z"), ("y", "z", "x"), ("z", "x", "y"))
SPLIT_ROWS = (False, False, False, True)


def where_am_i():
    dp = lax.axis_index("dp")
    seq = lax.axis_index("seq")
    return {"x": (seq // 2 % 2) * 2 + dp % 2, "y": dp // 2, "z": seq // 4, "c": seq % 2}


def device(at):
    return (at["y"] * 2 + at["x"] % 2, at["z"] * 4 + (at["x"] // 2) * 2 + at["c"])


def moved(at, axis, by):
    out = dict(at)
    out[axis] = (at[axis] + by) % RING if axis != "c" else 1 - at[axis]
    return out


def block(ref, at, whole, lo, hi, rows):
    every = slice(None)
    pick = lambda axis, value: every if axis in whole else value
    span = pl.ds(lo, hi - lo)
    return ref.at[
        pick("y", at["y"]), pick("x", at["x"] % 2), pick("z", at["z"]), pick("x", at["x"] // 2), at["c"],
        span if rows else every, every if rows else span,
    ]


def middle(lo, hi, rows):
    grain = 8 if rows else 128
    return lo + ((hi - lo) // grain // 2) * grain


def ag_kernel(*refs):
    n_arr = 4
    ins, outs = refs[:n_arr], refs[n_arr:2 * n_arr]
    local_sem, send_sem, recv_sem, csend_sem, crecv_sem = refs[2 * n_arr:]
    me = where_am_i()
    barrier = pltpu.get_barrier_semaphore()
    partners = [moved(me, a, d) for a in "xyz" for d in (1, -1)] + [moved(me, "c", 1)]
    for other in partners:
        pl.semaphore_signal(barrier, inc=1, device_id=device(other), device_id_type=MESH)

    copies = []
    for i in range(n_arr):
        cp = pltpu.make_async_copy(
            ins[i], outs[i].at[me["y"], me["x"] % 2, me["z"], me["x"] // 2, me["c"]], local_sem.at[i])
        cp.start()
        copies.append(cp)
    pl.semaphore_wait(barrier, len(partners))
    for cp in copies:
        cp.wait()

    sends = []
    def send(src, u, slot, to):
        cp = pltpu.make_async_remote_copy(src_ref=src, dst_ref=src, send_sem=send_sem.at[u, slot],
            recv_sem=recv_sem.at[u, slot], device_id=device(to), device_id_type=MESH)
        cp.start()
        sends.append(cp)

    def got(ref, u, slot):
        pltpu.make_async_remote_copy(src_ref=ref, dst_ref=ref, send_sem=send_sem.at[u, slot],
            recv_sem=recv_sem.at[u, slot], device_id=device(me), device_id_type=MESH).wait_recv()

    def csend(src, u, slot):
        cp = pltpu.make_async_remote_copy(src_ref=src, dst_ref=src, send_sem=csend_sem.at[u, slot],
            recv_sem=crecv_sem.at[u, slot], device_id=device(moved(me, "c", 1)), device_id_type=MESH)
        cp.start()
        sends.append(cp)

    ctail = []
    for stage in range(3):
        for u, (i, s, lo, hi) in enumerate(UNITS):
            axis, whole = ORDERS[s][stage], ORDERS[s][:stage]
            mine = block(outs[i], me, whole, lo, hi, SPLIT_ROWS[i])
            send(mine, u, 4 * stage + 0, moved(me, axis, 1))
            send(mine, u, 4 * stage + 1, moved(me, axis, -1))
            if stage == 2:
                csend(mine, u, 0)
        for u, (i, s, lo, hi) in enumerate(UNITS):
            axis, whole = ORDERS[s][stage], ORDERS[s][:stage]
            rows = SPLIT_ROWS[i]
            mid = middle(lo, hi, rows)
            below, above = moved(me, axis, -1), moved(me, axis, 1)
            got(block(outs[i], below, whole, lo, hi, rows), u, 4 * stage + 0)
            send(block(outs[i], below, whole, lo, mid, rows), u, 4 * stage + 2, above)
            got(block(outs[i], above, whole, lo, hi, rows), u, 4 * stage + 1)
            send(block(outs[i], above, whole, mid, hi, rows), u, 4 * stage + 3, below)
            if stage == 2:
                csend(block(outs[i], below, whole, lo, hi, rows), u, 1)
                csend(block(outs[i], above, whole, lo, hi, rows), u, 2)
        for u, (i, s, lo, hi) in enumerate(UNITS):
            axis, whole = ORDERS[s][stage], ORDERS[s][:stage]
            rows = SPLIT_ROWS[i]
            mid = middle(lo, hi, rows)
            far = moved(me, axis, 2)
            got(block(outs[i], far, whole, lo, mid, rows), u, 4 * stage + 2)
            got(block(outs[i], far, whole, mid, hi, rows), u, 4 * stage + 3)
            if stage == 2:
                csend(block(outs[i], far, whole, lo, hi, rows), u, 3)
    sib = moved(me, "c", 1)
    for u, (i, s, lo, hi) in enumerate(UNITS):
        axis, whole = ORDERS[s][2], ORDERS[s][:2]
        for k, by in enumerate((0, -1, 1, 2)):
            ref = block(outs[i], moved(sib, axis, by), whole, lo, hi, SPLIT_ROWS[i])
            pltpu.make_async_remote_copy(src_ref=ref, dst_ref=ref, send_sem=csend_sem.at[u, k],
                recv_sem=crecv_sem.at[u, k], device_id=device(sib), device_id_type=MESH).wait_recv()
    for cp in sends:
        cp.wait_send()


def gather_all(pieces):
    outs = [jax.ShapeDtypeStruct((4, 2, 4, 2, 2) + p.shape, p.dtype) for p in pieces]
    n = len(UNITS)
    return pl.pallas_call(
        ag_kernel, out_shape=outs,
        in_specs=[pl.BlockSpec(memory_space=pl.ANY)] * len(pieces),
        out_specs=[pl.BlockSpec(memory_space=pl.ANY)] * len(pieces),
        scratch_shapes=[pltpu.SemaphoreType.DMA((4,)), pltpu.SemaphoreType.DMA((n, 12)), pltpu.SemaphoreType.DMA((n, 12)),
            pltpu.SemaphoreType.DMA((n, 4)), pltpu.SemaphoreType.DMA((n, 4))],
        compiler_params=pltpu.CompilerParams(collective_id=0, has_side_effects=True),
        name="gather_weights",
    )(*pieces)


RS_ORDERS = tuple(o[::-1] for o in ORDERS)
SIZES = {"y": (4,), "x": (2, 2), "z": (4,)}
DIMS = (("y", 4), ("x", 2), ("z", 4), ("x", 2))


def live_dims(fixed):
    return tuple(n for a, n in DIMS if a not in fixed)


def part(ref, at, fixed, gone, lo, hi, rows, lead=()):
    every = slice(None)
    idx = []
    for k, (a, n) in enumerate(DIMS):
        if a in gone:
            continue
        if a in fixed:
            idx.append((at["x"] % 2 if k == 1 else at["x"] // 2) if a == "x" else at[a])
        else:
            idx.append(every)
    span = pl.ds(lo, hi - lo)
    return ref.at[(*lead, *idx, span if rows else every, every if rows else span)]


def accumulate(dst, srcs, dims, out=None):
    n = 1
    for d in dims:
        n *= d
    def one(k, _):
        idx = []
        rest = k
        for d in dims[::-1]:
            idx.append(rest % d)
            rest = rest // d
        idx = tuple(idx[::-1])
        total = dst[idx].astype(jnp.float32) if dims else dst[...].astype(jnp.float32)
        for s in srcs:
            total = total + (s[idx] if dims else s[...]).astype(jnp.float32)
        target = dst if out is None else out
        if dims:
            target[idx] = total.astype(target.dtype)
        else:
            target[...] = total.astype(target.dtype)
        return 0
    if n == 1:
        one(0, 0)
    else:
        lax.fori_loop(0, n, one, 0)


def rs_kernel(*refs):
    n_arr, n = 4, len(UNITS)
    ins, outs = refs[:n_arr], refs[n_arr:2 * n_arr]
    refs = refs[2 * n_arr:]
    held, other = refs[:n], refs[n:2 * n]
    slots = [refs[2 * n + k * n: 3 * n + k * n] for k in range(3)]
    load_sem, csend_sem, crecv_sem, send_sem, recv_sem = refs[5 * n:]
    me = where_am_i()
    sib = moved(me, "c", 1)
    barrier = pltpu.get_barrier_semaphore()
    partners = [moved(me, a, d) for a in "xyz" for d in (1, -1)] + [sib]
    for one in partners:
        pl.semaphore_signal(barrier, inc=1, device_id=device(one), device_id_type=MESH)
    loads = []
    def half_of(i, c, lo, hi, rows):
        every, span = slice(None), pl.ds(lo, hi - lo)
        return ins[i].at[:, :, :, :, c, span if rows else every, every if rows else span]
    for u, (i, s, lo, hi) in enumerate(UNITS):
        cp = pltpu.make_async_copy(half_of(i, me["c"], lo, hi, SPLIT_ROWS[i]), held[u], load_sem.at[u])
        cp.start()
        loads.append(cp)
    pl.semaphore_wait(barrier, len(partners))
    sends = []
    for u, (i, s, lo, hi) in enumerate(UNITS):
        cp = pltpu.make_async_remote_copy(src_ref=half_of(i, sib["c"], lo, hi, SPLIT_ROWS[i]), dst_ref=other[u],
            send_sem=csend_sem.at[u], recv_sem=crecv_sem.at[u], device_id=device(sib), device_id_type=MESH)
        cp.start()
        sends.append(cp)

    def send(src, dst, u, stage, slot, to):
        cp = pltpu.make_async_remote_copy(src_ref=src, dst_ref=dst, send_sem=send_sem.at[u, stage, slot],
            recv_sem=recv_sem.at[u, stage, slot], device_id=device(to), device_id_type=MESH)
        cp.start()
        sends.append(cp)

    def got(ref, u, stage, slot):
        pltpu.make_async_remote_copy(src_ref=ref, dst_ref=ref, send_sem=send_sem.at[u, stage, slot],
            recv_sem=recv_sem.at[u, stage, slot], device_id=device(sib), device_id_type=MESH).wait_recv()

    def spans(u):
        i, s, lo, hi = UNITS[u]
        width = hi - lo
        return s, SPLIT_ROWS[i], width, middle(0, width, SPLIT_ROWS[i])

    def send_far(u, stage):
        s, rows, width, mid = spans(u)
        order = RS_ORDERS[s]
        axis, gone, fixed = order[stage], order[:stage], order[:stage + 1]
        far = moved(me, axis, 2)
        send(part(held[u], far, fixed, (), 0, mid, rows), part(slots[stage][u], me, (), fixed, 0, mid, rows, (0,)), u, stage, 0, moved(me, axis, 1))
        send(part(held[u], far, fixed, (), mid, width, rows), part(slots[stage][u], me, (), fixed, mid, width, rows, (0,)), u, stage, 1, moved(me, axis, -1))

    for u in range(n):
        loads[u].wait()
        pltpu.make_async_remote_copy(src_ref=other[u], dst_ref=other[u], send_sem=csend_sem.at[u], recv_sem=crecv_sem.at[u],
            device_id=device(sib), device_id_type=MESH).wait_recv()
        accumulate(held[u], [other[u]], live_dims(()))
        send_far(u, 0)
    for stage in range(3):
        for u in range(n):
            s, rows, width, mid = spans(u)
            order = RS_ORDERS[s]
            axis, fixed = order[stage], order[:stage + 1]
            above, below = moved(me, axis, 1), moved(me, axis, -1)
            dims = live_dims(fixed)
            for k, (to, lo, hi) in enumerate(((above, 0, mid), (below, mid, width))):
                came = part(slots[stage][u], me, (), fixed, lo, hi, rows, (0,))
                got(came, u, stage, k)
                accumulate(part(held[u], to, fixed, (), lo, hi, rows), [came], dims)
                send(part(held[u], to, fixed, (), 0, width, rows), part(slots[stage][u], me, (), fixed, 0, width, rows, (1 + k,)), u, stage, 2 + k, to)
        for u in range(n):
            i, _, lo, hi = UNITS[u]
            s, rows, width, mid = spans(u)
            order = RS_ORDERS[s]
            fixed = order[:stage + 1]
            came = []
            for k in range(2):
                ref = part(slots[stage][u], me, (), fixed, 0, width, rows, (1 + k,))
                got(ref, u, stage, 2 + k)
                came.append(ref)
            mine = part(held[u], me, fixed, (), 0, width, rows)
            if stage == 2:
                span = pl.ds(lo, hi - lo)
                accumulate(mine, came, (), outs[i].at[(span, slice(None)) if rows else (slice(None), span)])
            else:
                accumulate(mine, came, live_dims(fixed))
                send_far(u, stage + 1)
    for cp in sends:
        cp.wait_send()


def scatter_all(grads):
    outs = [jax.ShapeDtypeStruct(g.shape[5:], jnp.float32) for g in grads]
    n = len(UNITS)
    held, slots = [], [[], [], []]
    for i, s, lo, hi in UNITS:
        tail = (hi - lo, 128) if SPLIT_ROWS[i] else (8, hi - lo)
        held.append(pltpu.VMEM(live_dims(()) + tail, jnp.bfloat16))
        for k in range(3):
            slots[k].append(pltpu.VMEM((3,) + live_dims(RS_ORDERS[s][:k + 1]) + tail, jnp.bfloat16))
    return pl.pallas_call(
        rs_kernel, out_shape=outs,
        in_specs=[pl.BlockSpec(memory_space=pl.ANY)] * len(grads),
        out_specs=[pl.BlockSpec(memory_space=pltpu.VMEM)] * len(grads),
        scratch_shapes=held + held + slots[0] + slots[1] + slots[2] + [
            pltpu.SemaphoreType.DMA((n,)), pltpu.SemaphoreType.DMA((n,)), pltpu.SemaphoreType.DMA((n,)),
            pltpu.SemaphoreType.DMA((n, 3, 4)), pltpu.SemaphoreType.DMA((n, 3, 4))],
        compiler_params=pltpu.CompilerParams(collective_id=1, has_side_effects=True, vmem_limit_bytes=60 << 20),
        name="scatter_grads",
    )(*grads)


def scan_kernel(backward, *refs):
    local, tags, fade, carried = refs[0], refs[1], refs[2], refs[3]
    tags_all = refs[4]
    came, going, tag_send, tag_recv, send1, recv1, send2, recv2 = refs[5:]
    me = lax.axis_index("seq")
    dp = lax.axis_index("dp")
    n = 16
    barrier = pltpu.get_barrier_semaphore()
    def greet(k, _):
        pl.semaphore_signal(barrier, inc=1, device_id=(dp, (me + k) % n), device_id_type=MESH)
        return 0
    lax.fori_loop(1, n, greet, 0)
    tags_all[me] = tags[...]
    came[me] = local[me]
    pl.semaphore_wait(barrier, n - 1)

    def tag_copy(to):
        return pltpu.make_async_remote_copy(src_ref=tags, dst_ref=tags_all.at[me], send_sem=tag_send.at[to],
            recv_sem=tag_recv.at[me], device_id=(dp, to), device_id_type=MESH)
    def state_copy(to):
        return pltpu.make_async_remote_copy(src_ref=local.at[to], dst_ref=came.at[me], send_sem=send1.at[to],
            recv_sem=recv1.at[me], device_id=(dp, to), device_id_type=MESH)
    def back_copy(to):
        return pltpu.make_async_remote_copy(src_ref=going.at[to], dst_ref=carried.at[me], send_sem=send2.at[to],
            recv_sem=recv2.at[me], device_id=(dp, to), device_id_type=MESH)
    def arrival(ref, ssem, rsem, frm):
        return pltpu.make_async_remote_copy(src_ref=ref.at[frm], dst_ref=ref.at[frm], send_sem=ssem.at[frm],
            recv_sem=rsem.at[frm], device_id=(dp, (me + 1) % n), device_id_type=MESH)

    def start1(k, _):
        to = (me + k) % n
        tag_copy(to).start()
        state_copy(to).start()
        return 0
    lax.fori_loop(1, n, start1, 0)
    def wait1(k, _):
        frm = (me + k) % n
        arrival(tags_all, tag_send, tag_recv, frm).wait_recv()
        arrival(came, send1, recv1, frm).wait_recv()
        return 0
    lax.fori_loop(1, n, wait1, 0)

    micro, head = me // 8, me % 8
    lam = fade[pl.ds(head, 1), :]
    def first(b):
        return tags_all[b, pl.ds(2 * micro, 1), :]
    def last(b):
        return tags_all[b, pl.ds(2 * micro + 1, 1), :]
    acc = jnp.zeros((128, 128), jnp.float32)
    order = range(n - 1, -1, -1) if backward else range(n)
    previous = None
    for b in order:
        going[b] = acc.astype(jnp.bfloat16)
        whole = first(b) == last(b)
        if previous is None:
            acc = came[b].astype(jnp.float32)
        else:
            near = (last(b) == first(previous)) if backward else (first(b) == last(previous))
            acc = came[b].astype(jnp.float32) + jnp.where(whole & near, lam, 0.0) * acc
        previous = b
    carried[me] = going[me]
    def start2(k, _):
        back_copy((me + k) % n).start()
        return 0
    lax.fori_loop(1, n, start2, 0)
    def wait2(k, _):
        frm = (me + k) % n
        arrival(carried, send2, recv2, frm).wait_recv()
        return 0
    lax.fori_loop(1, n, wait2, 0)
    def drain(k, _):
        to = (me + k) % n
        tag_copy(to).wait_send()
        state_copy(to).wait_send()
        back_copy(to).wait_send()
        return 0
    lax.fori_loop(1, n, drain, 0)


def scan_states(local, tags, fade, backward):
    D = pltpu.SemaphoreType.DMA
    v = pl.BlockSpec(memory_space=pltpu.VMEM)
    return pl.pallas_call(
        functools.partial(scan_kernel, backward),
        out_shape=[jax.ShapeDtypeStruct((16, 128, 128), jnp.bfloat16), jax.ShapeDtypeStruct((16, 8, 128), jnp.float32)],
        in_specs=[v] * 3, out_specs=[v] * 2,
        scratch_shapes=[pltpu.VMEM((16, 128, 128), jnp.bfloat16), pltpu.VMEM((16, 128, 128), jnp.bfloat16)] + [D((16,))] * 6,
        compiler_params=pltpu.CompilerParams(collective_id=3 if backward else 2, has_side_effects=True),
        name="scan_back" if backward else "scan_ahead",
    )(local, tags, fade)


D = 1024
H = 8
HD = 128
FF = 2816
EPSILON = 1e-06


def swish(values):
    return values * jax.nn.sigmoid(values)


def swish_slope(values):
    sigma = jax.nn.sigmoid(values)
    return sigma * (1.0 + values * (1.0 - sigma))


def rms_factor(values):
    return lax.rsqrt(jnp.mean(values * values, axis=-1, keepdims=True) + EPSILON)


def norm_back(upstream, normed, factor):
    return factor * (upstream - normed * jnp.mean(upstream * normed, axis=-1, keepdims=True))


def matmul(form, left_op, right_op):
    return jnp.einsum(form, left_op, right_op, preferred_element_type=jnp.float32)


def on_device(hidden_in, seg_ids, decay_rates, grad_out, w_query, w_key, w_value, w_gate, w_output, w_left, w_right, w_down):
    micros, length = hidden_in.shape[0], hidden_in.shape[2]
    rows = micros * length
    low = jnp.bfloat16
    pieces = [
        jnp.concatenate([w.reshape(8, D) for w in (w_query, w_key, w_value, w_gate)], axis=1),
        w_output.reshape(8, D),
        jnp.concatenate([w.reshape(8, FF) for w in (w_left, w_right)], axis=1),
        w_down.reshape(176, 128),
    ]
    m_in, m_output, m_up, m_down = gather_all(pieces)
    m_in = m_in.reshape(D, 4 * D)
    m_output = m_output.reshape(D, D)
    m_up = m_up.reshape(D, 2 * FF)
    m_down = m_down.reshape(FF, D)

    segments = seg_ids.reshape(micros, length)
    tags = jnp.stack([segments[0, 0], segments[0, -1], segments[1, 0], segments[1, -1]]).astype(jnp.float32)
    tags = jnp.concatenate([tags, jnp.zeros((4,), jnp.float32)])[:, None] * jnp.ones((8, 128), jnp.float32)
    fade = jnp.exp(-length * decay_rates)[:, None] * jnp.ones((8, 128), jnp.float32)
    places = jnp.arange(length, dtype=jnp.float32)
    distance = places[:, None] - places[None, :]
    allowed = (distance >= 0.0)[None] & (segments[:, :, None] == segments[:, None, :])
    decay_mask = jnp.where(
        allowed[:, None], jnp.exp(-decay_rates[None, :, None, None] * jnp.maximum(distance, 0.0)[None, None]), 0.0)
    rising = jnp.exp(-(places + 1.0)[None, :, None] * decay_rates)
    falling = jnp.exp(-(length - 1.0 - places)[None, :, None] * decay_rates)

    inputs = hidden_in.reshape(rows, D).astype(jnp.float32)
    factor_in = rms_factor(inputs)
    normed_in = inputs * factor_in
    first_in = normed_in.astype(low)
    pre = matmul("rd,de->re", first_in, m_in)
    q_pre, k_pre, v_pre, gate = (pre[:, k * D:(k + 1) * D] for k in range(4))
    heads = (micros, length, H, HD)
    queries = swish(q_pre).astype(low).reshape(heads)
    key_rows = swish(k_pre).astype(low).reshape(heads)
    value_rows = v_pre.astype(low).reshape(heads)
    keeping = falling * (segments == segments[:, -1:]).astype(jnp.float32)[:, :, None]
    kept = (key_rows.astype(jnp.float32) * keeping[..., None]).astype(low)
    local = matmul("sjhd,sjhe->shde", kept, value_rows).astype(low).reshape(micros * H, HD, HD)
    carried, tags_all = scan_states(local, tags, fade, False)
    carried = carried.reshape(micros, H, HD, HD)
    me = lax.axis_index("seq")
    ends = tags_all[:, :4, 0]
    before = jnp.where(me > 0, ends[jnp.maximum(me - 1, 0)], -1.0)
    after = jnp.where(me < 15, ends[jnp.minimum(me + 1, 15)], -1.0)
    boundary = before[1::2]
    reverse_tag = after[0::2]
    tokens = segments.astype(jnp.float32)
    scores = matmul("sihd,sjhd->shij", queries, key_rows)
    weighted = (scores * decay_mask).astype(low)
    within = matmul("shij,sjhe->sihe", weighted, value_rows)
    reaching = rising * (tokens == boundary[:, None]).astype(jnp.float32)[:, :, None]
    crossed = matmul("sihd,shde->sihe", queries, carried) * reaching[..., None]
    mixed = (within + crossed).reshape(rows, D)
    factor_mix = rms_factor(mixed)
    normed_mix = mixed * factor_mix
    gated = (normed_mix * gate).astype(low)
    resid = inputs + matmul("rd,de->re", gated, m_output)
    factor_res = rms_factor(resid)
    normed_res = resid * factor_res
    second = normed_res.astype(low)
    up = matmul("rd,df->rf", second, m_up)
    left_proj, right_proj = up[:, :FF], up[:, FF:]
    product = (left_proj * right_proj).astype(low)
    result = (resid + matmul("rf,fd->rd", product, m_down)).astype(low)

    d_branch = grad_out.reshape(rows, D)
    cotangent = d_branch.astype(jnp.float32)
    g_down = matmul("rf,rd->fd", product, d_branch).astype(low)
    d_prod = matmul("rd,fd->rf", d_branch, m_down)
    d_up = jnp.concatenate([(d_prod * right_proj).astype(low), (d_prod * left_proj).astype(low)], axis=1)
    g_up = matmul("rd,rf->df", second, d_up).astype(low)
    d_second = matmul("rf,df->rd", d_up, m_up)
    d_resid = cotangent + norm_back(d_second, normed_res, factor_res)
    d_attn = d_resid.astype(low)
    g_output = matmul("rd,re->de", gated, d_attn).astype(low)
    d_gated = matmul("re,de->rd", d_attn, m_output)
    d_gate = (d_gated * normed_mix).astype(low)
    d_mixed = norm_back(d_gated * gate, normed_mix, factor_mix).astype(low).reshape(heads)
    d_weighted = matmul("sihe,sjhe->shij", d_mixed, value_rows)
    d_scores = (d_weighted * decay_mask).astype(low)
    opening = rising * (segments == segments[:, :1]).astype(jnp.float32)[:, :, None]
    opened = (queries.astype(jnp.float32) * opening[..., None]).astype(low)
    back_local = matmul("sihd,sihe->shde", opened, d_mixed).astype(low).reshape(micros * H, HD, HD)
    reverse, _ = scan_states(back_local, tags, fade, True)
    reverse = reverse.reshape(micros, H, HD, HD)
    d_query = matmul("shij,sjhd->sihd", d_scores, key_rows)
    d_query = d_query + matmul("sihe,shde->sihd", d_mixed, carried) * reaching[..., None]
    d_key = matmul("shij,sihd->sjhd", d_scores, queries)
    d_value = matmul("shij,sihe->sjhe", weighted, d_mixed)
    closing = falling * (tokens == reverse_tag[:, None]).astype(jnp.float32)[:, :, None]
    d_key = d_key + matmul("sjhe,shde->sjhd", value_rows, reverse) * closing[..., None]
    d_value = d_value + matmul("sjhd,shde->sjhe", key_rows, reverse) * closing[..., None]
    d_pre = jnp.concatenate([
        (d_query.reshape(rows, D) * swish_slope(q_pre)).astype(low),
        (d_key.reshape(rows, D) * swish_slope(k_pre)).astype(low),
        d_value.reshape(rows, D).astype(low),
        d_gate,
    ], axis=1)
    g_in = matmul("rd,re->de", first_in, d_pre).astype(low)
    d_first = matmul("re,de->rd", d_pre, m_in)
    d_inputs = d_resid + norm_back(d_first, normed_in, factor_in)

    owners = (4, 2, 4, 2, 2)
    s_in, s_output, s_up, s_down = scatter_all([
        g_in.reshape(owners + (8, 4 * D)), g_output.reshape(owners + (8, D)),
        g_up.reshape(owners + (8, 2 * FF)), g_down.reshape(owners + (176, 128))])
    shape = hidden_in.shape
    return (
        result.reshape(shape), d_inputs.reshape(shape),
        *(s_in[:, k * D:(k + 1) * D].reshape(-1) for k in range(4)),
        s_output.reshape(-1), s_up[:, :FF].reshape(-1), s_up[:, FF:].reshape(-1), s_down.reshape(-1),
    )


def solution(mesh):
    tokens = P(None, "dp", "seq", None)
    flat = P(("dp", "seq"))
    return jax.shard_map(
        on_device, mesh=mesh,
        in_specs=(tokens, P(None, "dp", "seq"), P(), tokens) + (flat,) * 8,
        out_specs=(tokens, tokens) + (flat,) * 8,
        check_vma=False,
    )
```

time: 2600 us -> 351 us (0.14)
  waiting for transfers between devices: 2090 us -> 0 us
  Pallas kernels: 0 us -> 206 us
  local copies, waits for them, and re-layouts: 159 us -> 54 us
  loops' own time: 78.5 us -> 0 us
  other arithmetic: 77.6 us -> 18.2 us
  matrix products: 120 us -> 68.2 us
  blocking collectives: 34.2 us -> 0 us
  between operations: 33.1 us -> 1.17 us
    all_gather x12 -> x0, waiting for transfers between devices: 1710 us -> none  [the longest x4 246 us: carried_in(): lax.all_gather(a.astype(kind), axis)]
    unnamed x14 -> x0, waiting for transfers between devices: 376 us -> none
    pallas_call x0 -> x4, Pallas kernels: none -> 206 us  [the longest x1 79.8 us: scatter_all(): pl.pallas_call(rs_kernel, out_shape=outs, in_specs=[pl.BlockSpec(memory_s...]
    another operation x4 -> x0, loops' own time: 78.5 us -> none  [carried_in(): return lax.fori_loop(0, ahead, one, state)]
    dot_general x68 -> x24, matrix products: 114 us -> 68.2 us  [matmul(): jnp.einsum(form, left_op, right_op, preferred_element_type=jnp.float32)]
    unnamed x245 -> x75, local copies, waits for them, and re-layouts: 53.3 us -> 11.5 us
    unnamed x1 -> x0, blocking collectives: 34.2 us -> none
    add x30 -> x1, other arithmetic: 33.2 us -> 1.26 us  [on_device(): d_inputs = d_resid + norm_back(d_first, normed_in, factor_in)]
  transfers between devices with their start and end apart: 13 -> 0, of which waited for: 12 -> 0; matrix products, arithmetic and copies ran while one was open for 7% -> 0% of each run, Pallas kernels for 0% -> 0%
where the time goes in v1:
time: 351 us; the launch traced here: 348 us
  Pallas kernels  206 us (59%)
  matrix products  68.2 us (19%)
  local copies, waits for them, and re-layouts  54 us (15%)
  other arithmetic  18.2 us (5%)
    pallas_call x1, Pallas kernels, scatter_all(): pl.pallas_call(rs_kernel, out_shape=outs, in_specs=[pl.BlockSpec(memory_s...  79.8 us
    pallas_call x1, Pallas kernels, gather_all(): pl.pallas_call(ag_kernel, out_shape=outs, in_specs=[pl.BlockSpec(memory_s...  78.4 us
    dot_general x24, matrix products, matmul(): jnp.einsum(form, left_op, right_op, preferred_element_type=jnp.float32)  68.2 us
    pallas_call x2, Pallas kernels, scan_states(): pl.pallas_call(functools.partial(scan_kernel, backward), out_shape=[jax.S...  48 us
    unnamed x75, local copies, waits for them, and re-layouts  11.5 us
    reshape x1, local copies, waits for them, and re-layouts, on_device(): g_down.reshape(owners + (176, 128))  9.86 us
    reshape x1, local copies, waits for them, and re-layouts, on_device(): m_down = m_down.reshape(FF, D)  9.7 us

profile of v1, /device:TPU:1, one launch (start us, length us, event | category | flops | bytes accessed | tf_op | source)
XLA Modules:
  0.0 347.7 jit_solution(3794993242192903519)
XLA Ops:
  5.7 2.7 add_convert_fusion
  20.2 78.4 %gather_weights.1 = (bf16[4,2,4,2,2,8,4096]{6,5,4,3,2,1,0:T(8,128)(2,1)}, bf16[4,2,4,2,2,8,1024]{6,5,4,3,2,1,0:T(8,128)(2,1)}, bf16[4,2,4,2,2,8,5632]{6,5,4,3,2,...) custom-call(bf16[8,4096]{1,0:T(8,128)(2,1)} %pad_maximum_fusion.7.refs_0_, bf16[8,1024]{1,0:T(8,128)(2,1)} %reshape.427.refs_1_, ...), custom_call_target="tpu_custom_call" | custom-call | tf_op jit(solution)/shard_map/gather_weights/pallas_call | solution.py:133
  98.6 5.7 %fusion.42 = f32[256,4096]{1,0:T(8,128)S(1)} fusion(bf16[256,1024]{1,0:T(8,128)(2,1)S(1)} %bitcast.212, bf16[1024,4096]{1,0:T(8,128)(2,1)} %bitcast.228), kind=kOutput, calls=%fused_computation.130 | convolution fusion | flops 2147483648 | bytes 13107200 | tf_op jit(solution)/shard_map/rd,de->re/dot_general | solution.py:422
  108.4 23.5 %scan_ahead.1 = (bf16[16,128,128]{2,1,0:T(8,128)(2,1)}, f32[16,8,128]{2,1,0:T(8,128)}) custom-call(bf16[16,128,128]{2,1,0:T(8,128)(2,1)} %bitcast.201, f32[8,128]{1,0:T(8,128)} %mul.329.refs_1_, f32[8,128]{1,0:T(8,128)} %mul.331.refs_2_), custom_call_target="tpu_custom_call" | custom-call | tf_op jit(solution)/shard_map/scan_ahead/pallas_call | solution.py:387
  139.3 2.6 multiply_reduce_fusion.3
  141.9 9.7 %reshape.440 = bf16[2816,1024]{1,0:T(8,128)(2,1)} reshape(bf16[4,2,4,2,2,176,128]{6,5,4,3,2,1,0:T(8,128)(2,1)} %get-tuple-element.26) | data formatting | bytes 11534336 | tf_op jit(solution)/shard_map/reshape | solution.py:439
  151.6 6.2 %fusion.39 = f32[256,5632]{1,0:T(8,128)S(1)} fusion(bf16[1024,5632]{1,0:T(8,128)(2,1)} %bitcast.188, f32[256,1024]{1,0:T(8,128)S(1)} %get-tuple-element.91, f32[256]{0:T(256)S(1)} %add_rsqrt_fusion), kind=kOutput, calls=%fused_computation.127 | convolution fusion | flops 2953314304 | bytes 18351104 | tf_op jit(solution)/shard_map/rd,df->rf/dot_general | solution.py:422
  159.8 2.5 fusion.9
  162.3 6.3 %multiply_reduce_fusion.2 = (f32[256]{0:T(256)S(1)}, f32[256,1024]{1,0:T(8,128)S(1)}) fusion(f32[256,1024]{1,0:T(8,128)S(1)} %get-tuple-element.91, f32[256]{0:T(256)S(1)} %add_rsqrt_fusion, bf16[1024,5632]{1,0:T(8,128)(2,1)} %bitcast.189, bf16[256,2816]{1,0:T(8,128)(2,1)S(1)} %get-tuple-element.57, bf16[256,2816]{1,0:T(8,128)(2,1)S(1)} %get-tuple-element.56), kind=kOutput, calls=%fused_computation.51 | convolution fusion | flops 2959343360 | bytes 16517120 | tf_op jit(solution)/shard_map/rf,df->rd/dot_general | solution.py:422
  173.3 2.1 copy.66
  175.4 2.7 fusion.12
  178.1 2.3 convolution_convert_fusion.4
  180.4 24.5 %scan_back.1 = (bf16[16,128,128]{2,1,0:T(8,128)(2,1)}, f32[16,8,128]{2,1,0:T(8,128)}) custom-call(bf16[16,128,128]{2,1,0:T(8,128)(2,1)} %bitcast.200, f32[8,128]{1,0:T(8,128)} %mul.329.refs_1_, f32[8,128]{1,0:T(8,128)} %mul.331.refs_2_), custom_call_target="tpu_custom_call" | custom-call | tf_op jit(solution)/shard_map/scan_back/pallas_call | solution.py:387
  206.2 2.6 fusion.4
  208.8 2.6 copy.65
  213.2 2.3 fusion.6
  217.6 2.6 copy.60
  220.1 3.4 fusion.14
  223.6 5.9 %fusion.15 = (bf16[256,1024]{1,0:T(8,128)(2,1)S(1)}, f32[256]{0:T(256)S(1)}, f32[256,1024]{1,0:T(8,128)S(1)}) fusion(bf16[2,1,128,1024]{3,2,1,0:T(8,128)(2,1)S(1)} %copy-done.8, f32[256]{0:T(256)S(1)} %get-tuple-element.75, bf16[1024,4096]{1,0:T(8,128)(2,1)} %bitcast.229, bf16[256,1024]{1,0:T(8,128)(2,1)S(1)} %copy-done.29, ...), kind=kOutput, calls=%fused_computation.63 | convolution fusion | flops 2157182720 | bytes 12584960 | tf_op jit(solution)/shard_map/re,de->rd/dot_general | solution.py:422
  232.8 5.1 %convolution_convert_fusion.1 = bf16[1024,4096]{1,0:T(8,128)(2,1)} fusion(bf16[256,1024]{1,0:T(8,128)(2,1)S(1)} %get-tuple-element.65, bf16[256,1024]{1,0:T(8,128)(2,1)S(1)} %copy-done.29, bf16[256,1024]{1,0:T(8,128)(2,1)S(1)} %bitcast.214, bf16[256,1024]{1,0:T(8,128)(2,1)S(1)} %get-tuple-element.60, bf16[256,1024]{1,0:T(8,128)(2,1)S(1)} %get-tuple-element.59), kind=kOutput, calls=%fused_computation.1 | convolution fusion | flops 2160066560 | bytes 11010048 | tf_op jit(solution)/shard_map/rd,re->de/dot_general | solution.py:422
  237.9 4.2 %convolution_convert_fusion.2 = bf16[2816,1024]{1,0:T(8,128)(2,1)} fusion(bf16[256,2816]{1,0:T(8,128)(2,1)S(1)} %copy-done.20, bf16[256,1024]{1,0:T(8,128)(2,1)S(1)} %bitcast.210), kind=kOutput, calls=%fused_computation.2 | convolution fusion | flops 1479278592 | bytes 7733248 | tf_op jit(solution)/shard_map/rf,rd->fd/dot_general | solution.py:422
  242.1 9.9 %reshape.452.refs_3_ = bf16[4,2,4,2,2,176,128]{6,5,4,3,2,1,0:T(8,128)(2,1)} reshape(bf16[2816,1024]{1,0:T(8,128)(2,1)} %convolution_convert_fusion.2) | data formatting | bytes 11534336 | tf_op jit(solution)/shard_map/reshape | solution.py:533
  252.0 7.5 %convolution_convert_fusion = bf16[1024,5632]{1,0:T(8,128)(2,1)} fusion(bf16[256,2816]{1,0:T(8,128)(2,1)} %copy-done.27, bf16[256,2816]{1,0:T(8,128)(2,1)S(1)} %copy-done.26, f32[256,1024]{1,0:T(8,128)S(1)} %get-tuple-element.91, f32[256]{0:T(256)S(1)} %add_rsqrt_fusion), kind=kOutput, calls=%fused_computation | convolution fusion | flops 2964848640 | bytes 15467520 | tf_op jit(solution)/shard_map/rd,rf->df/dot_general | solution.py:422
  259.5 79.8 %scatter_grads.1 = (f32[8,4096]{1,0:T(8,128)}, f32[8,1024]{1,0:T(8,128)}, f32[8,5632]{1,0:T(8,128)}, f32[176,128]{1,0:T(8,128)}) custom-call(bf16[4,2,4,2,2,8,4096]{6,5,4,3,2,1,0:T(8,128)(2,1)} %bitcast.193, bf16[4,2,4,2,2,8,1024]{6,5,4,3,2,1,0:T(8,128)(2,1)} %bitcast.197, bf16[4,2,4,2,2,8,5632]{6,5,4,3,2,1,0:T(8,128)(2,1)} %bitcast.180, ...), custom_call_target="tpu_custom_call" | custom-call | tf_op jit(solution)/shard_map/scatter_grads/pallas_call | solution.py:293
  (136 shorter events, 51.6 us)
Async XLA Ops:
  18.8 114.9 %copy-start.16 = (f32[8,128,128]{2,1,0:T(8,128)}, f32[8,128,128]{2,1,0:T(8,128)S(1)}, u32[]{:S(2)}) copy-start(f32[8,128,128]{2,1,0:T(8,128)S(1)} %multiply_exponential_fusion) | copy-start | bytes 1572868
  104.4 28.7 %copy-start.30 = (s32[2,1,128]{2,1,0:T(1,128)S(1)}, s32[2,1,128]{2,1,0:T(1,128)}, u32[]{:S(2)}) copy-start(s32[2,1,128]{2,1,0:T(1,128)} %param.13) | copy-start | bytes 3076
  104.5 29.7 %copy-start.2 = (bf16[32,8,8,128]{3,2,1,0:T(8,128)(2,1)}, bf16[32,8,8,128]{3,2,1,0:T(8,128)(2,1)S(1)}, u32[]{:S(2)}) copy-start(bf16[32,8,8,128]{3,2,1,0:T(8,128)(2,1)S(1)} %copy.75) | copy-start | bytes 1572868
  106.9 27.3 %copy-start.10 = (bf16[32,8,8,128]{3,2,1,0:T(8,128)(2,1)}, bf16[32,8,8,128]{3,2,1,0:T(8,128)(2,1)S(1)}, u32[]{:S(2)}) copy-start(bf16[32,8,8,128]{3,2,1,0:T(8,128)(2,1)S(1)} %copy.77) | copy-start | bytes 1572868
  107.3 26.0 %copy-start.15 = (bf16[2,128,8,128]{1,3,2,0:T(8,128)(2,1)}, bf16[2,128,8,128]{1,3,2,0:T(8,128)(2,1)S(1)}, u32[]{:S(2)}) copy-start(bf16[2,128,8,128]{1,3,2,0:T(8,128)(2,1)S(1)} %copy.50) | copy-start | bytes 1572868
  133.7 4.1 %copy-start.4 = (bf16[2,128,8,128]{1,3,2,0:T(8,128)(2,1)}, bf16[2,128,8,128]{1,3,2,0:T(8,128)(2,1)S(1)}, u32[]{:S(2)}) copy-start(bf16[2,128,8,128]{1,3,2,0:T(8,128)(2,1)S(1)} %copy.61) | copy-start | bytes 1572868
  134.8 4.5 %copy-start.7 = (bf16[2,1,128,1024]{3,2,1,0:T(8,128)(2,1)S(1)}, bf16[2,1,128,1024]{3,2,1,0:T(8,128)(2,1)}, u32[]{:S(2)}) copy-start(bf16[2,1,128,1024]{3,2,1,0:T(8,128)(2,1)} %param.12) | copy-start | bytes 1572868
  139.3 12.3 %copy-start.13 = (bf16[256,1024]{1,0:T(8,128)(2,1)}, bf16[256,1024]{1,0:T(8,128)(2,1)S(1)}, u32[]{:S(2)}) copy-start(bf16[256,1024]{1,0:T(8,128)(2,1)S(1)} %multiply_convert_fusion.6) | copy-start | bytes 1572868
  151.6 6.3 %copy-start.12 = (bf16[2816,1024]{1,0:T(8,128)(2,1)S(1)}, bf16[2816,1024]{1,0:T(8,128)(2,1)}, u32[]{:S(2)}) copy-start(bf16[2816,1024]{1,0:T(8,128)(2,1)} %reshape.440) | copy-start | bytes 17301508
  151.6 6.3 %copy-start.23 = (bf16[2,1,128,1024]{3,2,1,0:T(8,128)(2,1)S(1)}, bf16[2,1,128,1024]{3,2,1,0:T(8,128)(2,1)}, u32[]{:S(2)}) copy-start(bf16[2,1,128,1024]{3,2,1,0:T(8,128)(2,1)} %param.15) | copy-start | bytes 1572868
  162.3 6.7 %copy-start.1 = (f32[256,4096]{1,0:T(8,128)S(1)}, f32[256,4096]{1,0:T(8,128)}, u32[]{:S(2)}) copy-start(f32[256,4096]{1,0:T(8,128)} %copy-done) | copy-start | bytes 12582916
  172.4 5.7 %copy-start.5 = (bf16[2,128,8,128]{1,3,2,0:T(8,128)(2,1)S(1)}, bf16[2,128,8,128]{1,3,2,0:T(8,128)(2,1)}, u32[]{:S(2)}) copy-start(bf16[2,128,8,128]{1,3,2,0:T(8,128)(2,1)} %copy-done.4) | copy-start | bytes 1572868
  172.4 33.8 %copy-start.3 = (bf16[32,8,8,128]{3,2,1,0:T(8,128)(2,1)S(1)}, bf16[32,8,8,128]{3,2,1,0:T(8,128)(2,1)}, u32[]{:S(2)}) copy-start(bf16[32,8,8,128]{3,2,1,0:T(8,128)(2,1)} %copy-done.2) | copy-start | bytes 1572868
  206.2 7.0 %copy-start.6 = (bf16[2,128,8,128]{1,3,2,0:T(8,128)(2,1)S(1)}, bf16[2,128,8,128]{1,3,2,0:T(8,128)(2,1)}, u32[]{:S(2)}) copy-start(bf16[2,128,8,128]{1,3,2,0:T(8,128)(2,1)} %copy.66) | copy-start | bytes 1572868
  208.8 6.7 %copy-start.18 = (bf16[2,8,128,128]{3,2,1,0:T(8,128)(2,1)S(1)}, bf16[2,8,128,128]{3,2,1,0:T(8,128)(2,1)}, u32[]{:S(2)}) copy-start(bf16[2,8,128,128]{3,2,1,0:T(8,128)(2,1)} %copy-done.17) | copy-start | bytes 1572868
  211.4 4.4 %copy-start.11 = (bf16[32,8,8,128]{3,2,1,0:T(8,128)(2,1)S(1)}, bf16[32,8,8,128]{3,2,1,0:T(8,128)(2,1)}, u32[]{:S(2)}) copy-start(bf16[32,8,8,128]{3,2,1,0:T(8,128)(2,1)} %copy-done.10) | copy-start | bytes 1572868
  211.4 4.4 %copy-start.21 = (bf16[16,128,128]{2,1,0:T(8,128)(2,1)S(1)}, bf16[16,128,128]{2,1,0:T(8,128)(2,1)}, u32[]{:S(2)}) copy-start(bf16[16,128,128]{2,1,0:T(8,128)(2,1)} %get-tuple-element.27) | copy-start | bytes 1572868
  216.6 6.9 %copy-start.8 = (bf16[2,1,128,1024]{3,2,1,0:T(8,128)(2,1)S(1)}, bf16[2,1,128,1024]{3,2,1,0:T(8,128)(2,1)}, u32[]{:S(2)}) copy-start(bf16[2,1,128,1024]{3,2,1,0:T(8,128)(2,1)} %param.12) | copy-start | bytes 1572868
  217.5 6.0 %copy-start.28 = (bf16[32,8,8,128]{3,1,2,0:T(8,128)(2,1)S(1)}, bf16[32,8,8,128]{3,1,2,0:T(8,128)(2,1)}, u32[]{:S(2)}) copy-start(bf16[32,8,8,128]{3,1,2,0:T(8,128)(2,1)} %copy.119) | copy-start | bytes 1572868
  220.1 3.4 copy-start.29
  223.6 7.2 %copy-start.14 = (bf16[256,1024]{1,0:T(8,128)(2,1)S(1)}, bf16[256,1024]{1,0:T(8,128)(2,1)}, u32[]{:S(2)}) copy-start(bf16[256,1024]{1,0:T(8,128)(2,1)} %copy-done.13) | copy-start | bytes 1572868
  232.8 5.1 %copy-start.20 = (bf16[256,2816]{1,0:T(8,128)(2,1)S(1)}, bf16[256,2816]{1,0:T(8,128)(2,1)}, u32[]{:S(2)}) copy-start(bf16[256,2816]{1,0:T(8,128)(2,1)} %copy-done.19) | copy-start | bytes 4325380
  232.8 5.1 %copy-start.24 = (bf16[2,1,128,1024]{3,2,1,0:T(8,128)(2,1)S(1)}, bf16[2,1,128,1024]{3,2,1,0:T(8,128)(2,1)}, u32[]{:S(2)}) copy-start(bf16[2,1,128,1024]{3,2,1,0:T(8,128)(2,1)} %param.15) | copy-start | bytes 1572868
  242.1 9.9 %copy-start.26 = (bf16[256,2816]{1,0:T(8,128)(2,1)S(1)}, bf16[256,2816]{1,0:T(8,128)(2,1)}, u32[]{:S(2)}) copy-start(bf16[256,2816]{1,0:T(8,128)(2,1)} %copy-done.25) | copy-start | bytes 4325380
  (7 other events, 14.4 us)

commit v2 on v1

--- a/solution.py
+++ b/solution.py
@@ -7,15 +7,32 @@
 
 MESH = pl.DeviceIdType.MESH
 RING = 4
-
-UNITS = (
-    (0, 0, 0, 13 * 128), (0, 1, 13 * 128, 26 * 128), (0, 2, 26 * 128, 32 * 128),
-    (1, 2, 0, 8 * 128),
-    (2, 0, 0, 22 * 128), (2, 1, 22 * 128, 44 * 128),
-    (3, 2, 0, 176),
-)
+D = 1024
+H = 8
+HD = 128
+FF = 2816
+ROWS = 256
+N_SEQ = 16
+EPSILON = 1e-06
+LOW = jnp.bfloat16
+F32 = jnp.float32
+OWNERS = (4, 2, 4, 2, 2)
+DMA = pltpu.SemaphoreType.DMA
 ORDERS = (("x", "y", "z"), ("y", "z", "x"), ("z", "x", "y"))
 SPLIT_ROWS = (False, False, False, True)
+
+
+def tiles(array, bounds, grain=128):
+    return [(array, s, lo * grain, hi * grain) for s, (lo, hi) in enumerate(zip(bounds[:-1], bounds[1:]))]
+
+
+CHUNKS = (
+    tuple(tiles(0, (0, 11, 22, 32)) + tiles(1, (0, 2, 5, 8))),
+    tuple(tiles(2, (0, 15, 30, 44))),
+    tuple(tiles(3, (0, 7, 14, 22), 8)),
+)
+UNITS = CHUNKS[0] + CHUNKS[1] + CHUNKS[2]
+C1, C2, C3 = (tuple(UNITS.index(u) for u in chunk) for chunk in CHUNKS)
 
 
 def where_am_i():
@@ -49,96 +66,388 @@
     return lo + ((hi - lo) // grain // 2) * grain
 
 
-def ag_kernel(*refs):
-    n_arr = 4
-    ins, outs = refs[:n_arr], refs[n_arr:2 * n_arr]
-    local_sem, send_sem, recv_sem, csend_sem, crecv_sem = refs[2 * n_arr:]
+def neighbours(me):
+    return [moved(me, a, d) for a in "xyz" for d in (1, -1)] + [moved(me, "c", 1)]
+
+
+def dot(a, b, dims=((1,), (0,))):
+    return lax.dot_general(a, b, (dims, ((), ())), preferred_element_type=F32)
+
+
+def by_rows(count, size, body):
+    def one(k, _):
+        body(pl.ds(pl.multiple_of(k * size, size), size))
+        return 0
+    lax.fori_loop(0, count // size, one, 0)
+
+
+def columns_of(k, size):
+    return pl.ds(pl.multiple_of(k * size, size), size)
+
+
+def sigmoid(u):
+    return 1.0 / (1.0 + jnp.exp(-u))
+
+
+def rms_factor(v):
+    return lax.rsqrt(jnp.mean(v * v, axis=-1, keepdims=True) + EPSILON)
+
+
+class Gather:
+    def __init__(self, arrays, me, send_sem, recv_sem, csend_sem, crecv_sem):
+        self.arrays, self.me = arrays, me
+        self.send_sem, self.recv_sem, self.csend_sem, self.crecv_sem = send_sem, recv_sem, csend_sem, crecv_sem
+        self.sends = []
+
+    def copy(self, ref, u, slot, to):
+        return pltpu.make_async_remote_copy(src_ref=ref, dst_ref=ref, send_sem=self.send_sem.at[u, slot],
+            recv_sem=self.recv_sem.at[u, slot], device_id=device(to), device_id_type=MESH)
+
+    def ccopy(self, ref, u, slot):
+        return pltpu.make_async_remote_copy(src_ref=ref, dst_ref=ref, send_sem=self.csend_sem.at[u, slot],
+            recv_sem=self.crecv_sem.at[u, slot], device_id=device(moved(self.me, "c", 1)), device_id_type=MESH)
+
+    def go(self, cp):
+        cp.start()
+        self.sends.append(cp)
+
+    def part(self, u, at, stage, half=None):
+        i, s, lo, hi = UNITS[u]
+        rows = SPLIT_ROWS[i]
+        mid = middle(lo, hi, rows)
+        lo, hi = (lo, hi) if half is None else ((lo, mid), (mid, hi))[half]
+        return block(self.arrays[i], at, ORDERS[s][:stage], lo, hi, rows)
+
+    def axis(self, u, stage):
+        return ORDERS[UNITS[u][1]][stage]
+
+    def begin(self, units, stage):
+        for u in units:
+            a = self.axis(u, stage)
+            mine = self.part(u, self.me, stage)
+            self.go(self.copy(mine, u, 4 * stage, moved(self.me, a, 1)))
+            self.go(self.copy(mine, u, 4 * stage + 1, moved(self.me, a, -1)))
+            if stage == 2:
+                self.go(self.ccopy(mine, u, 0))
+
+    def relay(self, units, stage):
+        for u in units:
+            a = self.axis(u, stage)
+            above, below = moved(self.me, a, 1), moved(self.me, a, -1)
+            self.copy(self.part(u, below, stage), u, 4 * stage, below).wait_recv()
+            self.go(self.copy(self.part(u, below, stage, 0), u, 4 * stage + 2, above))
+            self.copy(self.part(u, above, stage), u, 4 * stage + 1, above).wait_recv()
+            self.go(self.copy(self.part(u, above, stage, 1), u, 4 * stage + 3, below))
+            if stage == 2:
+                self.go(self.ccopy(self.part(u, below, stage), u, 1))
+                self.go(self.ccopy(self.part(u, above, stage), u, 2))
+
+    def finish(self, units, stage):
+        for u in units:
+            a = self.axis(u, stage)
+            far = moved(self.me, a, 2)
+            for half in range(2):
+                self.copy(self.part(u, far, stage, half), u, 4 * stage + 2 + half, moved(self.me, a, 1)).wait_recv()
+            if stage == 2:
+                self.go(self.ccopy(self.part(u, far, stage), u, 3))
+
+    def arrive(self, units):
+        sib = moved(self.me, "c", 1)
+        for u in units:
+            for k, by in enumerate((0, -1, 1, 2)):
+                self.ccopy(self.part(u, moved(sib, self.axis(u, 2), by), 2), u, k).wait_recv()
+
+    def drain(self):
+        for cp in self.sends:
+            cp.wait_send()
+
+
+class Scan:
+    def __init__(self, local, came, going, carried, sems):
+        self.me, self.dp = lax.axis_index("seq"), lax.axis_index("dp")
+        self.local, self.came, self.going, self.carried = local, came, going, carried
+        self.send1, self.recv1, self.send2, self.recv2 = sems
+
+    def to(self, k):
+        return (self.me + k) % N_SEQ
+
+    def out(self, to):
+        return pltpu.make_async_remote_copy(src_ref=self.local.at[to], dst_ref=self.came.at[self.me], send_sem=self.send1.at[to],
+            recv_sem=self.recv1.at[self.me], device_id=(self.dp, to), device_id_type=MESH)
+
+    def back(self, to):
+        return pltpu.make_async_remote_copy(src_ref=self.going.at[to], dst_ref=self.carried.at[self.me], send_sem=self.send2.at[to],
+            recv_sem=self.recv2.at[self.me], device_id=(self.dp, to), device_id_type=MESH)
+
+    def arrival(self, ref, ssem, rsem, frm):
+        return pltpu.make_async_remote_copy(src_ref=ref.at[frm], dst_ref=ref.at[frm], send_sem=ssem.at[frm],
+            recv_sem=rsem.at[frm], device_id=(self.dp, self.to(1)), device_id_type=MESH)
+
+    def each(self, body):
+        def one(k, _):
+            body(self.to(k))
+            return 0
+        lax.fori_loop(1, N_SEQ, one, 0)
+
+    def start(self):
+        self.each(lambda to: self.out(to).start())
+        self.came[self.me] = self.local[self.me]
+
+    def join(self, tags_all, decays, backward):
+        self.each(lambda frm: self.arrival(self.came, self.send1, self.recv1, frm).wait_recv())
+        micro, head = self.me // H, self.me % H
+        fade = jnp.exp(-float(HD) * jnp.full((1, HD), decays[head], F32))
+        first = lambda b: tags_all[b, pl.ds(2 * micro, 1), :]
+        last = lambda b: tags_all[b, pl.ds(2 * micro + 1, 1), :]
+        acc = jnp.zeros((HD, HD), F32)
+        previous = None
+        for b in (range(N_SEQ - 1, -1, -1) if backward else range(N_SEQ)):
+            self.going[b] = acc.astype(LOW)
+            if previous is None:
+                acc = self.came[b].astype(F32)
+            else:
+                near = (last(b) == first(previous)) if backward else (first(b) == last(previous))
+                acc = self.came[b].astype(F32) + jnp.where((first(b) == last(b)) & near, fade, 0.0) * acc
+            previous = b
+        self.carried[self.me] = self.going[self.me]
+        self.each(lambda to: self.back(to).start())
+
+    def finish(self):
+        self.each(lambda frm: self.arrival(self.carried, self.send2, self.recv2, frm).wait_recv())
+
+    def drain(self):
+        def one(to):
+            self.out(to).wait_send()
+            self.back(to).wait_send()
+        self.each(one)
+
+
+def spread(row):
+    across = jnp.broadcast_to(row, (HD, HD))
+    return across.T, across
+
+
+def row_index():
+    return lax.broadcasted_iota(jnp.int32, (HD, HD), 0).astype(F32)
+
+
+def column_index():
+    return lax.broadcasted_iota(jnp.int32, (HD, HD), 1).astype(F32)
+
+
+def pair_at(p):
+    micro, head = p // H, p % H
+    return micro, head, pl.ds(pl.multiple_of(micro * HD, HD), HD), pl.ds(pl.multiple_of(head * HD, HD), HD)
+
+
+def forward_kernel(*refs):
+    (x, ids, decays), small = refs[:3], refs[3:11]
+    (act, pre, mixed, resid, up, carried, tags_all, out_in, out_output, out_up, out_down) = refs[11:22]
+    (w_in, w_output, w_up, w_flat, w_down, first_in, qs, ks, vs, gated, second, product, local, came, going,
+     spare, tag, allowed, kept_mask, ids_down,
+     send_sem, recv_sem, csend_sem, crecv_sem, tag_send, tag_recv, s1, r1, s2, r2, out_sem) = refs[22:]
     me = where_am_i()
+    seq, dp = lax.axis_index("seq"), lax.axis_index("dp")
+    to = lambda k: (seq + k) % N_SEQ
     barrier = pltpu.get_barrier_semaphore()
-    partners = [moved(me, a, d) for a in "xyz" for d in (1, -1)] + [moved(me, "c", 1)]
-    for other in partners:
+    close = neighbours(me)
+    for other in close:
         pl.semaphore_signal(barrier, inc=1, device_id=device(other), device_id_type=MESH)
 
-    copies = []
-    for i in range(n_arr):
-        cp = pltpu.make_async_copy(
-            ins[i], outs[i].at[me["y"], me["x"] % 2, me["z"], me["x"] // 2, me["c"]], local_sem.at[i])
+    def greet(k, _):
+        pl.semaphore_signal(barrier, inc=1, device_id=(dp, to(k)), device_id_type=MESH)
+        return 0
+    lax.fori_loop(1, N_SEQ, greet, 0)
+
+    here = (me["y"], me["x"] % 2, me["z"], me["x"] // 2, me["c"])
+    def place(src, target, base, width):
+        n = width // 128
+        spare[pl.ds(0, 8 * n), :] = src[...].astype(F32)
+        for c in range(n):
+            target[(*here, slice(None), pl.ds(base + c * 128, 128))] = spare[pl.ds(c, 8, stride=n), :].astype(LOW)
+    for k in range(4):
+        place(small[k], w_in, k * D, D)
+    place(small[4], w_output, 0, D)
+    place(small[5], w_up, 0, FF)
+    place(small[6], w_up, FF, FF)
+    w_flat[here] = small[7][...]
+    for m in range(2):
+        down, across = spread(ids[m:m + 1, :])
+        ids_down[m] = down
+        allowed[m] = jnp.where((down == across) & (row_index() >= column_index()), 1.0, 0.0)
+        kept_mask[m] = jnp.where(down == jnp.broadcast_to(ids[m:m + 1, HD - 1:HD], (HD, HD)), 1.0, 0.0)
+    tag[...] = jnp.zeros((8, HD), F32)
+    for m in range(2):
+        tag[2 * m:2 * m + 1, :] = jnp.broadcast_to(ids[m:m + 1, 0:1], (1, HD))
+        tag[2 * m + 1:2 * m + 2, :] = jnp.broadcast_to(ids[m:m + 1, HD - 1:HD], (1, HD))
+    tags_all[seq] = tag[...]
+    pl.semaphore_wait(barrier, len(close) + N_SEQ - 1)
+
+    g = Gather((w_in, w_output, w_up, w_flat), me, send_sem, recv_sem, csend_sem, crecv_sem)
+    scan = Scan(local, came, going, carried, (s1, r1, s2, r2))
+    g.begin(C1, 0)
+    g.begin(C2, 0)
+    g.begin(C3, 0)
+
+    def tag_copy(other):
+        return pltpu.make_async_remote_copy(src_ref=tag, dst_ref=tags_all.at[seq], send_sem=tag_send.at[other],
+            recv_sem=tag_recv.at[seq], device_id=(dp, other), device_id_type=MESH)
+    scan.each(lambda other: tag_copy(other).start())
+
+    def norm_in(rows):
+        v = x[rows, :].astype(F32)
+        first_in[rows, :] = (v * rms_factor(v)).astype(LOW)
+    by_rows(ROWS, 32, norm_in)
+
+    g.relay(C1, 0)
+    g.relay(C2, 0)
+    g.relay(C3, 0)
+    g.finish(C1, 0)
+    g.begin(C1, 1)
+    g.finish(C2, 0)
+    g.begin(C2, 1)
+    g.finish(C3, 0)
+    g.begin(C3, 1)
+    g.relay(C1, 1)
+    g.relay(C2, 1)
+    g.relay(C3, 1)
+    g.finish(C1, 1)
+    g.begin(C1, 2)
+    g.finish(C2, 1)
+    g.finish(C3, 1)
+    g.relay(C1, 2)
+    g.begin(C2, 2)
+    g.finish(C1, 2)
+    g.arrive(C1)
+    keep = [pltpu.make_async_copy(w_in, out_in, out_sem.at[0]), pltpu.make_async_copy(w_output, out_output, out_sem.at[1])]
+    for cp in keep:
         cp.start()
-        copies.append(cp)
-    pl.semaphore_wait(barrier, len(partners))
-    for cp in copies:
+
+    m_in = w_in.reshape(D, 4 * D)
+    def project(k, _):
+        cols = columns_of(k, 512)
+        pre[:, cols] = dot(first_in[...], m_in[:, cols])
+        return 0
+    lax.fori_loop(0, 8, project, 0)
+    g.relay(C2, 2)
+    g.begin(C3, 2)
+
+    def rows_of_heads(rows):
+        q = pre[rows, 0:D]
+        qs[rows, :] = (q * sigmoid(q)).astype(LOW)
+        k = pre[rows, D:2 * D]
+        ks[rows, :] = (k * sigmoid(k)).astype(LOW)
+        vs[rows, :] = pre[rows, 2 * D:3 * D].astype(LOW)
+    by_rows(ROWS, 16, rows_of_heads)
+
+    def states(p, _):
+        micro, head, rows, cols = pair_at(p)
+        keeping = jnp.exp((row_index() - (HD - 1.0)) * decays[head]) * kept_mask[micro]
+        kept = (ks[rows, cols].astype(F32) * keeping).astype(LOW)
+        local[p] = dot(kept, vs[rows, cols], ((0,), (0,))).astype(LOW)
+        return 0
+    lax.fori_loop(0, 2 * H, states, 0)
+    scan.start()
+    g.finish(C2, 2)
+
+    def within(p, _):
+        micro, head, rows, cols = pair_at(p)
+        mask = allowed[micro] * jnp.exp(jnp.minimum(column_index() - row_index(), 0.0) * decays[head])
+        weighted = (dot(qs[rows, cols], ks[rows, cols], ((1,), (1,))) * mask).astype(LOW)
+        mixed[rows, cols] = dot(weighted, vs[rows, cols])
+        return 0
+    lax.fori_loop(0, 2 * H, within, 0)
+    scan.each(lambda frm: pltpu.make_async_remote_copy(src_ref=tag, dst_ref=tags_all.at[frm], send_sem=tag_send.at[frm],
+        recv_sem=tag_recv.at[frm], device_id=(dp, to(1)), device_id_type=MESH).wait_recv())
+    scan.join(tags_all, decays, False)
+    g.relay(C3, 2)
+    scan.finish()
+
+    def crossing(p, _):
+        micro, head, rows, cols = pair_at(p)
+        boundary = jnp.where(seq > 0, tags_all[jnp.maximum(seq - 1, 0), pl.ds(2 * micro + 1, 1), :], -1.0)
+        reaching = jnp.where(ids_down[micro] == boundary, jnp.exp(-(row_index() + 1.0) * decays[head]), 0.0)
+        mixed[rows, cols] += dot(qs[rows, cols], carried[p]) * reaching
+        return 0
+    lax.fori_loop(0, 2 * H, crossing, 0)
+
+    def gate_rows(rows):
+        v = mixed[rows, :]
+        gated[rows, :] = (v * rms_factor(v) * pre[rows, 3 * D:4 * D]).astype(LOW)
+    by_rows(ROWS, 16, gate_rows)
+    m_output = w_output.reshape(D, D)
+    def output(k, _):
+        cols = columns_of(k, 512)
+        resid[:, cols] = x[:, cols].astype(F32) + dot(gated[...], m_output[:, cols])
+        return 0
+    lax.fori_loop(0, 2, output, 0)
+    def norm_second(rows):
+        v = resid[rows, :]
+        second[rows, :] = (v * rms_factor(v)).astype(LOW)
+    by_rows(ROWS, 32, norm_second)
+    g.finish(C3, 2)
+    g.arrive(C2)
+    keep.append(pltpu.make_async_copy(w_up, out_up, out_sem.at[2]))
+    keep[-1].start()
+    m_up = w_up.reshape(D, 2 * FF)
+    def widen(k, _):
+        cols = columns_of(k, 512)
+        up[:, cols] = dot(second[...], m_up[:, cols])
+        return 0
+    lax.fori_loop(0, 11, widen, 0)
+    def multiply(rows):
+        product[rows, :] = (up[rows, 0:FF] * up[rows, FF:2 * FF]).astype(LOW)
+    by_rows(ROWS, 16, multiply)
+    g.arrive(C3)
+    flat = w_flat.reshape(128 * 176, 128)
+    def arrange(k, _):
+        spare[...] = flat[pl.ds(pl.multiple_of(k * 1408, 1408), 1408), :].astype(F32)
+        for c in range(8):
+            w_down[pl.ds(pl.multiple_of(k * 176, 176), 176), c * 128:(c + 1) * 128] = spare[pl.ds(c, 176, stride=8), :].astype(LOW)
+        return 0
+    lax.fori_loop(0, 16, arrange, 0)
+    keep.append(pltpu.make_async_copy(w_down, out_down, out_sem.at[3]))
+    keep[-1].start()
+    def last(k, _):
+        cols = columns_of(k, 512)
+        act[:, cols] = (resid[:, cols] + dot(product[...], w_down[:, cols])).astype(LOW)
+        return 0
+    lax.fori_loop(0, 2, last, 0)
+    for cp in keep:
         cp.wait()
-
-    sends = []
-    def send(src, u, slot, to):
-        cp = pltpu.make_async_remote_copy(src_ref=src, dst_ref=src, send_sem=send_sem.at[u, slot],
-            recv_sem=recv_sem.at[u, slot], device_id=device(to), device_id_type=MESH)
-        cp.start()
-        sends.append(cp)
-
-    def got(ref, u, slot):
-        pltpu.make_async_remote_copy(src_ref=ref, dst_ref=ref, send_sem=send_sem.at[u, slot],
-            recv_sem=recv_sem.at[u, slot], device_id=device(me), device_id_type=MESH).wait_recv()
-
-    def csend(src, u, slot):
-        cp = pltpu.make_async_remote_copy(src_ref=src, dst_ref=src, send_sem=csend_sem.at[u, slot],
-            recv_sem=crecv_sem.at[u, slot], device_id=device(moved(me, "c", 1)), device_id_type=MESH)
-        cp.start()
-        sends.append(cp)
-
-    ctail = []
-    for stage in range(3):
-        for u, (i, s, lo, hi) in enumerate(UNITS):
-            axis, whole = ORDERS[s][stage], ORDERS[s][:stage]
-            mine = block(outs[i], me, whole, lo, hi, SPLIT_ROWS[i])
-            send(mine, u, 4 * stage + 0, moved(me, axis, 1))
-            send(mine, u, 4 * stage + 1, moved(me, axis, -1))
-            if stage == 2:
-                csend(mine, u, 0)
-        for u, (i, s, lo, hi) in enumerate(UNITS):
-            axis, whole = ORDERS[s][stage], ORDERS[s][:stage]
-            rows = SPLIT_ROWS[i]
-            mid = middle(lo, hi, rows)
-            below, above = moved(me, axis, -1), moved(me, axis, 1)
-            got(block(outs[i], below, whole, lo, hi, rows), u, 4 * stage + 0)
-            send(block(outs[i], below, whole, lo, mid, rows), u, 4 * stage + 2, above)
-            got(block(outs[i], above, whole, lo, hi, rows), u, 4 * stage + 1)
-            send(block(outs[i], above, whole, mid, hi, rows), u, 4 * stage + 3, below)
-            if stage == 2:
-                csend(block(outs[i], below, whole, lo, hi, rows), u, 1)
-                csend(block(outs[i], above, whole, lo, hi, rows), u, 2)
-        for u, (i, s, lo, hi) in enumerate(UNITS):
-            axis, whole = ORDERS[s][stage], ORDERS[s][:stage]
-            rows = SPLIT_ROWS[i]
-            mid = middle(lo, hi, rows)
-            far = moved(me, axis, 2)
-            got(block(outs[i], far, whole, lo, mid, rows), u, 4 * stage + 2)
-            got(block(outs[i], far, whole, mid, hi, rows), u, 4 * stage + 3)
-            if stage == 2:
-                csend(block(outs[i], far, whole, lo, hi, rows), u, 3)
-    sib = moved(me, "c", 1)
-    for u, (i, s, lo, hi) in enumerate(UNITS):
-        axis, whole = ORDERS[s][2], ORDERS[s][:2]
-        for k, by in enumerate((0, -1, 1, 2)):
-            ref = block(outs[i], moved(sib, axis, by), whole, lo, hi, SPLIT_ROWS[i])
-            pltpu.make_async_remote_copy(src_ref=ref, dst_ref=ref, send_sem=csend_sem.at[u, k],
-                recv_sem=crecv_sem.at[u, k], device_id=device(sib), device_id_type=MESH).wait_recv()
-    for cp in sends:
-        cp.wait_send()
-
-
-def gather_all(pieces):
-    outs = [jax.ShapeDtypeStruct((4, 2, 4, 2, 2) + p.shape, p.dtype) for p in pieces]
+    scan.each(lambda other: tag_copy(other).wait_send())
+    scan.drain()
+    g.drain()
+
+
+def forward(x, ids, decays, pieces):
+    v = pl.BlockSpec(memory_space=pltpu.VMEM)
+    anywhere = pl.BlockSpec(memory_space=pl.ANY)
+    sds = jax.ShapeDtypeStruct
     n = len(UNITS)
+    outs = [sds((ROWS, D), LOW), sds((ROWS, 4 * D), F32), sds((ROWS, D), F32), sds((ROWS, D), F32), sds((ROWS, 2 * FF), F32),
+        sds((N_SEQ, HD, HD), LOW), sds((N_SEQ, 8, HD), F32),
+        sds(OWNERS + (8, 4 * D), LOW), sds(OWNERS + (8, D), LOW), sds(OWNERS + (8, 2 * FF), LOW), sds((FF, D), LOW)]
+    vm = pltpu.VMEM
+    scratch = [vm(OWNERS + (8, 4 * D), LOW), vm(OWNERS + (8, D), LOW), vm(OWNERS + (8, 2 * FF), LOW), vm(OWNERS + (176, 128), LOW),
+        vm((FF, D), LOW)] + [vm((ROWS, D), LOW)] * 6 + [vm((ROWS, FF), LOW)] + [vm((N_SEQ, HD, HD), LOW)] * 3 + [
+        vm((1408, 128), F32), vm((8, HD), F32)] + [vm((2, HD, HD), F32)] * 3 + [
+        DMA((n, 12)), DMA((n, 12)), DMA((n, 4)), DMA((n, 4))] + [DMA((N_SEQ,))] * 6 + [DMA((4,))]
     return pl.pallas_call(
-        ag_kernel, out_shape=outs,
-        in_specs=[pl.BlockSpec(memory_space=pl.ANY)] * len(pieces),
-        out_specs=[pl.BlockSpec(memory_space=pl.ANY)] * len(pieces),
-        scratch_shapes=[pltpu.SemaphoreType.DMA((4,)), pltpu.SemaphoreType.DMA((n, 12)), pltpu.SemaphoreType.DMA((n, 12)),
-            pltpu.SemaphoreType.DMA((n, 4)), pltpu.SemaphoreType.DMA((n, 4))],
-        compiler_params=pltpu.CompilerParams(collective_id=0, has_side_effects=True),
-        name="gather_weights",
-    )(*pieces)
+        forward_kernel, out_shape=outs,
+        in_specs=[v, v, pl.BlockSpec(memory_space=pltpu.SMEM)] + [v] * 8,
+        out_specs=[v] * 7 + [anywhere] * 4,
+        scratch_shapes=scratch,
+        compiler_params=pltpu.CompilerParams(collective_id=0, has_side_effects=True, vmem_limit_bytes=60 << 20),
+        name="gather_and_forward",
+    )(x, ids, decays, *pieces)
+
+RS_UNITS = (
+    (0, 0, 0, 13 * 128), (0, 1, 13 * 128, 26 * 128), (0, 2, 26 * 128, 32 * 128),
+    (1, 2, 0, 8 * 128),
+    (2, 0, 0, 22 * 128), (2, 1, 22 * 128, 44 * 128),
+    (3, 2, 0, 176),
+)
 
 
 RS_ORDERS = tuple(o[::-1] for o in ORDERS)
@@ -191,7 +500,7 @@
 
 
 def rs_kernel(*refs):
-    n_arr, n = 4, len(UNITS)
+    n_arr, n = 4, len(RS_UNITS)
     ins, outs = refs[:n_arr], refs[n_arr:2 * n_arr]
     refs = refs[2 * n_arr:]
     held, other = refs[:n], refs[n:2 * n]
@@ -207,13 +516,13 @@
     def half_of(i, c, lo, hi, rows):
         every, span = slice(None), pl.ds(lo, hi - lo)
         return ins[i].at[:, :, :, :, c, span if rows else every, every if rows else span]
-    for u, (i, s, lo, hi) in enumerate(UNITS):
+    for u, (i, s, lo, hi) in enumerate(RS_UNITS):
         cp = pltpu.make_async_copy(half_of(i, me["c"], lo, hi, SPLIT_ROWS[i]), held[u], load_sem.at[u])
         cp.start()
         loads.append(cp)
     pl.semaphore_wait(barrier, len(partners))
     sends = []
-    for u, (i, s, lo, hi) in enumerate(UNITS):
+    for u, (i, s, lo, hi) in enumerate(RS_UNITS):
         cp = pltpu.make_async_remote_copy(src_ref=half_of(i, sib["c"], lo, hi, SPLIT_ROWS[i]), dst_ref=other[u],
             send_sem=csend_sem.at[u], recv_sem=crecv_sem.at[u], device_id=device(sib), device_id_type=MESH)
         cp.start()
@@ -230,7 +539,7 @@
             recv_sem=recv_sem.at[u, stage, slot], device_id=device(sib), device_id_type=MESH).wait_recv()
 
     def spans(u):
-        i, s, lo, hi = UNITS[u]
+        i, s, lo, hi = RS_UNITS[u]
         width = hi - lo
         return s, SPLIT_ROWS[i], width, middle(0, width, SPLIT_ROWS[i])
 
@@ -261,7 +570,7 @@
                 accumulate(part(held[u], to, fixed, (), lo, hi, rows), [came], dims)
                 send(part(held[u], to, fixed, (), 0, width, rows), part(slots[stage][u], me, (), fixed, 0, width, rows, (1 + k,)), u, stage, 2 + k, to)
         for u in range(n):
-            i, _, lo, hi = UNITS[u]
+            i, _, lo, hi = RS_UNITS[u]
             s, rows, width, mid = spans(u)
             order = RS_ORDERS[s]
             fixed = order[:stage + 1]
@@ -283,9 +592,9 @@
 
 def scatter_all(grads):
     outs = [jax.ShapeDtypeStruct(g.shape[5:], jnp.float32) for g in grads]
-    n = len(UNITS)
+    n = len(RS_UNITS)
     held, slots = [], [[], [], []]
-    for i, s, lo, hi in UNITS:
+    for i, s, lo, hi in RS_UNITS:
         tail = (hi - lo, 128) if SPLIT_ROWS[i] else (8, hi - lo)
         held.append(pltpu.VMEM(live_dims(()) + tail, jnp.bfloat16))
         for k in range(3):
@@ -394,26 +703,11 @@
     )(local, tags, fade)
 
 
-D = 1024
-H = 8
-HD = 128
-FF = 2816
-EPSILON = 1e-06
-
-
-def swish(values):
-    return values * jax.nn.sigmoid(values)
-
-
 def swish_slope(values):
     sigma = jax.nn.sigmoid(values)
     return sigma * (1.0 + values * (1.0 - sigma))
 
 
-def rms_factor(values):
-    return lax.rsqrt(jnp.mean(values * values, axis=-1, keepdims=True) + EPSILON)
-
-
 def norm_back(upstream, normed, factor):
     return factor * (upstream - normed * jnp.mean(upstream * normed, axis=-1, keepdims=True))
 
@@ -422,26 +716,16 @@
     return jnp.einsum(form, left_op, right_op, preferred_element_type=jnp.float32)
 
 
-def on_device(hidden_in, seg_ids, decay_rates, grad_out, w_query, w_key, w_value, w_gate, w_output, w_left, w_right, w_down):
+def on_device(hidden_in, seg_ids, decay_rates, grad_out, *weights):
     micros, length = hidden_in.shape[0], hidden_in.shape[2]
     rows = micros * length
     low = jnp.bfloat16
-    pieces = [
-        jnp.concatenate([w.reshape(8, D) for w in (w_query, w_key, w_value, w_gate)], axis=1),
-        w_output.reshape(8, D),
-        jnp.concatenate([w.reshape(8, FF) for w in (w_left, w_right)], axis=1),
-        w_down.reshape(176, 128),
-    ]
-    m_in, m_output, m_up, m_down = gather_all(pieces)
-    m_in = m_in.reshape(D, 4 * D)
-    m_output = m_output.reshape(D, D)
-    m_up = m_up.reshape(D, 2 * FF)
-    m_down = m_down.reshape(FF, D)
-
     segments = seg_ids.reshape(micros, length)
-    tags = jnp.stack([segments[0, 0], segments[0, -1], segments[1, 0], segments[1, -1]]).astype(jnp.float32)
-    tags = jnp.concatenate([tags, jnp.zeros((4,), jnp.float32)])[:, None] * jnp.ones((8, 128), jnp.float32)
-    fade = jnp.exp(-length * decay_rates)[:, None] * jnp.ones((8, 128), jnp.float32)
+    tokens = segments.astype(jnp.float32)
+    (act, pre, mixed, resid, up, carried, tags_all, m_in, m_output, m_up, m_down) = forward(
+        hidden_in.reshape(rows, D), tokens, decay_rates, [w.reshape(-1, 128) for w in weights])
+    m_in, m_output, m_up = m_in.reshape(D, 4 * D), m_output.reshape(D, D), m_up.reshape(D, 2 * FF)
+
     places = jnp.arange(length, dtype=jnp.float32)
     distance = places[:, None] - places[None, :]
     allowed = (distance >= 0.0)[None] & (segments[:, :, None] == segments[:, None, :])
@@ -449,21 +733,16 @@
         allowed[:, None], jnp.exp(-decay_rates[None, :, None, None] * jnp.maximum(distance, 0.0)[None, None]), 0.0)
     rising = jnp.exp(-(places + 1.0)[None, :, None] * decay_rates)
     falling = jnp.exp(-(length - 1.0 - places)[None, :, None] * decay_rates)
-
+    fade = jnp.exp(-length * decay_rates)[:, None] * jnp.ones((8, 128), jnp.float32)
     inputs = hidden_in.reshape(rows, D).astype(jnp.float32)
     factor_in = rms_factor(inputs)
     normed_in = inputs * factor_in
     first_in = normed_in.astype(low)
-    pre = matmul("rd,de->re", first_in, m_in)
     q_pre, k_pre, v_pre, gate = (pre[:, k * D:(k + 1) * D] for k in range(4))
     heads = (micros, length, H, HD)
-    queries = swish(q_pre).astype(low).reshape(heads)
-    key_rows = swish(k_pre).astype(low).reshape(heads)
+    queries = (q_pre * jax.nn.sigmoid(q_pre)).astype(low).reshape(heads)
+    key_rows = (k_pre * jax.nn.sigmoid(k_pre)).astype(low).reshape(heads)
     value_rows = v_pre.astype(low).reshape(heads)
-    keeping = falling * (segments == segments[:, -1:]).astype(jnp.float32)[:, :, None]
-    kept = (key_rows.astype(jnp.float32) * keeping[..., None]).astype(low)
-    local = matmul("sjhd,sjhe->shde", kept, value_rows).astype(low).reshape(micros * H, HD, HD)
-    carried, tags_all = scan_states(local, tags, fade, False)
     carried = carried.reshape(micros, H, HD, HD)
     me = lax.axis_index("seq")
     ends = tags_all[:, :4, 0]
@@ -471,24 +750,17 @@
     after = jnp.where(me < 15, ends[jnp.minimum(me + 1, 15)], -1.0)
     boundary = before[1::2]
     reverse_tag = after[0::2]
-    tokens = segments.astype(jnp.float32)
     scores = matmul("sihd,sjhd->shij", queries, key_rows)
     weighted = (scores * decay_mask).astype(low)
-    within = matmul("shij,sjhe->sihe", weighted, value_rows)
     reaching = rising * (tokens == boundary[:, None]).astype(jnp.float32)[:, :, None]
-    crossed = matmul("sihd,shde->sihe", queries, carried) * reaching[..., None]
-    mixed = (within + crossed).reshape(rows, D)
     factor_mix = rms_factor(mixed)
     normed_mix = mixed * factor_mix
     gated = (normed_mix * gate).astype(low)
-    resid = inputs + matmul("rd,de->re", gated, m_output)
     factor_res = rms_factor(resid)
     normed_res = resid * factor_res
     second = normed_res.astype(low)
-    up = matmul("rd,df->rf", second, m_up)
     left_proj, right_proj = up[:, :FF], up[:, FF:]
     product = (left_proj * right_proj).astype(low)
-    result = (resid + matmul("rf,fd->rd", product, m_down)).astype(low)
 
     d_branch = grad_out.reshape(rows, D)
     cotangent = d_branch.astype(jnp.float32)
@@ -508,6 +780,8 @@
     opening = rising * (segments == segments[:, :1]).astype(jnp.float32)[:, :, None]
     opened = (queries.astype(jnp.float32) * opening[..., None]).astype(low)
     back_local = matmul("sihd,sihe->shde", opened, d_mixed).astype(low).reshape(micros * H, HD, HD)
+    tags = jnp.stack([segments[0, 0], segments[0, -1], segments[1, 0], segments[1, -1]]).astype(jnp.float32)
+    tags = jnp.concatenate([tags, jnp.zeros((4,), jnp.float32)])[:, None] * jnp.ones((8, 128), jnp.float32)
     reverse, _ = scan_states(back_local, tags, fade, True)
     reverse = reverse.reshape(micros, H, HD, HD)
     d_query = matmul("shij,sjhd->sihd", d_scores, key_rows)
@@ -527,13 +801,12 @@
     d_first = matmul("re,de->rd", d_pre, m_in)
     d_inputs = d_resid + norm_back(d_first, normed_in, factor_in)
 
-    owners = (4, 2, 4, 2, 2)
     s_in, s_output, s_up, s_down = scatter_all([
-        g_in.reshape(owners + (8, 4 * D)), g_output.reshape(owners + (8, D)),
-        g_up.reshape(owners + (8, 2 * FF)), g_down.reshape(owners + (176, 128))])
+        g_in.reshape(OWNERS + (8, 4 * D)), g_output.reshape(OWNERS + (8, D)),
+        g_up.reshape(OWNERS + (8, 2 * FF)), g_down.reshape(OWNERS + (176, 128))])
     shape = hidden_in.shape
     return (
-        result.reshape(shape), d_inputs.reshape(shape),
+        act.reshape(shape), d_inputs.reshape(shape),
         *(s_in[:, k * D:(k + 1) * D].reshape(-1) for k in range(4)),
         s_output.reshape(-1), s_up[:, :FF].reshape(-1), s_up[:, FF:].reshape(-1), s_down.reshape(-1),
     )

time: 351 us -> 320 us (0.912)
  local copies, waits for them, and re-layouts: 54 us -> 36 us
  matrix products: 68.2 us -> 57.2 us
  other arithmetic: 18.2 us -> 14.3 us
    pallas_call x1, Pallas kernels: 78.4 us -> 104 us  [forward(): pl.pallas_call(forward_kernel, out_shape=outs, in_specs=[v, v, pl.BlockSp...]
    pallas_call x2 -> x1, Pallas kernels: 48 us -> 23.9 us  [scan_states(): pl.pallas_call(functools.partial(scan_kernel, backward), out_shape=[jax.S...]
    reshape x11 -> x2, local copies, waits for them, and re-layouts: 26.3 us -> 11.9 us  [the longest x1 9.73 us: on_device(): g_down.reshape(OWNERS + (176, 128))]
    dot_general x24 -> x16, matrix products: 68.2 us -> 57.2 us  [matmul(): jnp.einsum(form, left_op, right_op, preferred_element_type=jnp.float32)]
    unnamed x75 -> x68, local copies, waits for them, and re-layouts: 11.5 us -> 12.9 us
where the time goes in v2:
time: 320 us; the launch traced here: 318 us
  Pallas kernels  209 us (65%)
  matrix products  57.2 us (18%)
  local copies, waits for them, and re-layouts  36 us (11%)
  other arithmetic  14.3 us (4%)
    pallas_call x1, Pallas kernels, forward(): pl.pallas_call(forward_kernel, out_shape=outs, in_specs=[v, v, pl.BlockSp...  104 us
    pallas_call x1, Pallas kernels, scatter_all(): pl.pallas_call(rs_kernel, out_shape=outs, in_specs=[pl.BlockSpec(memory_s...  81.2 us
    dot_general x16, matrix products, matmul(): jnp.einsum(form, left_op, right_op, preferred_element_type=jnp.float32)  57.2 us
    pallas_call x1, Pallas kernels, scan_states(): pl.pallas_call(functools.partial(scan_kernel, backward), out_shape=[jax.S...  23.9 us
    unnamed x68, local copies, waits for them, and re-layouts  12.9 us
    reshape x1, local copies, waits for them, and re-layouts, on_device(): g_down.reshape(OWNERS + (176, 128))  9.73 us

profile of v2, /device:TPU:1, one launch (start us, length us, event | category | flops | bytes accessed | tf_op | source)
XLA Modules:
  0.0 317.9 jit_solution(16037356726421773198)
XLA Ops:
  1.9 104.2 %gather_and_forward.1 = (bf16[256,1024]{1,0:T(8,128)(2,1)}, f32[256,4096]{1,0:T(8,128)}, f32[256,1024]{1,0:T(8,128)}, f32[256,1024]{1,0:T(8,128)}, f32[256,5632]...) custom-call(bf16[256,1024]{1,0:T(8,128)(2,1)} %bitcast.144, ...), custom_call_target="tpu_custom_call" | custom-call | tf_op jit(solution)/shard_map/gather_and_forward/pallas_call | solution.py:436
  107.5 6.3 %multiply_convert_fusion.2 = (bf16[256,2816]{1,0:T(8,128)(2,1)S(1)}, bf16[256,2816]{1,0:T(8,128)(2,1)S(1)}) fusion(f32[256,5632]{1,0:T(8,128)} %get-tuple-element.29, bf16[2816,1024]{1,0:T(8,128)(2,1)} %get-tuple-element.28, bf16[256,1024]{1,0:T(8,128)(2,1)} %bitcast.159), kind=kOutput, calls=%fused_computation.7 | convolution fusion | flops 1479278592 | bytes 14942208 | tf_op jit(solution)/shard_map/rd,fd->rf/dot_general | solution.py:716
  113.9 7.4 %multiply_reduce_fusion.4 = (f32[256]{0:T(256)S(1)}, f32[256,1024]{1,0:T(8,128)S(1)}) fusion(f32[256,1024]{1,0:T(8,128)S(1)} %copy-done.2, f32[256]{0:T(256)S(1)} %add_rsqrt_fusion.1, bf16[1024,5632]{1,0:T(8,128)(2,1)} %bitcast.186, bf16[256,2816]{1,0:T(8,128)(2,1)S(1)} %get-tuple-element.65, bf16[256,2816]{1,0:T(8,128)(2,1)S(1)} %get-tuple-element.64), kind=kOutput, calls=%fused_computation.50 | convolution fusion | flops 2959343360 | bytes 16517120 | tf_op jit(solution)/shard_map/rf,df->rd/dot_general | solution.py:716
  129.7 1.5 convolution_bitcast_fusion.6
  131.8 2.7 fusion.6
  134.5 2.5 copy.44
  137.1 3.0 fusion.11
  140.9 2.1 copy.45
  143.0 2.9 convolution_bitcast_fusion.2
  145.9 2.3 convolution_convert_fusion.4
  148.8 2.7 add_convert_fusion
  152.8 23.9 %scan_back.1 = (bf16[16,128,128]{2,1,0:T(8,128)(2,1)}, f32[16,8,128]{2,1,0:T(8,128)}) custom-call(bf16[16,128,128]{2,1,0:T(8,128)(2,1)} %bitcast.152, f32[8,128]{1,0:T(8,128)} %mul.317.refs_1_, f32[8,128]{1,0:T(8,128)} %mul.319.refs_2_), custom_call_target="tpu_custom_call" | custom-call | tf_op jit(solution)/shard_map/scan_back/pallas_call | solution.py:696
  176.7 2.7 fusion.7
  182.9 2.7 fusion.4
  185.7 2.5 copy.49
  188.2 2.1 fusion.10
  190.4 6.4 %multiply_reduce_fusion = (f32[256]{0:T(256)S(1)}, f32[256,1024]{1,0:T(8,128)S(1)}) fusion(f32[256]{0:T(256)S(1)} %rsqrt_bitcast_fusion, bf16[2,1,128,1024]{3,2,1,0:T(8,128)(2,1)S(1)} %copy-done.6, bf16[1024,4096]{1,0:T(8,128)(2,1)} %bitcast.187, bf16[256,1024]{1,0:T(8,128)(2,1)} %get-tuple-element.70, bf16[256,1024]{1,0:T(8,128)(2,1)} %bitcast.163, ...), kind=kOutput, calls=%fused_computation.36 | convolution fusion | flops 2156920576 | bytes 12060672 | tf_op jit(solution)/shard_map/re,de->rd/dot_general | solution.py:716
  198.1 5.4 %convolution_convert_fusion.1 = bf16[1024,4096]{1,0:T(8,128)(2,1)} fusion(bf16[256,1024]{1,0:T(8,128)(2,1)S(1)} %bitcast.145, f32[256]{0:T(256)S(1)} %rsqrt_bitcast_fusion, bf16[256,1024]{1,0:T(8,128)(2,1)S(1)} %copy-done.21, bf16[256,1024]{1,0:T(8,128)(2,1)S(1)} %bitcast.164, bf16[256,1024]{1,0:T(8,128)(2,1)S(1)} %fusion.10, ...), kind=kOutput, calls=%fused_computation.1 | convolution fusion | flops 2160852992 | bytes 11011072 | tf_op jit(solution)/shard_map/rd,re->de/dot_general | solution.py:716
  203.5 3.7 %convolution_convert_fusion.3 = bf16[1024,1024]{1,0:T(8,128)(2,1)} fusion(f32[256,4096]{1,0:T(8,128)} %get-tuple-element.31, f32[256,1024]{1,0:T(8,128)S(1)} %copy-done, f32[256]{0:T(256)S(1)} %add_rsqrt_fusion, f32[256,1024]{1,0:T(8,128)S(1)} %get-tuple-element.97), kind=kOutput, calls=%fused_computation.9 | convolution fusion | flops 538968064 | bytes 5243904 | tf_op jit(solution)/shard_map/rd,re->de/dot_general | solution.py:716
  207.2 6.3 %convolution_convert_fusion = bf16[1024,5632]{1,0:T(8,128)(2,1)} fusion(bf16[256,2816]{1,0:T(8,128)(2,1)S(1)} %copy-done.17, bf16[256,2816]{1,0:T(8,128)(2,1)S(1)} %copy-done.15, f32[256,1024]{1,0:T(8,128)S(1)} %copy-done.3, f32[256]{0:T(256)S(1)} %add_rsqrt_fusion.1), kind=kOutput, calls=%fused_computation | convolution fusion | flops 2964848640 | bytes 15467520 | tf_op jit(solution)/shard_map/rd,rf->df/dot_general | solution.py:716
  213.4 4.3 %convolution_convert_fusion.2 = bf16[2816,1024]{1,0:T(8,128)(2,1)} fusion(bf16[256,1024]{1,0:T(8,128)(2,1)S(1)} %bitcast.160, f32[256,5632]{1,0:T(8,128)S(1)} %bitcast.149), kind=kOutput, calls=%fused_computation.2 | convolution fusion | flops 1480720384 | bytes 12058624 | tf_op jit(solution)/shard_map/rf,rd->fd/dot_general | solution.py:716
  217.7 9.7 %reshape.405.refs_3_ = bf16[4,2,4,2,2,176,128]{6,5,4,3,2,1,0:T(8,128)(2,1)} reshape(bf16[2816,1024]{1,0:T(8,128)(2,1)} %convolution_convert_fusion.2) | data formatting | bytes 11534336 | tf_op jit(solution)/shard_map/reshape | solution.py:806
  227.4 81.2 %scatter_grads.1 = (f32[8,4096]{1,0:T(8,128)}, f32[8,1024]{1,0:T(8,128)}, f32[8,5632]{1,0:T(8,128)}, f32[176,128]{1,0:T(8,128)}) custom-call(bf16[4,2,4,2,2,8,4096]{6,5,4,3,2,1,0:T(8,128)(2,1)} %bitcast.142, bf16[4,2,4,2,2,8,1024]{6,5,4,3,2,1,0:T(8,128)(2,1)} %bitcast.143, bf16[4,2,4,2,2,8,5632]{6,5,4,3,2,1,0:T(8,128)(2,1)} %bitcast.138, ...), custom_call_target="tpu_custom_call" | custom-call | tf_op jit(solution)/shard_map/scatter_grads/pallas_call | solution.py:602
  316.4 1.5 copy.99
  (107 shorter events, 26.8 us)
Async XLA Ops:
  107.5 6.3 %copy-start.2 = (f32[256,1024]{1,0:T(8,128)S(1)}, f32[256,1024]{1,0:T(8,128)}, u32[]{:S(2)}) copy-start(f32[256,1024]{1,0:T(8,128)} %get-tuple-element.27) | copy-start | bytes 3145732
  113.8 7.5 %copy-start.14 = (bf16[256,2816]{1,0:T(8,128)(2,1)}, bf16[256,2816]{1,0:T(8,128)(2,1)S(1)}, u32[]{:S(2)}) copy-start(bf16[256,2816]{1,0:T(8,128)(2,1)S(1)} %get-tuple-element.64) | copy-start | bytes 4325380
  113.8 7.5 %copy-start.16 = (bf16[256,2816]{1,0:T(8,128)(2,1)}, bf16[256,2816]{1,0:T(8,128)(2,1)S(1)}, u32[]{:S(2)}) copy-start(bf16[256,2816]{1,0:T(8,128)(2,1)S(1)} %get-tuple-element.65) | copy-start | bytes 4325380
  113.9 7.5 %copy-start = (f32[256,1024]{1,0:T(8,128)S(1)}, f32[256,1024]{1,0:T(8,128)}, u32[]{:S(2)}) copy-start(f32[256,1024]{1,0:T(8,128)} %get-tuple-element.32) | copy-start | bytes 3145732
  113.9 7.5 %copy-start.12 = (bf16[2,1,128,1024]{3,2,1,0:T(8,128)(2,1)S(1)}, bf16[2,1,128,1024]{3,2,1,0:T(8,128)(2,1)}, u32[]{:S(2)}) copy-start(bf16[2,1,128,1024]{3,2,1,0:T(8,128)(2,1)} %param.15) | copy-start | bytes 1572868
  113.9 8.7 %copy-start.10 = (bf16[4,2,4,2,2,8,1024]{6,5,4,3,2,1,0:T(8,128)(2,1)S(1)}, bf16[4,2,4,2,2,8,1024]{6,5,4,3,2,1,0:T(8,128)(2,1)}, u32[]{:S(2)}) copy-start(bf16[4,2,4,2,2,8,1024]{6,5,4,3,2,1,0:T(8,128)(2,1)} %get-tuple-element.33) | copy-start | bytes 6291460
  121.3 2.3 copy-start.1
  124.6 2.0 copy-start.24
  124.6 2.2 copy-start.22
  126.5 2.7 copy-start.11
  126.6 4.6 %copy-start.23 = (f32[16,8,128]{2,1,0:T(8,128)S(1)}, f32[16,8,128]{2,1,0:T(8,128)}, u32[]{:S(2)}) copy-start(f32[16,8,128]{2,1,0:T(8,128)} %get-tuple-element.35) | copy-start | bytes 196612
  126.8 2.1 copy-start.7
  148.2 33.4 %copy-start.4 = (bf16[2,128,8,128]{1,3,2,0:T(8,128)(2,1)S(1)}, bf16[2,128,8,128]{1,3,2,0:T(8,128)(2,1)}, u32[]{:S(2)}) copy-start(bf16[2,128,8,128]{1,3,2,0:T(8,128)(2,1)} %copy.45) | copy-start | bytes 1572868
  182.9 7.4 %copy-start.6 = (bf16[2,1,128,1024]{3,2,1,0:T(8,128)(2,1)S(1)}, bf16[2,1,128,1024]{3,2,1,0:T(8,128)(2,1)}, u32[]{:S(2)}) copy-start(bf16[2,1,128,1024]{3,2,1,0:T(8,128)(2,1)} %param.12) | copy-start | bytes 1572868
  190.3 7.7 %copy-start.19 = (bf16[32,8,8,128]{3,1,2,0:T(8,128)(2,1)S(1)}, bf16[32,8,8,128]{3,1,2,0:T(8,128)(2,1)}, u32[]{:S(2)}) copy-start(bf16[32,8,8,128]{3,1,2,0:T(8,128)(2,1)} %copy.90) | copy-start | bytes 1572868
  190.3 7.7 %copy-start.20 = (bf16[256,1024]{1,0:T(8,128)(2,1)S(1)}, bf16[256,1024]{1,0:T(8,128)(2,1)}, u32[]{:S(2)}) copy-start(bf16[256,1024]{1,0:T(8,128)(2,1)} %get-tuple-element.66) | copy-start | bytes 1572868
  190.3 7.7 %copy-start.21 = (bf16[256,1024]{1,0:T(8,128)(2,1)S(1)}, bf16[256,1024]{1,0:T(8,128)(2,1)}, u32[]{:S(2)}) copy-start(bf16[256,1024]{1,0:T(8,128)(2,1)} %get-tuple-element.70) | copy-start | bytes 1572868
  203.5 3.7 %copy-start.3 = (f32[256,1024]{1,0:T(8,128)S(1)}, f32[256,1024]{1,0:T(8,128)}, u32[]{:S(2)}) copy-start(f32[256,1024]{1,0:T(8,128)} %get-tuple-element.27) | copy-start | bytes 3145732
  203.5 3.7 %copy-start.15 = (bf16[256,2816]{1,0:T(8,128)(2,1)S(1)}, bf16[256,2816]{1,0:T(8,128)(2,1)}, u32[]{:S(2)}) copy-start(bf16[256,2816]{1,0:T(8,128)(2,1)} %copy-done.14) | copy-start | bytes 4325380
  203.5 3.7 %copy-start.17 = (bf16[256,2816]{1,0:T(8,128)(2,1)S(1)}, bf16[256,2816]{1,0:T(8,128)(2,1)}, u32[]{:S(2)}) copy-start(bf16[256,2816]{1,0:T(8,128)(2,1)} %copy-done.16) | copy-start | bytes 4325380
  203.5 10.0 %slice-start = ((s8[5767168]{0:T(1024)(128)(4,1)}), s8[4194304]{0:T(1024)(128)(4,1)S(1)}, s32[]{:S(2)}) async-start(s8[5767168]{0:T(1024)(128)(4,1)} %bitcast.148), calls=%async_computation | async-start | bytes 8388608
  207.1 6.3 %slice-start.1 = ((s8[5767168]{0:T(1024)(128)(4,1)}), s8[1572864]{0:T(1024)(128)(4,1)S(1)}, s32[]{:S(2)}) async-start(s8[5767168]{0:T(1024)(128)(4,1)} %bitcast.148), calls=%async_computation.1 | async-start | bytes 3145728
  207.1 6.3 %copy-start.13 = (bf16[2,1,128,1024]{3,2,1,0:T(8,128)(2,1)S(1)}, bf16[2,1,128,1024]{3,2,1,0:T(8,128)(2,1)}, u32[]{:S(2)}) copy-start(bf16[2,1,128,1024]{3,2,1,0:T(8,128)(2,1)} %param.15) | copy-start | bytes 1572868
  227.4 88.1 %copy-start.18 = (bf16[256,1024]{1,0:T(8,128)(2,1)S(1)}, bf16[256,1024]{1,0:T(8,128)(2,1)}, u32[]{:S(2)}) copy-start(bf16[256,1024]{1,0:T(8,128)(2,1)} %get-tuple-element.26) | copy-start | bytes 1572868
  (3 other events, 2.6 us)

commit v3 on v2

v3 whole, which is shorter than its diff:
```python
import functools
import jax, jax.numpy as jnp
from jax import lax
from jax.experimental import pallas as pl
from jax.experimental.pallas import tpu as pltpu
from jax.sharding import PartitionSpec as P

MESH = pl.DeviceIdType.MESH
RING = 4
D = 1024
H = 8
HD = 128
FF = 2816
ROWS = 256
N_SEQ = 16
EPSILON = 1e-06
LOW = jnp.bfloat16
F32 = jnp.float32
OWNERS = (4, 2, 4, 2, 2)
DMA = pltpu.SemaphoreType.DMA
ORDERS = (("x", "y", "z"), ("y", "z", "x"), ("z", "x", "y"))
SPLIT_ROWS = (False, False, False, True)


def tiles(array, bounds, grain=128):
    return [(array, s, lo * grain, hi * grain) for s, (lo, hi) in enumerate(zip(bounds[:-1], bounds[1:]))]


CHUNKS = (
    tuple(tiles(0, (0, 11, 22, 32)) + tiles(1, (0, 2, 5, 8))),
    tuple(tiles(2, (0, 15, 30, 44))),
    tuple(tiles(3, (0, 7, 14, 22), 8)),
)
UNITS = CHUNKS[0] + CHUNKS[1] + CHUNKS[2]
C1, C2, C3 = (tuple(UNITS.index(u) for u in chunk) for chunk in CHUNKS)


def where_am_i():
    dp = lax.axis_index("dp")
    seq = lax.axis_index("seq")
    return {"x": (seq // 2 % 2) * 2 + dp % 2, "y": dp // 2, "z": seq // 4, "c": seq % 2}


def device(at):
    return (at["y"] * 2 + at["x"] % 2, at["z"] * 4 + (at["x"] // 2) * 2 + at["c"])


def moved(at, axis, by):
    out = dict(at)
    out[axis] = (at[axis] + by) % RING if axis != "c" else 1 - at[axis]
    return out


def block(ref, at, whole, lo, hi, rows):
    every = slice(None)
    pick = lambda axis, value: every if axis in whole else value
    span = pl.ds(lo, hi - lo)
    return ref.at[
        pick("y", at["y"]), pick("x", at["x"] % 2), pick("z", at["z"]), pick("x", at["x"] // 2), at["c"],
        span if rows else every, every if rows else span,
    ]


def middle(lo, hi, rows):
    grain = 8 if rows else 128
    return lo + ((hi - lo) // grain // 2) * grain


def neighbours(me):
    return [moved(me, a, d) for a in "xyz" for d in (1, -1)] + [moved(me, "c", 1)]


def dot(a, b, dims=((1,), (0,))):
    return lax.dot_general(a, b, (dims, ((), ())), preferred_element_type=F32)


def by_rows(count, size, body):
    def one(k, _):
        body(pl.ds(pl.multiple_of(k * size, size), size))
        return 0
    lax.fori_loop(0, count // size, one, 0)


def columns_of(k, size):
    return pl.ds(pl.multiple_of(k * size, size), size)


def sigmoid(u):
    return 1.0 / (1.0 + jnp.exp(-u))


def rms_factor(v):
    return lax.rsqrt(jnp.mean(v * v, axis=-1, keepdims=True) + EPSILON)


class Gather:
    def __init__(self, arrays, me, send_sem, recv_sem, csend_sem, crecv_sem):
        self.arrays, self.me = arrays, me
        self.send_sem, self.recv_sem, self.csend_sem, self.crecv_sem = send_sem, recv_sem, csend_sem, crecv_sem
        self.sends = []

    def copy(self, ref, u, slot, to):
        return pltpu.make_async_remote_copy(src_ref=ref, dst_ref=ref, send_sem=self.send_sem.at[u, slot],
            recv_sem=self.recv_sem.at[u, slot], device_id=device(to), device_id_type=MESH)

    def ccopy(self, ref, u, slot):
        return pltpu.make_async_remote_copy(src_ref=ref, dst_ref=ref, send_sem=self.csend_sem.at[u, slot],
            recv_sem=self.crecv_sem.at[u, slot], device_id=device(moved(self.me, "c", 1)), device_id_type=MESH)

    def go(self, cp):
        cp.start()
        self.sends.append(cp)

    def part(self, u, at, stage, half=None):
        i, s, lo, hi = UNITS[u]
        rows = SPLIT_ROWS[i]
        mid = middle(lo, hi, rows)
        lo, hi = (lo, hi) if half is None else ((lo, mid), (mid, hi))[half]
        return block(self.arrays[i], at, ORDERS[s][:stage], lo, hi, rows)

    def axis(self, u, stage):
        return ORDERS[UNITS[u][1]][stage]

    def begin(self, units, stage):
        for u in units:
            a = self.axis(u, stage)
            mine = self.part(u, self.me, stage)
            self.go(self.copy(mine, u, 4 * stage, moved(self.me, a, 1)))
            self.go(self.copy(mine, u, 4 * stage + 1, moved(self.me, a, -1)))
            if stage == 2:
                self.go(self.ccopy(mine, u, 0))

    def relay(self, units, stage):
        for u in units:
            a = self.axis(u, stage)
            above, below = moved(self.me, a, 1), moved(self.me, a, -1)
            self.copy(self.part(u, below, stage), u, 4 * stage, below).wait_recv()
            self.go(self.copy(self.part(u, below, stage, 0), u, 4 * stage + 2, above))
            self.copy(self.part(u, above, stage), u, 4 * stage + 1, above).wait_recv()
            self.go(self.copy(self.part(u, above, stage, 1), u, 4 * stage + 3, below))
            if stage == 2:
                self.go(self.ccopy(self.part(u, below, stage), u, 1))
                self.go(self.ccopy(self.part(u, above, stage), u, 2))

    def finish(self, units, stage):
        for u in units:
            a = self.axis(u, stage)
            far = moved(self.me, a, 2)
            for half in range(2):
                self.copy(self.part(u, far, stage, half), u, 4 * stage + 2 + half, moved(self.me, a, 1)).wait_recv()
            if stage == 2:
                self.go(self.ccopy(self.part(u, far, stage), u, 3))

    def arrive(self, units):
        sib = moved(self.me, "c", 1)
        for u in units:
            for k, by in enumerate((0, -1, 1, 2)):
                self.ccopy(self.part(u, moved(sib, self.axis(u, 2), by), 2), u, k).wait_recv()

    def drain(self):
        for cp in self.sends:
            cp.wait_send()


class Scan:
    def __init__(self, local, came, going, carried, sems):
        self.me, self.dp = lax.axis_index("seq"), lax.axis_index("dp")
        self.local, self.came, self.going, self.carried = local, came, going, carried
        self.send1, self.recv1, self.send2, self.recv2 = sems

    def to(self, k):
        return (self.me + k) % N_SEQ

    def out(self, to):
        return pltpu.make_async_remote_copy(src_ref=self.local.at[to], dst_ref=self.came.at[self.me], send_sem=self.send1.at[to],
            recv_sem=self.recv1.at[self.me], device_id=(self.dp, to), device_id_type=MESH)

    def back(self, to):
        return pltpu.make_async_remote_copy(src_ref=self.going.at[to], dst_ref=self.carried.at[self.me], send_sem=self.send2.at[to],
            recv_sem=self.recv2.at[self.me], device_id=(self.dp, to), device_id_type=MESH)

    def arrival(self, ref, ssem, rsem, frm):
        return pltpu.make_async_remote_copy(src_ref=ref.at[frm], dst_ref=ref.at[frm], send_sem=ssem.at[frm],
            recv_sem=rsem.at[frm], device_id=(self.dp, self.to(1)), device_id_type=MESH)

    def each(self, body):
        def one(k, _):
            body(self.to(k))
            return 0
        lax.fori_loop(1, N_SEQ, one, 0)

    def start(self):
        self.each(lambda to: self.out(to).start())
        self.came[self.me] = self.local[self.me]

    def join(self, tags_all, decays, backward):
        self.each(lambda frm: self.arrival(self.came, self.send1, self.recv1, frm).wait_recv())
        micro, head = self.me // H, self.me % H
        fade = jnp.exp(-float(HD) * jnp.full((1, HD), decays[head], F32))
        first = lambda b: tags_all[b, pl.ds(2 * micro, 1), :]
        last = lambda b: tags_all[b, pl.ds(2 * micro + 1, 1), :]
        acc = jnp.zeros((HD, HD), F32)
        previous = None
        for b in (range(N_SEQ - 1, -1, -1) if backward else range(N_SEQ)):
            self.going[b] = acc.astype(LOW)
            if previous is None:
                acc = self.came[b].astype(F32)
            else:
                near = (last(b) == first(previous)) if backward else (first(b) == last(previous))
                acc = self.came[b].astype(F32) + jnp.where((first(b) == last(b)) & near, fade, 0.0) * acc
            previous = b
        self.carried[self.me] = self.going[self.me]
        self.each(lambda to: self.back(to).start())

    def finish(self):
        self.each(lambda frm: self.arrival(self.carried, self.send2, self.recv2, frm).wait_recv())

    def drain(self):
        def one(to):
            self.out(to).wait_send()
            self.back(to).wait_send()
        self.each(one)


def spread(row):
    across = jnp.broadcast_to(row, (HD, HD))
    return across.T, across


def row_index():
    return lax.broadcasted_iota(jnp.int32, (HD, HD), 0).astype(F32)


def column_index():
    return lax.broadcasted_iota(jnp.int32, (HD, HD), 1).astype(F32)


def pair_at(p):
    micro, head = p // H, p % H
    return micro, head, pl.ds(pl.multiple_of(micro * HD, HD), HD), pl.ds(pl.multiple_of(head * HD, HD), HD)


def transpose_into(src, dst, count):
    def one(k, _):
        at = columns_of(k, 128)
        dst[at, :] = src[:, at].T
        return 0
    lax.fori_loop(0, count // 128, one, 0)


def forward_kernel(*refs):
    (x, cot, ids, decays), small = refs[:4], refs[4:12]
    (act, tags_all, o_qkv, o_slopes, o_gate, o_mixed, o_resid, o_up, o_carried, o_in, o_output, o_wide, o_down,
     t_first, t_gated, t_second, t_product, b_branch) = refs[12:30]
    (w_in, w_output, w_up, w_flat, w_down, pre, first_in, qkv, slopes, gate, mixed, resid, up, gated, second, product,
     first_t, gated_t, second_t, product_t, carried, local, came, going, spare, tag, allowed, kept_mask, ids_down,
     send_sem, recv_sem, csend_sem, crecv_sem, tag_send, tag_recv, s1, r1, s2, r2, out_sem, pass_send, pass_recv) = refs[30:]
    me = where_am_i()
    sib = moved(me, "c", 1)
    seq, dp = lax.axis_index("seq"), lax.axis_index("dp")
    to = lambda k: (seq + k) % N_SEQ
    barrier = pltpu.get_barrier_semaphore()
    close = neighbours(me)
    for other in close:
        pl.semaphore_signal(barrier, inc=1, device_id=device(other), device_id_type=MESH)

    def greet(k, _):
        pl.semaphore_signal(barrier, inc=1, device_id=(dp, to(k)), device_id_type=MESH)
        return 0
    lax.fori_loop(1, N_SEQ, greet, 0)

    here = (me["y"], me["x"] % 2, me["z"], me["x"] // 2, me["c"])
    def place(src, target, base, width):
        n = width // 128
        spare[pl.ds(0, 8 * n), :] = src[...].astype(F32)
        for c in range(n):
            target[(*here, slice(None), pl.ds(base + c * 128, 128))] = spare[pl.ds(c, 8, stride=n), :].astype(LOW)
    for k in range(4):
        place(small[k], w_in, k * D, D)
    place(small[4], w_output, 0, D)
    place(small[5], w_up, 0, FF)
    place(small[6], w_up, FF, FF)
    w_flat[here] = small[7][...]
    tag[...] = jnp.zeros((8, HD), F32)
    for m in range(2):
        tag[2 * m:2 * m + 1, :] = jnp.broadcast_to(ids[m:m + 1, 0:1], (1, HD))
        tag[2 * m + 1:2 * m + 2, :] = jnp.broadcast_to(ids[m:m + 1, HD - 1:HD], (1, HD))
    tags_all[seq] = tag[...]
    pl.semaphore_wait(barrier, len(close) + N_SEQ - 1)

    g = Gather((w_in, w_output, w_up, w_flat), me, send_sem, recv_sem, csend_sem, crecv_sem)
    scan = Scan(local, came, going, carried, (s1, r1, s2, r2))
    g.begin(C1, 0)
    g.begin(C2, 0)
    g.begin(C3, 0)

    kept, passed = [], []
    def keep(src, dst):
        cp = pltpu.make_async_copy(src, dst, out_sem.at[len(kept)])
        cp.start()
        kept.append(cp)
    def hand(mine, theirs, dst):
        keep(mine, dst.at[me["c"]])
        k = len(passed)
        cp = pltpu.make_async_remote_copy(src_ref=theirs, dst_ref=dst.at[me["c"]], send_sem=pass_send.at[k],
            recv_sem=pass_recv.at[k], device_id=device(sib), device_id_type=MESH)
        cp.start()
        passed.append((cp, dst))

    def tag_copy(other):
        return pltpu.make_async_remote_copy(src_ref=tag, dst_ref=tags_all.at[seq], send_sem=tag_send.at[other],
            recv_sem=tag_recv.at[seq], device_id=(dp, other), device_id_type=MESH)
    scan.each(lambda other: tag_copy(other).start())

    def norm_in(rows):
        v = x[rows, :].astype(F32)
        first_in[rows, :] = (v * rms_factor(v)).astype(LOW)
    by_rows(ROWS, 32, norm_in)
    g.relay(C1, 0)
    g.relay(C2, 0)
    g.relay(C3, 0)
    for m in range(2):
        down, across = spread(ids[m:m + 1, :])
        ids_down[m] = down
        allowed[m] = jnp.where((down == across) & (row_index() >= column_index()), 1.0, 0.0)
        kept_mask[m] = jnp.where(down == jnp.broadcast_to(ids[m:m + 1, HD - 1:HD], (HD, HD)), 1.0, 0.0)
    half = lambda c: cot.at[:, pl.ds(pl.multiple_of(c * 512, 512), 512)]
    hand(half(me["c"]), half(sib["c"]), b_branch)
    g.finish(C1, 0)
    g.begin(C1, 1)
    g.finish(C2, 0)
    g.begin(C2, 1)
    g.finish(C3, 0)
    g.begin(C3, 1)
    g.relay(C1, 1)
    g.relay(C2, 1)
    g.relay(C3, 1)
    g.finish(C1, 1)
    g.begin(C1, 2)
    g.finish(C2, 1)
    g.finish(C3, 1)
    transpose_into(first_in, first_t, D)
    hand(first_t, first_t, t_first)
    g.relay(C1, 2)
    g.begin(C2, 2)
    g.finish(C1, 2)
    g.arrive(C1)
    keep(w_in, o_in)
    keep(w_output, o_output)

    m_in = w_in.reshape(D, 4 * D)
    def project(k, _):
        cols = columns_of(k, 512)
        pre[:, cols] = dot(first_in[...], m_in[:, cols])
        return 0
    lax.fori_loop(0, 8, project, 0)
    g.relay(C2, 2)
    g.begin(C3, 2)

    def rows_of_heads(rows):
        for k in range(2):
            u = pre[rows, k * D:(k + 1) * D]
            s = sigmoid(u)
            qkv[rows, k * D:(k + 1) * D] = (u * s).astype(LOW)
            slopes[rows, k * D:(k + 1) * D] = (s * (1.0 + u * (1.0 - s))).astype(LOW)
        qkv[rows, 2 * D:3 * D] = pre[rows, 2 * D:3 * D].astype(LOW)
        gate[rows, :] = pre[rows, 3 * D:4 * D].astype(LOW)
    by_rows(ROWS, 16, rows_of_heads)
    keep(qkv, o_qkv)
    keep(slopes, o_slopes)
    keep(gate, o_gate)

    def states(p, _):
        micro, head, rows, _ = pair_at(p)
        keeping = jnp.exp((row_index() - (HD - 1.0)) * decays[head]) * kept_mask[micro]
        held = (qkv[rows, head_of(head, 1)].astype(F32) * keeping).astype(LOW)
        local[p] = dot(held, qkv[rows, head_of(head, 2)], ((0,), (0,))).astype(LOW)
        return 0
    lax.fori_loop(0, 2 * H, states, 0)
    scan.start()
    g.finish(C2, 2)

    def within(p, _):
        micro, head, rows, cols = pair_at(p)
        mask = allowed[micro] * jnp.exp(jnp.minimum(column_index() - row_index(), 0.0) * decays[head])
        weighted = (dot(qkv[rows, head_of(head, 0)], qkv[rows, head_of(head, 1)], ((1,), (1,))) * mask).astype(LOW)
        mixed[rows, cols] = dot(weighted, qkv[rows, head_of(head, 2)])
        return 0
    lax.fori_loop(0, 2 * H, within, 0)
    scan.each(lambda frm: pltpu.make_async_remote_copy(src_ref=tag, dst_ref=tags_all.at[frm], send_sem=tag_send.at[frm],
        recv_sem=tag_recv.at[frm], device_id=(dp, to(1)), device_id_type=MESH).wait_recv())
    scan.join(tags_all, decays, False)
    g.relay(C3, 2)
    scan.finish()
    keep(carried, o_carried)

    def crossing(p, _):
        micro, head, rows, cols = pair_at(p)
        boundary = jnp.where(seq > 0, tags_all[jnp.maximum(seq - 1, 0), pl.ds(2 * micro + 1, 1), :], -1.0)
        reaching = jnp.where(ids_down[micro] == boundary, jnp.exp(-(row_index() + 1.0) * decays[head]), 0.0)
        mixed[rows, cols] += dot(qkv[rows, head_of(head, 0)], carried[p]) * reaching
        return 0
    lax.fori_loop(0, 2 * H, crossing, 0)
    keep(mixed, o_mixed)

    def gate_rows(rows):
        v = mixed[rows, :]
        gated[rows, :] = (v * rms_factor(v) * pre[rows, 3 * D:4 * D]).astype(LOW)
    by_rows(ROWS, 16, gate_rows)
    m_output = w_output.reshape(D, D)
    def output(k, _):
        cols = columns_of(k, 512)
        resid[:, cols] = x[:, cols].astype(F32) + dot(gated[...], m_output[:, cols])
        return 0
    lax.fori_loop(0, 2, output, 0)
    keep(resid, o_resid)
    def norm_second(rows):
        v = resid[rows, :]
        second[rows, :] = (v * rms_factor(v)).astype(LOW)
    by_rows(ROWS, 32, norm_second)
    g.finish(C3, 2)
    g.arrive(C2)
    keep(w_up, o_wide)
    m_up = w_up.reshape(D, 2 * FF)
    def widen(k, _):
        cols, more = columns_of(k, 256), pl.ds(pl.multiple_of(k * 256 + FF, 256), 256)
        left = dot(second[...], m_up[:, cols])
        right = dot(second[...], m_up[:, more])
        up[:, cols] = left.astype(LOW)
        up[:, more] = right.astype(LOW)
        product[:, cols] = (left * right).astype(LOW)
        return 0
    lax.fori_loop(0, 11, widen, 0)
    keep(up, o_up)
    transpose_into(product, product_t, FF)
    hand(product_t, product_t, t_product)
    transpose_into(gated, gated_t, D)
    hand(gated_t, gated_t, t_gated)
    transpose_into(second, second_t, D)
    hand(second_t, second_t, t_second)
    g.arrive(C3)
    flat = w_flat.reshape(128 * 176, 128)
    def arrange(k, _):
        spare[...] = flat[pl.ds(pl.multiple_of(k * 1408, 1408), 1408), :].astype(F32)
        for c in range(8):
            w_down[pl.ds(pl.multiple_of(k * 176, 176), 176), c * 128:(c + 1) * 128] = spare[pl.ds(c, 176, stride=8), :].astype(LOW)
        return 0
    lax.fori_loop(0, 16, arrange, 0)
    keep(w_down, o_down)
    def last(k, _):
        cols = columns_of(k, 512)
        act[:, cols] = (resid[:, cols] + dot(product[...], w_down[:, cols])).astype(LOW)
        return 0
    lax.fori_loop(0, 2, last, 0)
    for cp in kept:
        cp.wait()
    for k, (cp, dst) in enumerate(passed):
        cp.wait_send()
        there = dst.at[sib["c"]]
        pltpu.make_async_remote_copy(src_ref=there, dst_ref=there, send_sem=pass_send.at[k], recv_sem=pass_recv.at[k],
            device_id=device(sib), device_id_type=MESH).wait_recv()
    scan.each(lambda other: tag_copy(other).wait_send())
    scan.drain()
    g.drain()


def forward(x, cot, ids, decays, pieces):
    v = pl.BlockSpec(memory_space=pltpu.VMEM)
    anywhere = pl.BlockSpec(memory_space=pl.ANY)
    sds = jax.ShapeDtypeStruct
    n = len(UNITS)
    outs = [sds((ROWS, D), LOW), sds((N_SEQ, 8, HD), F32), sds((ROWS, 3 * D), LOW), sds((ROWS, 2 * D), LOW), sds((ROWS, D), LOW),
        sds((ROWS, D), F32), sds((ROWS, D), F32), sds((ROWS, 2 * FF), LOW), sds((N_SEQ, HD, HD), LOW),
        sds(OWNERS + (8, 4 * D), LOW), sds(OWNERS + (8, D), LOW), sds(OWNERS + (8, 2 * FF), LOW), sds((FF, D), LOW),
        sds((2, D, ROWS), LOW), sds((2, D, ROWS), LOW), sds((2, D, ROWS), LOW), sds((2, FF, ROWS), LOW), sds((2, ROWS, D // 2), LOW)]
    vm = pltpu.VMEM
    scratch = [vm(OWNERS + (8, 4 * D), LOW), vm(OWNERS + (8, D), LOW), vm(OWNERS + (8, 2 * FF), LOW), vm(OWNERS + (176, 128), LOW),
        vm((FF, D), LOW), vm((ROWS, 4 * D), F32), vm((ROWS, D), LOW), vm((ROWS, 3 * D), LOW), vm((ROWS, 2 * D), LOW), vm((ROWS, D), LOW),
        vm((ROWS, D), F32), vm((ROWS, D), F32), vm((ROWS, 2 * FF), LOW), vm((ROWS, D), LOW), vm((ROWS, D), LOW), vm((ROWS, FF), LOW),
        vm((D, ROWS), LOW), vm((D, ROWS), LOW), vm((D, ROWS), LOW), vm((FF, ROWS), LOW)] + [vm((N_SEQ, HD, HD), LOW)] * 4 + [
        vm((1408, 128), F32), vm((8, HD), F32)] + [vm((2, HD, HD), F32)] * 3 + [
        DMA((n, 12)), DMA((n, 12)), DMA((n, 4)), DMA((n, 4))] + [DMA((N_SEQ,))] * 6 + [DMA((20,)), DMA((5,)), DMA((5,))]
    return pl.pallas_call(
        forward_kernel, out_shape=outs,
        in_specs=[v, v, v, pl.BlockSpec(memory_space=pltpu.SMEM)] + [v] * 8,
        out_specs=[v] * 2 + [anywhere] * 16,
        scratch_shapes=scratch,
        compiler_params=pltpu.CompilerParams(collective_id=0, has_side_effects=True, vmem_limit_bytes=60 << 20),
        name="gather_and_forward",
    )(x, cot, ids, decays, *pieces)


def head_of(head, part):
    return pl.ds(pl.multiple_of(part * D + head * HD, HD), HD)


DOWN, WIDE, OUTPUT, INPUT = range(4)
HELD = ((88, 256), (16, FF), (16, D // 2), (16, 2 * D))
BACK_UNITS = tuple(tiles(DOWN, (0, 3, 7, 11), 8) + tiles(WIDE, (0, 7, 14, 22)) + tiles(OUTPUT, (0, 2, 4)) + tiles(INPUT, (0, 5, 10, 16)))
BACK_OF = [tuple(u for u, unit in enumerate(BACK_UNITS) if unit[0] == i) for i in range(4)]
BACK_ORDERS = tuple(order[::-1] for order in ORDERS)
DIMS = (("y", 4), ("x", 2), ("z", 4), ("x", 2))


def live_dims(fixed):
    return tuple(n for a, n in DIMS if a not in fixed)


def part_of(ref, at, fixed, gone, lo, hi, rows, lead=()):
    every = slice(None)
    idx = []
    for k, (a, n) in enumerate(DIMS):
        if a in gone:
            continue
        if a in fixed:
            idx.append((at["x"] % 2 if k == 1 else at["x"] // 2) if a == "x" else at[a])
        else:
            idx.append(every)
    span = pl.ds(lo, hi - lo)
    return ref.at[(*lead, *idx, span if rows else every, every if rows else span)]


def accumulate(dst, srcs, dims, out=None):
    target = dst if out is None else out
    def one(k, _):
        idx, rest = [], k
        for d in dims[::-1]:
            idx.append(rest % d)
            rest = rest // d
        at = tuple(idx[::-1]) if dims else ...
        total = dst[at].astype(F32)
        for s in srcs:
            total = total + s[at].astype(F32)
        target[at] = total.astype(target.dtype)
        return 0
    n = 1
    for d in dims:
        n *= d
    if n == 1:
        one(0, 0)
    else:
        lax.fori_loop(0, n, one, 0)


class Scatter:
    def __init__(self, held, slots, final, me, send_sem, recv_sem):
        self.held, self.slots, self.final, self.me = held, slots, final, me
        self.send_sem, self.recv_sem = send_sem, recv_sem
        self.sends = []

    def spans(self, u):
        i, s, lo, hi = BACK_UNITS[u]
        return self.held[i], BACK_ORDERS[s], i == DOWN, lo, middle(lo, hi, i == DOWN), hi

    def slot(self, u, stage, k, lo, hi):
        _, order, rows, base, _, _ = self.spans(u)
        return part_of(self.slots[stage][u], self.me, (), order[:stage + 1], lo - base, hi - base, rows, (k,))

    def send(self, src, dst, u, stage, k, to):
        cp = pltpu.make_async_remote_copy(src_ref=src, dst_ref=dst, send_sem=self.send_sem.at[u, stage, k],
            recv_sem=self.recv_sem.at[u, stage, k], device_id=device(to), device_id_type=MESH)
        cp.start()
        self.sends.append(cp)

    def got(self, ref, u, stage, k):
        pltpu.make_async_remote_copy(src_ref=ref, dst_ref=ref, send_sem=self.send_sem.at[u, stage, k],
            recv_sem=self.recv_sem.at[u, stage, k], device_id=device(moved(self.me, "c", 1)), device_id_type=MESH).wait_recv()

    def far(self, units, stage):
        for u in units:
            held, order, rows, lo, mid, hi = self.spans(u)
            at = moved(self.me, order[stage], 2)
            fixed = order[:stage + 1]
            self.send(part_of(held, at, fixed, (), lo, mid, rows), self.slot(u, stage, 0, lo, mid), u, stage, 0, moved(self.me, order[stage], 1))
            self.send(part_of(held, at, fixed, (), mid, hi, rows), self.slot(u, stage, 0, mid, hi), u, stage, 1, moved(self.me, order[stage], -1))

    def turn(self, units, stage):
        for u in units:
            held, order, rows, lo, mid, hi = self.spans(u)
            fixed = order[:stage + 1]
            for k, (by, a, b) in enumerate(((1, lo, mid), (-1, mid, hi))):
                to = moved(self.me, order[stage], by)
                came = self.slot(u, stage, 0, a, b)
                self.got(came, u, stage, k)
                accumulate(part_of(held, to, fixed, (), a, b, rows), [came], live_dims(fixed))
                self.send(part_of(held, to, fixed, (), lo, hi, rows), self.slot(u, stage, 1 + k, lo, hi), u, stage, 2 + k, to)

    def land(self, units, stage):
        for u in units:
            held, order, rows, lo, mid, hi = self.spans(u)
            fixed = order[:stage + 1]
            came = [self.slot(u, stage, 1 + k, lo, hi) for k in range(2)]
            for k in range(2):
                self.got(came[k], u, stage, 2 + k)
            mine = part_of(held, self.me, fixed, (), lo, hi, rows)
            if stage < 2:
                accumulate(mine, came, live_dims(fixed))
            else:
                span = pl.ds(lo, hi - lo)
                accumulate(mine, came, (), self.final[BACK_UNITS[u][0]].at[(span, slice(None)) if rows else (slice(None), span)])
        if stage < 2:
            self.far(units, stage + 1)

    def drain(self):
        for cp in self.sends:
            cp.wait_send()


def norm_back(upstream, normed, factor):
    return factor * (upstream - normed * jnp.mean(upstream * normed, axis=-1, keepdims=True))


def backward_kernel(*refs):
    (ids, tags_all, decays, h_x, h_cot, h_qkv, h_slopes, h_gate, h_mixed, h_resid, h_up, h_carried, w_in, w_output, w_up, w_down,
     t_first, t_gated, t_second, t_product, b_branch) = refs[:21]
    input_grad, grads = refs[21], refs[22:30]
    refs = refs[30:]
    n = len(BACK_UNITS)
    held, refs = refs[:4], refs[4:]
    slots = [refs[k * n:(k + 1) * n] for k in range(3)]
    refs = refs[3 * n:]
    final, theirs, refs = refs[:4], refs[4:7], refs[7:]
    (quarters, regroup, wbuf, product_t, lhs_a, lhs_b, branch, cot, d_up, up_sib, d_attn, attn_sib, pre_sib,
     up, qkv, slopes, gate, mixed, resid, x, d_resid, work, d_mixed, carried, local, came, going, reverse, ids_down, allowed,
     load_sem, wsem, send_sem, recv_sem, s1, r1, s2, r2, pass_send, pass_recv, end_send, end_recv, q_send, q_recv) = refs
    me = where_am_i()
    sib = moved(me, "c", 1)
    core, other_core = me["c"], sib["c"]
    seq, dp = lax.axis_index("seq"), lax.axis_index("dp")
    to = lambda k: (seq + k) % N_SEQ
    barrier = pltpu.get_barrier_semaphore()
    close = neighbours(me)
    for other in close:
        pl.semaphore_signal(barrier, inc=1, device_id=device(other), device_id_type=MESH)

    def greet(k, _):
        pl.semaphore_signal(barrier, inc=1, device_id=(dp, to(k)), device_id_type=MESH)
        return 0
    lax.fori_loop(1, N_SEQ, greet, 0)

    loads = {}
    def load(name, src, dst):
        cp = pltpu.make_async_copy(src, dst, load_sem.at[len(loads)])
        cp.start()
        loads[name] = cp
    load("product", t_product, product_t)
    load("branch", b_branch, branch)
    load("cot", h_cot, cot)

    phases = ((w_down, 11, 0, D), (w_up, 4, 0, FF), (w_up, 4, FF, FF), (w_output, 4, 0, D), (w_in, 4, 0, 2 * D), (w_in, 4, 2 * D, 2 * D))
    first = [sum(p[1] for p in phases[:k]) for k in range(len(phases))]
    def piece(phase, k):
        w, _, col, width = phases[phase]
        slot = (first[phase] + k) % 2
        row = pl.multiple_of(k * 256, 256)
        return pltpu.make_async_copy(w.at[pl.ds(row, 256), pl.ds(col, width)], wbuf.at[slot, :, pl.ds(0, width)], wsem.at[slot])
    def stream(phase, compute):
        count, width = phases[phase][1], phases[phase][3]
        def one(k, _):
            piece(phase, k).wait()
            @pl.when(k + 1 < count)
            def _():
                piece(phase, k + 1).start()
            if phase + 1 < len(phases):
                @pl.when(k + 1 == count)
                def _():
                    piece(phase + 1, 0).start()
            compute(k, wbuf.at[(first[phase] + k) % 2, :, pl.ds(0, width)])
            return 0
        lax.fori_loop(0, count, one, 0)
    piece(0, 0).start()
    load("up", h_up, up)
    load("second", t_second, lhs_a)
    load("resid", h_resid, resid)
    load("gated", t_gated, lhs_b)
    load("mixed", h_mixed, mixed)
    load("gate", h_gate, gate)
    load("qkv", h_qkv, qkv)
    load("slopes", h_slopes, slopes)
    load("carried", h_carried, carried)
    load("x", h_x, x)
    pl.semaphore_wait(barrier, len(close) + N_SEQ - 1)

    rs = Scatter(held, slots, final, me, send_sem, recv_sem)
    scan = Scan(local, came, going, reverse, (s1, r1, s2, r2))
    passed = []
    def hand(src, dst):
        k = len(passed)
        cp = pltpu.make_async_remote_copy(src_ref=src, dst_ref=dst, send_sem=pass_send.at[k], recv_sem=pass_recv.at[k],
            device_id=device(sib), device_id_type=MESH)
        cp.start()
        passed.append(cp)
        return cp

    loads["product"].wait()
    loads["branch"].wait()
    def down_rows(k, _):
        rows = pl.ds(pl.multiple_of(k * 352, 32), 352)
        for j in range(2):
            cols = slice(j * 256, (j + 1) * 256)
            total = dot(product_t[0, rows, :], branch[0, :, cols]) + dot(product_t[1, rows, :], branch[1, :, cols])
            for i in range(4):
                held[DOWN][k // 2, k % 2, i, j] = total[i * 88:(i + 1) * 88].astype(LOW)
        return 0
    lax.fori_loop(0, 8, down_rows, 0)
    rs.far(BACK_OF[DOWN], 0)

    loads["cot"].wait()
    loads["up"].wait()
    def up_back(k, w):
        cols, more = columns_of(k, 256), pl.ds(pl.multiple_of(k * 256 + FF, 256), 256)
        d_product = dot(cot[...], w[...], ((1,), (1,)))
        d_up[:, cols] = (d_product * up[:, more].astype(F32)).astype(LOW)
        d_up[:, more] = (d_product * up[:, cols].astype(F32)).astype(LOW)
    stream(0, up_back)
    side = lambda c, width: pl.ds(pl.multiple_of(c * width, width), width)
    hand(d_up.at[:, side(other_core, FF)], up_sib)
    rs.turn(BACK_OF[DOWN], 0)
    def second_left(k, w):
        work[:, columns_of(k, 256)] = dot(d_up[:, 0:FF], w[...], ((1,), (1,)))
    stream(1, second_left)
    def second_right(k, w):
        work[:, columns_of(k, 256)] += dot(d_up[:, FF:2 * FF], w[...], ((1,), (1,)))
    stream(2, second_right)
    rs.land(BACK_OF[DOWN], 0)

    loads["resid"].wait()
    def resid_back(rows):
        v = resid[rows, :]
        factor = rms_factor(v)
        total = cot[rows, :].astype(F32) + norm_back(work[rows, :], v * factor, factor)
        d_resid[rows, :] = total
        d_attn[rows, :] = total.astype(LOW)
    by_rows(ROWS, 16, resid_back)
    hand(d_attn.at[:, side(other_core, D // 2)], attn_sib)
    rs.turn(BACK_OF[DOWN], 1)
    def gated_back(k, w):
        work[:, columns_of(k, 256)] = dot(d_attn[...], w[...], ((1,), (1,)))
    stream(3, gated_back)
    loads["mixed"].wait()
    loads["gate"].wait()
    d_gate = resid
    def mixed_back(rows):
        v = mixed[rows, :]
        factor = rms_factor(v)
        normed = v * factor
        g = work[rows, :]
        d_gate[rows, :] = g * normed
        d_mixed[rows, :] = norm_back(g * gate[rows, :].astype(F32), normed, factor).astype(LOW)
    by_rows(ROWS, 16, mixed_back)
    loads["qkv"].wait()
    for m in range(2):
        below, across = spread(ids[m:m + 1, :])
        ids_down[m] = below
        allowed[m] = jnp.where((below == across) & (row_index() >= column_index()), 1.0, 0.0)
    def back_states(p, _):
        micro, head, rows, cols = pair_at(p)
        start = ids[pl.ds(micro, 1), 0:1]
        opening = jnp.where(ids_down[micro] == start, jnp.exp(-(row_index() + 1.0) * decays[head]), 0.0)
        opened = (qkv[rows, head_of(head, 0)].astype(F32) * opening).astype(LOW)
        local[p] = dot(opened, d_mixed[rows, cols], ((0,), (0,))).astype(LOW)
        return 0
    lax.fori_loop(0, 2 * H, back_states, 0)
    scan.start()
    rs.land(BACK_OF[DOWN], 1)
    rs.turn(BACK_OF[DOWN], 2)

    def grad_half(i, lhs, own, base, sibling, units):
        out = held[i].reshape(D, HELD[i][1])
        for u in units:
            _, _, lo, hi = BACK_UNITS[u]
            a = lo
            while a < hi:
                wide = min(256, hi - a)
                mine = own[:, pl.ds(pl.multiple_of(base + a, 128), wide)]
                total = dot(lhs[core], mine) + dot(lhs[other_core], sibling[:, a:a + wide])
                out[:, a:a + wide] = total.astype(LOW)
                a += wide
            rs.far((u,), 0)

    loads["second"].wait()
    passed[0].wait_recv()
    grad_half(WIDE, lhs_a, d_up, core * FF, up_sib, BACK_OF[WIDE])
    load("first", t_first, lhs_a)
    rs.land(BACK_OF[DOWN], 2)
    loads["gated"].wait()
    passed[1].wait_recv()
    grad_half(OUTPUT, lhs_b, d_attn, core * (D // 2), attn_sib, BACK_OF[OUTPUT])
    scan.join(tags_all, decays, True)
    rs.turn(BACK_OF[WIDE], 0)

    passed[0].wait_send()
    loads["slopes"].wait()
    loads["carried"].wait()
    d_pre = d_up.at[:, 0:4 * D]
    def pair_back(p, _):
        micro, head, rows, cols = pair_at(p)
        q, k, v = (qkv[rows, head_of(head, part)] for part in range(3))
        dm = d_mixed[rows, cols]
        mask = allowed[micro] * jnp.exp(jnp.minimum(column_index() - row_index(), 0.0) * decays[head])
        weighted = (dot(q, k, ((1,), (1,))) * mask).astype(LOW)
        d_scores = (dot(dm, v, ((1,), (1,))) * mask).astype(LOW)
        boundary = jnp.where(seq > 0, tags_all[jnp.maximum(seq - 1, 0), pl.ds(2 * micro + 1, 1), :], -1.0)
        reaching = jnp.where(ids_down[micro] == boundary, jnp.exp(-(row_index() + 1.0) * decays[head]), 0.0)
        d_q = dot(d_scores, k) + dot(dm, carried[p], ((1,), (1,))) * reaching
        d_pre[rows, head_of(head, 0)] = (d_q * slopes[rows, head_of(head, 0)].astype(F32)).astype(LOW)
        work[rows, cols] = dot(d_scores, q, ((0,), (0,)))
        mixed[rows, cols] = dot(weighted, dm, ((0,), (0,)))
        return 0
    lax.fori_loop(0, 2 * H, pair_back, 0)
    def gate_out(rows):
        d_pre[rows, 3 * D:4 * D] = d_gate[rows, :].astype(LOW)
    by_rows(ROWS, 16, gate_out)
    rs.land(BACK_OF[WIDE], 0)
    rs.turn(BACK_OF[OUTPUT], 0)
    scan.finish()
    def pair_close(p, _):
        micro, head, rows, cols = pair_at(p)
        after = jnp.where(seq < N_SEQ - 1, tags_all[jnp.minimum(seq + 1, N_SEQ - 1), pl.ds(2 * micro, 1), :], -1.0)
        closing = jnp.where(ids_down[micro] == after, jnp.exp((row_index() - (HD - 1.0)) * decays[head]), 0.0)
        d_k = work[rows, cols] + dot(qkv[rows, head_of(head, 2)], reverse[p], ((1,), (1,))) * closing
        d_v = mixed[rows, cols] + dot(qkv[rows, head_of(head, 1)], reverse[p]) * closing
        d_pre[rows, head_of(head, 1)] = (d_k * slopes[rows, head_of(head, 1)].astype(F32)).astype(LOW)
        d_pre[rows, head_of(head, 2)] = d_v.astype(LOW)
        return 0
    lax.fori_loop(0, 2 * H, pair_close, 0)
    hand(d_pre.at[:, side(other_core, 2 * D)], pre_sib)
    rs.turn(BACK_OF[WIDE], 1)
    rs.land(BACK_OF[OUTPUT], 0)
    loads["first"].wait()
    passed[2].wait_recv()
    grad_half(INPUT, lhs_a, d_pre, core * 2 * D, pre_sib, BACK_OF[INPUT])
    rs.land(BACK_OF[WIDE], 1)
    rs.turn(BACK_OF[OUTPUT], 1)
    def first_left(k, w):
        work[:, columns_of(k, 256)] = dot(d_pre[:, 0:2 * D], w[...], ((1,), (1,)))
    stream(4, first_left)
    rs.turn(BACK_OF[INPUT], 0)
    rs.turn(BACK_OF[WIDE], 2)
    rs.land(BACK_OF[OUTPUT], 1)
    def first_right(k, w):
        work[:, columns_of(k, 256)] += dot(d_pre[:, 2 * D:4 * D], w[...], ((1,), (1,)))
    stream(5, first_right)
    rs.land(BACK_OF[INPUT], 0)
    rs.land(BACK_OF[WIDE], 2)
    rs.turn(BACK_OF[OUTPUT], 2)
    loads["x"].wait()
    def input_back(rows):
        v = x[rows, :].astype(F32)
        factor = rms_factor(v)
        input_grad[rows, :] = d_resid[rows, :] + norm_back(work[rows, :], v * factor, factor)
    by_rows(ROWS, 16, input_back)
    rs.turn(BACK_OF[INPUT], 1)
    rs.land(BACK_OF[OUTPUT], 2)

    place = me["x"] // 2 * 2 + core
    def owner(j):
        return (dp, me["z"] * 4 + j)
    for j in range(4):
        quarters[j, 0:22, :] = final[DOWN][j * 22:(j + 1) * 22, :]
    def quarter(k):
        j = (place + k) % 4
        return pltpu.make_async_remote_copy(src_ref=quarters.at[j], dst_ref=regroup.at[place], send_sem=q_send.at[j],
            recv_sem=q_recv.at[place], device_id=owner(j), device_id_type=MESH)
    for k in range(1, 4):
        quarter(k).start()
    regroup[place] = quarters[place]
    ends = []
    def swap(i):
        k = len(ends)
        cp = pltpu.make_async_remote_copy(src_ref=final[i].at[side(other_core, 8), :], dst_ref=theirs[i - 1], send_sem=end_send.at[k],
            recv_sem=end_recv.at[k], device_id=device(sib), device_id_type=MESH)
        cp.start()
        ends.append(cp)
    def give(i, outs):
        ends[i - 1].wait_recv()
        mine, came = final[i][side(core, 8), :], theirs[i - 1][...]
        both = (jnp.where(core == 0, mine, came), jnp.where(core == 0, came, mine))
        width = HELD[i][1]
        n = len(outs) // 2
        for k, out in enumerate(outs):
            tiles_out = width // 128 if n == 0 else width // 128 // n
            for c in range(tiles_out):
                a = ((k % n) * tiles_out + c) * 128
                out[pl.ds(c, 8, stride=tiles_out), :] = both[k // n][:, a:a + 128]
    swap(WIDE)
    swap(OUTPUT)
    rs.land(BACK_OF[INPUT], 1)
    for k in range(1, 4):
        j = (place + k) % 4
        pltpu.make_async_remote_copy(src_ref=regroup.at[j], dst_ref=regroup.at[j], send_sem=q_send.at[j],
            recv_sem=q_recv.at[j], device_id=owner((place + 1) % 4), device_id_type=MESH).wait_recv()
    for j in range(4):
        for k in range(2):
            t = (j % 2) * 4 + (j // 2) * 2 + k
            grads[7][pl.ds(t, 22, stride=8), :] = regroup[j, 0:22, k * 128:(k + 1) * 128]
    give(WIDE, grads[5:7])
    ends[OUTPUT - 1].wait_recv()
    mine, came = final[OUTPUT][side(core, 8), :], theirs[OUTPUT - 1][...]
    both = (jnp.where(core == 0, mine, came), jnp.where(core == 0, came, mine))
    for c in range(8):
        grads[4][pl.ds(c, 8, stride=8), :] = both[c // 4][:, (c % 4) * 128:(c % 4 + 1) * 128]
    rs.turn(BACK_OF[INPUT], 2)
    rs.land(BACK_OF[INPUT], 2)
    swap(INPUT)
    give(INPUT, grads[0:4])
    for cp in ends:
        cp.wait_send()
    for k in range(1, 4):
        quarter(k).wait_send()
    passed[1].wait_send()
    passed[2].wait_send()
    scan.drain()
    rs.drain()


def backward(ids, tags_all, decays, arrays):
    v = pl.BlockSpec(memory_space=pltpu.VMEM)
    anywhere = pl.BlockSpec(memory_space=pl.ANY)
    sds = jax.ShapeDtypeStruct
    vm = pltpu.VMEM
    n = len(BACK_UNITS)
    scratch = [vm(live_dims(()) + tail, LOW) for tail in HELD]
    for stage in range(3):
        for i, s, lo, hi in BACK_UNITS:
            tail = (hi - lo, 256) if i == DOWN else (HELD[i][0], hi - lo)
            scratch.append(vm((3,) + live_dims(BACK_ORDERS[s][:stage + 1]) + tail, LOW))
    scratch += [vm(tail, F32) for tail in HELD] + [vm((8, tail[1]), F32) for tail in HELD[1:]]
    full = lambda width, kind=LOW: vm((ROWS, width), kind)
    scratch += [vm((4, 24, 256), F32), vm((4, 24, 256), F32), vm((2, 256, FF), LOW), vm((2, FF, ROWS), LOW),
        vm((2, D, ROWS), LOW), vm((2, D, ROWS), LOW), vm((2, ROWS, D // 2), LOW), full(D), full(2 * FF), full(FF), full(D), full(D // 2),
        full(2 * D), full(2 * FF), full(3 * D), full(2 * D), full(D), full(D, F32), full(D, F32), full(D), full(D, F32), full(D, F32), full(D)]
    scratch += [vm((N_SEQ, HD, HD), LOW)] * 5 + [vm((2, HD, HD), F32)] * 2
    scratch += [DMA((16,)), DMA((2,)), DMA((n, 3, 4)), DMA((n, 3, 4))] + [DMA((N_SEQ,))] * 4 + [DMA((3,))] * 4 + [DMA((4,))] * 2
    return pl.pallas_call(
        backward_kernel,
        out_shape=[sds((ROWS, D), F32)] + [sds((64, 128), F32)] * 5 + [sds((176, 128), F32)] * 3,
        in_specs=[v, v, pl.BlockSpec(memory_space=pltpu.SMEM)] + [anywhere] * len(arrays),
        out_specs=[v] * 9,
        scratch_shapes=scratch,
        compiler_params=pltpu.CompilerParams(collective_id=1, has_side_effects=True, vmem_limit_bytes=60 << 20),
        name="backward_and_scatter",
    )(ids, tags_all, decays, *arrays)


def on_device(hidden_in, seg_ids, decay_rates, grad_out, *weights):
    x, cot = hidden_in.reshape(ROWS, D), grad_out.reshape(ROWS, D)
    ids = seg_ids.reshape(2, HD).astype(F32)
    (act, tags_all, qkv, slopes, gate, mixed, resid, up, carried, w_in, w_output, w_up, w_down, t_first, t_gated, t_second,
     t_product, b_branch) = forward(x, cot, ids, decay_rates, [w.reshape(-1, 128) for w in weights])
    input_grad, *grads = backward(ids, tags_all, decay_rates, [
        x, cot, qkv, slopes, gate, mixed, resid, up, carried, w_in.reshape(D, 4 * D), w_output.reshape(D, D),
        w_up.reshape(D, 2 * FF), w_down, t_first, t_gated, t_second, t_product, b_branch])
    return (act.reshape(hidden_in.shape), input_grad.reshape(hidden_in.shape), *(g.reshape(-1) for g in grads))


def solution(mesh):
    tokens = P(None, "dp", "seq", None)
    flat = P(("dp", "seq"))
    return jax.shard_map(
        on_device, mesh=mesh,
        in_specs=(tokens, P(None, "dp", "seq"), P(), tokens) + (flat,) * 8,
        out_specs=(tokens, tokens) + (flat,) * 8,
        check_vma=False,
    )
```

time: 320 us -> 249 us (0.78)
  matrix products: 57.2 us -> 0 us
  Pallas kernels: 209 us -> 238 us
  local copies, waits for them, and re-layouts: 36 us -> 8.16 us
  other arithmetic: 14.3 us -> 1.24 us
    dot_general x16 -> x0, matrix products: 57.2 us -> none  [matmul(): jnp.einsum(form, left_op, right_op, preferred_element_type=jnp.float32)]
    pallas_call x3 -> x2, Pallas kernels: 209 us -> 238 us  [the longest x1 135 us: backward(): pl.pallas_call(backward_kernel, out_shape=[sds((ROWS, D), F32)] + [sds((6...]
    reshape x5 -> x0, local copies, waits for them, and re-layouts: 13.5 us -> none  [the longest x1 9.73 us: on_device(): g_down.reshape(OWNERS + (176, 128))]
    convert_element_type x5 -> x1, other arithmetic: 9.05 us -> 1.24 us  [on_device(): ids = seg_ids.reshape(2, HD).astype(F32)]
    add x2 -> x0, local copies, waits for them, and re-layouts: 5.09 us -> none  [the longest x1 2.54 us: on_device(): d_query + matmul('sihe,shde->sihd', d_mixed, carried) * reaching[..., None]]
    unnamed x68 -> x28, local copies, waits for them, and re-layouts: 12.9 us -> 8.16 us
where the time goes in v3:
time: 249 us; the launch traced here: 248 us
  Pallas kernels  238 us (96%)
  local copies, waits for them, and re-layouts  8.16 us (3%)
    pallas_call x1, Pallas kernels, backward(): pl.pallas_call(backward_kernel, out_shape=[sds((ROWS, D), F32)] + [sds((6...  135 us
    pallas_call x1, Pallas kernels, forward(): pl.pallas_call(forward_kernel, out_shape=outs, in_specs=[v, v, v, pl.Bloc...  103 us
    unnamed x28, local copies, waits for them, and re-layouts  8.16 us

profile of v3, /device:TPU:1, one launch (start us, length us, event | category | flops | bytes accessed | tf_op | source)
XLA Modules:
  0.0 248.1 jit_solution(2447904821318869067)
XLA Ops:
  0.6 1.2 convert_bitcast_fusion.refs_2_.refs_0_
  1.9 103.4 %gather_and_forward.1 = (bf16[256,1024]{1,0:T(8,128)(2,1)}, f32[16,8,128]{2,1,0:T(8,128)}, bf16[256,3072]{1,0:T(8,128)(2,1)}, bf16[256,2048]{1,0:T(8,128)(2,1)},...) custom-call(bf16[256,1024]{1,0:T(8,128)(2,1)} %bitcast.32, ...), custom_call_target="tpu_custom_call" | custom-call | tf_op jit(solution)/shard_map/gather_and_forward/pallas_call | solution.py:483
  105.3 134.5 %backward_and_scatter.1 = (f32[256,1024]{1,0:T(8,128)}, f32[64,128]{1,0:T(8,128)}, f32[64,128]{1,0:T(8,128)}, f32[64,128]{1,0:T(8,128)}, f32[64,128]{1,0:T(8,128...) custom-call(f32[2,128]{1,0:T(2,128)} %convert_bitcast_fusion.refs_2_.refs_0_, ...), custom_call_target="tpu_custom_call" | custom-call | tf_op jit(solution)/shard_map/backward_and_scatter/pallas_call | solution.py:935
  239.8 0.0 copy-start.8
  239.9 0.0 copy-start.7
  239.9 0.0 copy-start.6
  239.9 0.0 copy-start.5
  239.9 0.0 copy-start.4
  239.9 0.0 copy-start.3
  239.9 0.0 copy-start.2
  239.9 0.0 copy-start.1
  239.9 0.0 copy-done
  239.9 0.8 copy.35
  240.7 2.3 copy.36
  243.0 0.6 copy.37
  243.7 0.6 copy.38
  244.3 0.6 copy.39
  244.9 0.6 copy.40
  245.5 0.6 copy.41
  246.1 0.0 copy-done.3
  246.1 0.6 copy.42
  246.8 0.6 copy.43
  247.4 0.0 copy-done.1
  247.4 0.6 copy.44
  (7 shorter events, 0.0 us)
Async XLA Ops:
  105.3 134.6 %copy-start = (bf16[256,1024]{1,0:T(8,128)(2,1)S(1)}, bf16[256,1024]{1,0:T(8,128)(2,1)}, u32[]{:S(2)}) copy-start(bf16[256,1024]{1,0:T(8,128)(2,1)} %get-tuple-element.37) | copy-start | bytes 1572868
  239.8 3.2 %copy-start.8 = (f32[64,128]{1,0:T(8,128)S(1)}, f32[64,128]{1,0:T(8,128)}, u32[]{:S(2)}) copy-start(f32[64,128]{1,0:T(8,128)} %get-tuple-element.56) | copy-start | bytes 98308
  239.9 3.8 %copy-start.7 = (f32[64,128]{1,0:T(8,128)S(1)}, f32[64,128]{1,0:T(8,128)}, u32[]{:S(2)}) copy-start(f32[64,128]{1,0:T(8,128)} %get-tuple-element.57) | copy-start | bytes 98308
  239.9 4.4 %copy-start.6 = (f32[64,128]{1,0:T(8,128)S(1)}, f32[64,128]{1,0:T(8,128)}, u32[]{:S(2)}) copy-start(f32[64,128]{1,0:T(8,128)} %get-tuple-element.58) | copy-start | bytes 98308
  239.9 5.0 %copy-start.5 = (f32[64,128]{1,0:T(8,128)S(1)}, f32[64,128]{1,0:T(8,128)}, u32[]{:S(2)}) copy-start(f32[64,128]{1,0:T(8,128)} %get-tuple-element.59) | copy-start | bytes 98308
  239.9 5.6 %copy-start.4 = (f32[64,128]{1,0:T(8,128)S(1)}, f32[64,128]{1,0:T(8,128)}, u32[]{:S(2)}) copy-start(f32[64,128]{1,0:T(8,128)} %get-tuple-element.60) | copy-start | bytes 98308
  239.9 6.2 %copy-start.3 = (f32[176,128]{1,0:T(8,128)S(1)}, f32[176,128]{1,0:T(8,128)}, u32[]{:S(2)}) copy-start(f32[176,128]{1,0:T(8,128)} %get-tuple-element.61) | copy-start | bytes 270340
  239.9 6.9 %copy-start.2 = (f32[176,128]{1,0:T(8,128)S(1)}, f32[176,128]{1,0:T(8,128)}, u32[]{:S(2)}) copy-start(f32[176,128]{1,0:T(8,128)} %get-tuple-element.62) | copy-start | bytes 270340
  239.9 7.5 %copy-start.1 = (f32[176,128]{1,0:T(8,128)S(1)}, f32[176,128]{1,0:T(8,128)}, u32[]{:S(2)}) copy-start(f32[176,128]{1,0:T(8,128)} %get-tuple-element.63) | copy-start | bytes 270340

commit v4 on v3

--- a/solution.py
+++ b/solution.py
@@ -27,12 +27,13 @@
 
 
 CHUNKS = (
-    tuple(tiles(0, (0, 11, 22, 32)) + tiles(1, (0, 2, 5, 8))),
-    tuple(tiles(2, (0, 15, 30, 44))),
+    tuple(tiles(0, (0, 10, 20, 32))),
+    tuple(tiles(1, (0, 4, 8)) + tiles(2, (0, 15, 30, 44))),
     tuple(tiles(3, (0, 7, 14, 22), 8)),
 )
 UNITS = CHUNKS[0] + CHUNKS[1] + CHUNKS[2]
 C1, C2, C3 = (tuple(UNITS.index(u) for u in chunk) for chunk in CHUNKS)
+C2_FIRST = C2[:2]
 
 
 def where_am_i():
@@ -124,32 +125,32 @@
     def begin(self, units, stage):
         for u in units:
             a = self.axis(u, stage)
-            mine = self.part(u, self.me, stage)
-            self.go(self.copy(mine, u, 4 * stage, moved(self.me, a, 1)))
-            self.go(self.copy(mine, u, 4 * stage + 1, moved(self.me, a, -1)))
+            for k, (half, by) in enumerate(((0, 1), (1, -1), (1, 1), (0, -1))):
+                self.go(self.copy(self.part(u, self.me, stage, half), u, 6 * stage + k, moved(self.me, a, by)))
             if stage == 2:
-                self.go(self.ccopy(mine, u, 0))
+                self.go(self.ccopy(self.part(u, self.me, stage), u, 0))
 
     def relay(self, units, stage):
         for u in units:
             a = self.axis(u, stage)
-            above, below = moved(self.me, a, 1), moved(self.me, a, -1)
-            self.copy(self.part(u, below, stage), u, 4 * stage, below).wait_recv()
-            self.go(self.copy(self.part(u, below, stage, 0), u, 4 * stage + 2, above))
-            self.copy(self.part(u, above, stage), u, 4 * stage + 1, above).wait_recv()
-            self.go(self.copy(self.part(u, above, stage, 1), u, 4 * stage + 3, below))
-            if stage == 2:
-                self.go(self.ccopy(self.part(u, below, stage), u, 1))
-                self.go(self.ccopy(self.part(u, above, stage), u, 2))
+            for half, by in ((0, 1), (1, -1)):
+                first = self.part(u, moved(self.me, a, -by), stage, half)
+                self.copy(first, u, 6 * stage + half, moved(self.me, a, by)).wait_recv()
+                self.go(self.copy(first, u, 6 * stage + 4 + half, moved(self.me, a, by)))
 
     def finish(self, units, stage):
         for u in units:
             a = self.axis(u, stage)
-            far = moved(self.me, a, 2)
-            for half in range(2):
-                self.copy(self.part(u, far, stage, half), u, 4 * stage + 2 + half, moved(self.me, a, 1)).wait_recv()
+            for k, by, half in ((2, -1, 1), (3, 1, 0), (4, 2, 0), (5, 2, 1)):
+                self.copy(self.part(u, moved(self.me, a, by), stage, half), u, 6 * stage + k, moved(self.me, a, 1)).wait_recv()
             if stage == 2:
-                self.go(self.ccopy(self.part(u, far, stage), u, 3))
+                for k, by in enumerate((-1, 1, 2)):
+                    self.go(self.ccopy(self.part(u, moved(self.me, a, by), stage), u, 1 + k))
+
+    def advance(self, units, stage):
+        for u in units:
+            self.finish((u,), stage)
+            self.begin((u,), stage + 1)
 
     def arrive(self, units):
         sib = moved(self.me, "c", 1)
@@ -319,34 +320,27 @@
     g.relay(C1, 0)
     g.relay(C2, 0)
     g.relay(C3, 0)
+    g.advance(C1, 0)
     for m in range(2):
         down, across = spread(ids[m:m + 1, :])
         ids_down[m] = down
         allowed[m] = jnp.where((down == across) & (row_index() >= column_index()), 1.0, 0.0)
         kept_mask[m] = jnp.where(down == jnp.broadcast_to(ids[m:m + 1, HD - 1:HD], (HD, HD)), 1.0, 0.0)
+    g.relay(C1, 1)
+    g.advance(C2, 0)
+    g.advance(C1, 1)
+    g.advance(C3, 0)
     half = lambda c: cot.at[:, pl.ds(pl.multiple_of(c * 512, 512), 512)]
     hand(half(me["c"]), half(sib["c"]), b_branch)
-    g.finish(C1, 0)
-    g.begin(C1, 1)
-    g.finish(C2, 0)
-    g.begin(C2, 1)
-    g.finish(C3, 0)
-    g.begin(C3, 1)
-    g.relay(C1, 1)
-    g.relay(C2, 1)
-    g.relay(C3, 1)
-    g.finish(C1, 1)
-    g.begin(C1, 2)
-    g.finish(C2, 1)
-    g.finish(C3, 1)
     transpose_into(first_in, first_t, D)
     hand(first_t, first_t, t_first)
+    g.relay(C2, 1)
     g.relay(C1, 2)
-    g.begin(C2, 2)
+    g.relay(C3, 1)
+    g.advance(C2, 1)
     g.finish(C1, 2)
     g.arrive(C1)
     keep(w_in, o_in)
-    keep(w_output, o_output)
 
     m_in = w_in.reshape(D, 4 * D)
     def project(k, _):
@@ -355,7 +349,7 @@
         return 0
     lax.fori_loop(0, 8, project, 0)
     g.relay(C2, 2)
-    g.begin(C3, 2)
+    g.advance(C3, 1)
 
     def rows_of_heads(rows):
         for k in range(2):
@@ -378,7 +372,6 @@
         return 0
     lax.fori_loop(0, 2 * H, states, 0)
     scan.start()
-    g.finish(C2, 2)
 
     def within(p, _):
         micro, head, rows, cols = pair_at(p)
@@ -390,7 +383,10 @@
     scan.each(lambda frm: pltpu.make_async_remote_copy(src_ref=tag, dst_ref=tags_all.at[frm], send_sem=tag_send.at[frm],
         recv_sem=tag_recv.at[frm], device_id=(dp, to(1)), device_id_type=MESH).wait_recv())
     scan.join(tags_all, decays, False)
+    g.finish(C2, 2)
     g.relay(C3, 2)
+    g.arrive(C2_FIRST)
+    keep(w_output, o_output)
     scan.finish()
     keep(carried, o_carried)
 
@@ -411,6 +407,9 @@
     def output(k, _):
         cols = columns_of(k, 512)
         resid[:, cols] = x[:, cols].astype(F32) + dot(gated[...], m_output[:, cols])
+        for c in range(4):
+            at = columns_of(k * 4 + c, 128)
+            gated_t[at, :] = gated[:, at].T
         return 0
     lax.fori_loop(0, 2, output, 0)
     keep(resid, o_resid)
@@ -418,8 +417,9 @@
         v = resid[rows, :]
         second[rows, :] = (v * rms_factor(v)).astype(LOW)
     by_rows(ROWS, 32, norm_second)
+    hand(gated_t, gated_t, t_gated)
     g.finish(C3, 2)
-    g.arrive(C2)
+    g.arrive(C2[2:])
     keep(w_up, o_wide)
     m_up = w_up.reshape(D, 2 * FF)
     def widen(k, _):
@@ -428,16 +428,13 @@
         right = dot(second[...], m_up[:, more])
         up[:, cols] = left.astype(LOW)
         up[:, more] = right.astype(LOW)
-        product[:, cols] = (left * right).astype(LOW)
+        both = (left * right).astype(LOW)
+        product[:, cols] = both
+        product_t[cols, :] = both.T
         return 0
     lax.fori_loop(0, 11, widen, 0)
     keep(up, o_up)
-    transpose_into(product, product_t, FF)
     hand(product_t, product_t, t_product)
-    transpose_into(gated, gated_t, D)
-    hand(gated_t, gated_t, t_gated)
-    transpose_into(second, second_t, D)
-    hand(second_t, second_t, t_second)
     g.arrive(C3)
     flat = w_flat.reshape(128 * 176, 128)
     def arrange(k, _):
@@ -450,8 +447,12 @@
     def last(k, _):
         cols = columns_of(k, 512)
         act[:, cols] = (resid[:, cols] + dot(product[...], w_down[:, cols])).astype(LOW)
+        for c in range(4):
+            at = columns_of(k * 4 + c, 128)
+            second_t[at, :] = second[:, at].T
         return 0
     lax.fori_loop(0, 2, last, 0)
+    hand(second_t, second_t, t_second)
     for cp in kept:
         cp.wait()
     for k, (cp, dst) in enumerate(passed):
@@ -479,7 +480,7 @@
         vm((ROWS, D), F32), vm((ROWS, D), F32), vm((ROWS, 2 * FF), LOW), vm((ROWS, D), LOW), vm((ROWS, D), LOW), vm((ROWS, FF), LOW),
         vm((D, ROWS), LOW), vm((D, ROWS), LOW), vm((D, ROWS), LOW), vm((FF, ROWS), LOW)] + [vm((N_SEQ, HD, HD), LOW)] * 4 + [
         vm((1408, 128), F32), vm((8, HD), F32)] + [vm((2, HD, HD), F32)] * 3 + [
-        DMA((n, 12)), DMA((n, 12)), DMA((n, 4)), DMA((n, 4))] + [DMA((N_SEQ,))] * 6 + [DMA((20,)), DMA((5,)), DMA((5,))]
+        DMA((n, 18)), DMA((n, 18)), DMA((n, 4)), DMA((n, 4))] + [DMA((N_SEQ,))] * 6 + [DMA((20,)), DMA((5,)), DMA((5,))]
     return pl.pallas_call(
         forward_kernel, out_shape=outs,
         in_specs=[v, v, v, pl.BlockSpec(memory_space=pltpu.SMEM)] + [v] * 8,
@@ -496,8 +497,16 @@
 
 DOWN, WIDE, OUTPUT, INPUT = range(4)
 HELD = ((88, 256), (16, FF), (16, D // 2), (16, 2 * D))
-BACK_UNITS = tuple(tiles(DOWN, (0, 3, 7, 11), 8) + tiles(WIDE, (0, 7, 14, 22)) + tiles(OUTPUT, (0, 2, 4)) + tiles(INPUT, (0, 5, 10, 16)))
-BACK_OF = [tuple(u for u, unit in enumerate(BACK_UNITS) if unit[0] == i) for i in range(4)]
+GROUPS = (
+    tiles(DOWN, (0, 3, 7, 11), 8),
+    tiles(WIDE, (0, 7, 14, 22)),
+    [(OUTPUT, 0, 0, 256), (OUTPUT, 1, 256, 512)],
+    [(INPUT, 1, 1536, 1792), (INPUT, 2, 1792, 2048)],
+    [(INPUT, 2, 0, 256), (INPUT, 0, 256, 512)],
+    [(INPUT, 0, 512, 896), (INPUT, 1, 896, 1280), (INPUT, 2, 1280, 1536)],
+)
+BACK_UNITS = tuple(unit for group in GROUPS for unit in group)
+G_DOWN, G_WIDE, G_OUTPUT, G_GATE, G_QUERY, G_VALUE = (tuple(BACK_UNITS.index(unit) for unit in group) for group in GROUPS)
 BACK_ORDERS = tuple(order[::-1] for order in ORDERS)
 DIMS = (("y", 4), ("x", 2), ("z", 4), ("x", 2))
 
@@ -569,10 +578,17 @@
     def far(self, units, stage):
         for u in units:
             held, order, rows, lo, mid, hi = self.spans(u)
-            at = moved(self.me, order[stage], 2)
-            fixed = order[:stage + 1]
-            self.send(part_of(held, at, fixed, (), lo, mid, rows), self.slot(u, stage, 0, lo, mid), u, stage, 0, moved(self.me, order[stage], 1))
-            self.send(part_of(held, at, fixed, (), mid, hi, rows), self.slot(u, stage, 0, mid, hi), u, stage, 1, moved(self.me, order[stage], -1))
+            axis, fixed = order[stage], order[:stage + 1]
+            above, below, across = (moved(self.me, axis, by) for by in (1, -1, 2))
+            mine = lambda at, a, b: part_of(held, at, fixed, (), a, b, rows)
+            if stage == 2:
+                for k, at in enumerate((across, above, below)):
+                    self.send(mine(at, lo, hi), self.slot(u, stage, k, lo, hi), u, stage, k, at)
+                continue
+            self.send(mine(across, lo, mid), self.slot(u, stage, 0, lo, mid), u, stage, 0, above)
+            self.send(mine(across, mid, hi), self.slot(u, stage, 0, mid, hi), u, stage, 1, below)
+            self.send(mine(above, mid, hi), self.slot(u, stage, 1, mid, hi), u, stage, 2, above)
+            self.send(mine(below, lo, mid), self.slot(u, stage, 2, lo, mid), u, stage, 3, below)
 
     def turn(self, units, stage):
         for u in units:
@@ -582,24 +598,26 @@
                 to = moved(self.me, order[stage], by)
                 came = self.slot(u, stage, 0, a, b)
                 self.got(came, u, stage, k)
-                accumulate(part_of(held, to, fixed, (), a, b, rows), [came], live_dims(fixed))
-                self.send(part_of(held, to, fixed, (), lo, hi, rows), self.slot(u, stage, 1 + k, lo, hi), u, stage, 2 + k, to)
+                sums = part_of(held, to, fixed, (), a, b, rows)
+                accumulate(sums, [came], live_dims(fixed))
+                self.send(sums, self.slot(u, stage, 1 + k, a, b), u, stage, 4 + k, to)
 
     def land(self, units, stage):
         for u in units:
             held, order, rows, lo, mid, hi = self.spans(u)
             fixed = order[:stage + 1]
-            came = [self.slot(u, stage, 1 + k, lo, hi) for k in range(2)]
-            for k in range(2):
-                self.got(came[k], u, stage, 2 + k)
             mine = part_of(held, self.me, fixed, (), lo, hi, rows)
-            if stage < 2:
-                accumulate(mine, came, live_dims(fixed))
-            else:
+            if stage == 2:
+                came = [self.slot(u, stage, k, lo, hi) for k in range(3)]
+                for k in range(3):
+                    self.got(came[k], u, stage, k)
                 span = pl.ds(lo, hi - lo)
                 accumulate(mine, came, (), self.final[BACK_UNITS[u][0]].at[(span, slice(None)) if rows else (slice(None), span)])
-        if stage < 2:
-            self.far(units, stage + 1)
+                continue
+            for k, (a, b) in ((2, (mid, hi)), (3, (lo, mid)), (4, (lo, mid)), (5, (mid, hi))):
+                self.got(self.slot(u, stage, 1 + k % 2, a, b), u, stage, k)
+            accumulate(mine, [self.slot(u, stage, 1 + k, lo, hi) for k in range(2)], live_dims(fixed))
+            self.far((u,), stage + 1)
 
     def drain(self):
         for cp in self.sends:
@@ -621,7 +639,7 @@
     refs = refs[3 * n:]
     final, theirs, refs = refs[:4], refs[4:7], refs[7:]
     (quarters, regroup, wbuf, product_t, lhs_a, lhs_b, branch, cot, d_up, up_sib, d_attn, attn_sib, pre_sib,
-     up, qkv, slopes, gate, mixed, resid, x, d_resid, work, d_mixed, carried, local, came, going, reverse, ids_down, allowed,
+     up, qkv, slopes, gate, mixed, resid, x, work, d_mixed, carried, local, came, going, reverse, ids_down, allowed,
      load_sem, wsem, send_sem, recv_sem, s1, r1, s2, r2, pass_send, pass_recv, end_send, end_recv, q_send, q_recv) = refs
     me = where_am_i()
     sib = moved(me, "c", 1)
@@ -629,7 +647,7 @@
     seq, dp = lax.axis_index("seq"), lax.axis_index("dp")
     to = lambda k: (seq + k) % N_SEQ
     barrier = pltpu.get_barrier_semaphore()
-    close = neighbours(me)
+    close = neighbours(me) + [moved(me, a, 2) for a in "xyz"]
     for other in close:
         pl.semaphore_signal(barrier, inc=1, device_id=device(other), device_id_type=MESH)
 
@@ -647,38 +665,44 @@
     load("branch", b_branch, branch)
     load("cot", h_cot, cot)
 
-    phases = ((w_down, 11, 0, D), (w_up, 4, 0, FF), (w_up, 4, FF, FF), (w_output, 4, 0, D), (w_in, 4, 0, 2 * D), (w_in, 4, 2 * D, 2 * D))
+    phases = ((w_down, 11, 0, D), (w_up, 4, 0, FF), (w_up, 4, FF, FF), (w_output, 4, 0, D),
+        (w_in, 4, 3 * D, D), (w_in, 4, 0, 2 * D), (w_in, 4, 2 * D, D))
     first = [sum(p[1] for p in phases[:k]) for k in range(len(phases))]
     def piece(phase, k):
         w, _, col, width = phases[phase]
-        slot = (first[phase] + k) % 2
+        slot = (first[phase] + k) % 3
         row = pl.multiple_of(k * 256, 256)
         return pltpu.make_async_copy(w.at[pl.ds(row, 256), pl.ds(col, width)], wbuf.at[slot, :, pl.ds(0, width)], wsem.at[slot])
     def stream(phase, compute):
         count, width = phases[phase][1], phases[phase][3]
         def one(k, _):
+            @pl.when(k + 2 < count)
+            def _():
+                piece(phase, k + 2).start()
+            if phase + 1 < len(phases):
+                @pl.when(k + 2 >= count)
+                def _():
+                    piece(phase + 1, k + 2 - count).start()
             piece(phase, k).wait()
-            @pl.when(k + 1 < count)
-            def _():
-                piece(phase, k + 1).start()
-            if phase + 1 < len(phases):
-                @pl.when(k + 1 == count)
-                def _():
-                    piece(phase + 1, 0).start()
-            compute(k, wbuf.at[(first[phase] + k) % 2, :, pl.ds(0, width)])
+            compute(k, wbuf.at[(first[phase] + k) % 3, :, pl.ds(0, width)])
             return 0
         lax.fori_loop(0, count, one, 0)
     piece(0, 0).start()
+    piece(0, 1).start()
     load("up", h_up, up)
-    load("second", t_second, lhs_a)
     load("resid", h_resid, resid)
-    load("gated", t_gated, lhs_b)
     load("mixed", h_mixed, mixed)
     load("gate", h_gate, gate)
     load("qkv", h_qkv, qkv)
+    load("second", t_second, lhs_a)
+    load("gated", t_gated, lhs_b)
+    load("carried", h_carried, carried)
     load("slopes", h_slopes, slopes)
-    load("carried", h_carried, carried)
     load("x", h_x, x)
+    for m in range(2):
+        below, across = spread(ids[m:m + 1, :])
+        ids_down[m] = below
+        allowed[m] = jnp.where((below == across) & (row_index() >= column_index()), 1.0, 0.0)
     pl.semaphore_wait(barrier, len(close) + N_SEQ - 1)
 
     rs = Scatter(held, slots, final, me, send_sem, recv_sem)
@@ -703,7 +727,7 @@
                 held[DOWN][k // 2, k % 2, i, j] = total[i * 88:(i + 1) * 88].astype(LOW)
         return 0
     lax.fori_loop(0, 8, down_rows, 0)
-    rs.far(BACK_OF[DOWN], 0)
+    rs.far(G_DOWN, 0)
 
     loads["cot"].wait()
     loads["up"].wait()
@@ -713,46 +737,61 @@
         d_up[:, cols] = (d_product * up[:, more].astype(F32)).astype(LOW)
         d_up[:, more] = (d_product * up[:, cols].astype(F32)).astype(LOW)
     stream(0, up_back)
-    side = lambda c, width: pl.ds(pl.multiple_of(c * width, width), width)
-    hand(d_up.at[:, side(other_core, FF)], up_sib)
-    rs.turn(BACK_OF[DOWN], 0)
+    side = lambda c, width, base=0: pl.ds(pl.multiple_of(c * width + base, 128), width)
+    h_wide = hand(d_up.at[:, side(other_core, FF)], up_sib)
     def second_left(k, w):
         work[:, columns_of(k, 256)] = dot(d_up[:, 0:FF], w[...], ((1,), (1,)))
     stream(1, second_left)
+    rs.turn(G_DOWN, 0)
+
+    def grad_half(i, lhs, own, base, shift, sibling, units):
+        out = held[i].reshape(D, HELD[i][1])
+        for u in units:
+            _, _, lo, hi = BACK_UNITS[u]
+            a = lo
+            while a < hi:
+                wide = min(256, hi - a)
+                mine = own[:, pl.ds(pl.multiple_of(base + (a - shift), 128), wide)]
+                total = dot(lhs[core], mine) + dot(lhs[other_core], sibling[:, a:a + wide])
+                out[:, a:a + wide] = total.astype(LOW)
+                a += wide
+            rs.far((u,), 0)
+
+    loads["second"].wait()
+    h_wide.wait_recv()
+    grad_half(WIDE, lhs_a, d_up, core * FF, 0, up_sib, G_WIDE)
+    load("first", t_first, lhs_a)
+    rs.land(G_DOWN, 0)
     def second_right(k, w):
         work[:, columns_of(k, 256)] += dot(d_up[:, FF:2 * FF], w[...], ((1,), (1,)))
     stream(2, second_right)
-    rs.land(BACK_OF[DOWN], 0)
 
     loads["resid"].wait()
     def resid_back(rows):
         v = resid[rows, :]
         factor = rms_factor(v)
         total = cot[rows, :].astype(F32) + norm_back(work[rows, :], v * factor, factor)
-        d_resid[rows, :] = total
+        resid[rows, :] = total
         d_attn[rows, :] = total.astype(LOW)
     by_rows(ROWS, 16, resid_back)
-    hand(d_attn.at[:, side(other_core, D // 2)], attn_sib)
-    rs.turn(BACK_OF[DOWN], 1)
+    h_attn = hand(d_attn.at[:, side(other_core, D // 2)], attn_sib)
+    rs.turn(G_DOWN, 1)
+    rs.turn(G_WIDE, 0)
     def gated_back(k, w):
         work[:, columns_of(k, 256)] = dot(d_attn[...], w[...], ((1,), (1,)))
     stream(3, gated_back)
     loads["mixed"].wait()
     loads["gate"].wait()
-    d_gate = resid
     def mixed_back(rows):
         v = mixed[rows, :]
         factor = rms_factor(v)
         normed = v * factor
         g = work[rows, :]
-        d_gate[rows, :] = g * normed
         d_mixed[rows, :] = norm_back(g * gate[rows, :].astype(F32), normed, factor).astype(LOW)
+        gate[rows, :] = (g * normed).astype(LOW)
     by_rows(ROWS, 16, mixed_back)
+    h_gate_out = hand(gate.at[:, side(other_core, D // 2)], pre_sib.at[:, pl.ds(1536, 512)])
     loads["qkv"].wait()
-    for m in range(2):
-        below, across = spread(ids[m:m + 1, :])
-        ids_down[m] = below
-        allowed[m] = jnp.where((below == across) & (row_index() >= column_index()), 1.0, 0.0)
     def back_states(p, _):
         micro, head, rows, cols = pair_at(p)
         start = ids[pl.ds(micro, 1), 0:1]
@@ -762,37 +801,20 @@
         return 0
     lax.fori_loop(0, 2 * H, back_states, 0)
     scan.start()
-    rs.land(BACK_OF[DOWN], 1)
-    rs.turn(BACK_OF[DOWN], 2)
-
-    def grad_half(i, lhs, own, base, sibling, units):
-        out = held[i].reshape(D, HELD[i][1])
-        for u in units:
-            _, _, lo, hi = BACK_UNITS[u]
-            a = lo
-            while a < hi:
-                wide = min(256, hi - a)
-                mine = own[:, pl.ds(pl.multiple_of(base + a, 128), wide)]
-                total = dot(lhs[core], mine) + dot(lhs[other_core], sibling[:, a:a + wide])
-                out[:, a:a + wide] = total.astype(LOW)
-                a += wide
-            rs.far((u,), 0)
-
-    loads["second"].wait()
-    passed[0].wait_recv()
-    grad_half(WIDE, lhs_a, d_up, core * FF, up_sib, BACK_OF[WIDE])
-    load("first", t_first, lhs_a)
-    rs.land(BACK_OF[DOWN], 2)
+    rs.land(G_DOWN, 1)
     loads["gated"].wait()
-    passed[1].wait_recv()
-    grad_half(OUTPUT, lhs_b, d_attn, core * (D // 2), attn_sib, BACK_OF[OUTPUT])
+    h_attn.wait_recv()
+    grad_half(OUTPUT, lhs_b, d_attn, core * (D // 2), 0, attn_sib, G_OUTPUT)
+    loads["first"].wait()
+    h_gate_out.wait_recv()
+    grad_half(INPUT, lhs_a, gate, core * (D // 2), 1536, pre_sib, G_GATE)
+    rs.land(G_WIDE, 0)
     scan.join(tags_all, decays, True)
-    rs.turn(BACK_OF[WIDE], 0)
-
-    passed[0].wait_send()
+
+    h_wide.wait_send()
     loads["slopes"].wait()
     loads["carried"].wait()
-    d_pre = d_up.at[:, 0:4 * D]
+    d_pre = d_up.at[:, 0:3 * D]
     def pair_back(p, _):
         micro, head, rows, cols = pair_at(p)
         q, k, v = (qkv[rows, head_of(head, part)] for part in range(3))
@@ -808,11 +830,13 @@
         mixed[rows, cols] = dot(weighted, dm, ((0,), (0,)))
         return 0
     lax.fori_loop(0, 2 * H, pair_back, 0)
-    def gate_out(rows):
-        d_pre[rows, 3 * D:4 * D] = d_gate[rows, :].astype(LOW)
-    by_rows(ROWS, 16, gate_out)
-    rs.land(BACK_OF[WIDE], 0)
-    rs.turn(BACK_OF[OUTPUT], 0)
+    h_query = hand(d_pre.at[:, side(other_core, D // 2)], pre_sib.at[:, pl.ds(0, 512)])
+    rs.turn(G_OUTPUT, 0)
+    rs.turn(G_GATE, 0)
+    rs.land(G_DOWN, 2)
+    rs.turn(G_WIDE, 1)
+    h_query.wait_recv()
+    grad_half(INPUT, lhs_a, d_pre, core * (D // 2), 0, pre_sib, G_QUERY)
     scan.finish()
     def pair_close(p, _):
         micro, head, rows, cols = pair_at(p)
@@ -824,34 +848,53 @@
         d_pre[rows, head_of(head, 2)] = d_v.astype(LOW)
         return 0
     lax.fori_loop(0, 2 * H, pair_close, 0)
-    hand(d_pre.at[:, side(other_core, 2 * D)], pre_sib)
-    rs.turn(BACK_OF[WIDE], 1)
-    rs.land(BACK_OF[OUTPUT], 0)
-    loads["first"].wait()
-    passed[2].wait_recv()
-    grad_half(INPUT, lhs_a, d_pre, core * 2 * D, pre_sib, BACK_OF[INPUT])
-    rs.land(BACK_OF[WIDE], 1)
-    rs.turn(BACK_OF[OUTPUT], 1)
-    def first_left(k, w):
-        work[:, columns_of(k, 256)] = dot(d_pre[:, 0:2 * D], w[...], ((1,), (1,)))
-    stream(4, first_left)
-    rs.turn(BACK_OF[INPUT], 0)
-    rs.turn(BACK_OF[WIDE], 2)
-    rs.land(BACK_OF[OUTPUT], 1)
-    def first_right(k, w):
-        work[:, columns_of(k, 256)] += dot(d_pre[:, 2 * D:4 * D], w[...], ((1,), (1,)))
-    stream(5, first_right)
-    rs.land(BACK_OF[INPUT], 0)
-    rs.land(BACK_OF[WIDE], 2)
-    rs.turn(BACK_OF[OUTPUT], 2)
+    h_key = hand(d_pre.at[:, side(other_core, D // 2, D)], pre_sib.at[:, pl.ds(512, 512)])
+    h_value = hand(d_pre.at[:, side(other_core, D // 2, 2 * D)], pre_sib.at[:, pl.ds(1024, 512)])
+    rs.land(G_OUTPUT, 0)
+    rs.land(G_GATE, 0)
+    h_key.wait_recv()
+    h_value.wait_recv()
+    out = held[INPUT].reshape(D, 2 * D)
+    for u in G_VALUE:
+        _, _, lo, hi = BACK_UNITS[u]
+        a = lo
+        while a < hi:
+            part, within = a // 512, a % 512
+            wide = min(256, hi - a, 512 - within)
+            mine = d_pre[:, pl.ds(pl.multiple_of(part * D + core * 512 + within, 128), wide)]
+            out[:, a:a + wide] = (dot(lhs_a[core], mine) + dot(lhs_a[other_core], pre_sib[:, a:a + wide])).astype(LOW)
+            a += wide
+        rs.far((u,), 0)
+    rs.turn(G_QUERY, 0)
+    rs.land(G_WIDE, 1)
+    def first_gate(k, w):
+        work[:, columns_of(k, 256)] = dot(gate[...], w[...], ((1,), (1,)))
+    stream(4, first_gate)
+    rs.turn(G_VALUE, 0)
+    rs.turn(G_OUTPUT, 1)
+    rs.turn(G_GATE, 1)
+    rs.land(G_QUERY, 0)
+    def first_keys(k, w):
+        work[:, columns_of(k, 256)] += dot(d_pre[:, 0:2 * D], w[...], ((1,), (1,)))
+    stream(5, first_keys)
+    rs.land(G_VALUE, 0)
+    rs.land(G_OUTPUT, 1)
+    rs.land(G_GATE, 1)
+    rs.turn(G_QUERY, 1)
+    rs.land(G_WIDE, 2)
+    def first_values(k, w):
+        work[:, columns_of(k, 256)] += dot(d_pre[:, 2 * D:3 * D], w[...], ((1,), (1,)))
+    stream(6, first_values)
+    rs.turn(G_VALUE, 1)
+    rs.land(G_QUERY, 1)
     loads["x"].wait()
     def input_back(rows):
         v = x[rows, :].astype(F32)
         factor = rms_factor(v)
-        input_grad[rows, :] = d_resid[rows, :] + norm_back(work[rows, :], v * factor, factor)
+        input_grad[rows, :] = resid[rows, :] + norm_back(work[rows, :], v * factor, factor)
     by_rows(ROWS, 16, input_back)
-    rs.turn(BACK_OF[INPUT], 1)
-    rs.land(BACK_OF[OUTPUT], 2)
+    rs.land(G_OUTPUT, 2)
+    rs.land(G_VALUE, 1)
 
     place = me["x"] // 2 * 2 + core
     def owner(j):
@@ -865,27 +908,22 @@
     for k in range(1, 4):
         quarter(k).start()
     regroup[place] = quarters[place]
-    ends = []
+    ends = {}
     def swap(i):
-        k = len(ends)
-        cp = pltpu.make_async_remote_copy(src_ref=final[i].at[side(other_core, 8), :], dst_ref=theirs[i - 1], send_sem=end_send.at[k],
-            recv_sem=end_recv.at[k], device_id=device(sib), device_id_type=MESH)
+        cp = pltpu.make_async_remote_copy(src_ref=final[i].at[pl.ds(pl.multiple_of(other_core * 8, 8), 8), :], dst_ref=theirs[i - 1],
+            send_sem=end_send.at[i - 1], recv_sem=end_recv.at[i - 1], device_id=device(sib), device_id_type=MESH)
         cp.start()
-        ends.append(cp)
-    def give(i, outs):
-        ends[i - 1].wait_recv()
-        mine, came = final[i][side(core, 8), :], theirs[i - 1][...]
+        ends[i] = cp
+    def give(i, outs, part):
+        ends[i].wait_recv()
+        mine, came = final[i][pl.ds(pl.multiple_of(core * 8, 8), 8), :], theirs[i - 1][...]
         both = (jnp.where(core == 0, mine, came), jnp.where(core == 0, came, mine))
-        width = HELD[i][1]
-        n = len(outs) // 2
+        n = part // 128
         for k, out in enumerate(outs):
-            tiles_out = width // 128 if n == 0 else width // 128 // n
-            for c in range(tiles_out):
-                a = ((k % n) * tiles_out + c) * 128
-                out[pl.ds(c, 8, stride=tiles_out), :] = both[k // n][:, a:a + 128]
+            for c in range(2 * n):
+                out[pl.ds(c, 8, stride=2 * n), :] = both[c // n][:, k * part + (c % n) * 128:k * part + (c % n + 1) * 128]
     swap(WIDE)
     swap(OUTPUT)
-    rs.land(BACK_OF[INPUT], 1)
     for k in range(1, 4):
         j = (place + k) % 4
         pltpu.make_async_remote_copy(src_ref=regroup.at[j], dst_ref=regroup.at[j], send_sem=q_send.at[j],
@@ -894,22 +932,23 @@
         for k in range(2):
             t = (j % 2) * 4 + (j // 2) * 2 + k
             grads[7][pl.ds(t, 22, stride=8), :] = regroup[j, 0:22, k * 128:(k + 1) * 128]
-    give(WIDE, grads[5:7])
-    ends[OUTPUT - 1].wait_recv()
-    mine, came = final[OUTPUT][side(core, 8), :], theirs[OUTPUT - 1][...]
-    both = (jnp.where(core == 0, mine, came), jnp.where(core == 0, came, mine))
-    for c in range(8):
-        grads[4][pl.ds(c, 8, stride=8), :] = both[c // 4][:, (c % 4) * 128:(c % 4 + 1) * 128]
-    rs.turn(BACK_OF[INPUT], 2)
-    rs.land(BACK_OF[INPUT], 2)
+    ends[WIDE].wait_recv()
+    mine, came = final[WIDE][pl.ds(pl.multiple_of(core * 8, 8), 8), :], theirs[WIDE - 1][...]
+    for k, both in enumerate((jnp.where(core == 0, mine, came), jnp.where(core == 0, came, mine))):
+        for c in range(22):
+            grads[5 + k][pl.ds(c, 8, stride=22), :] = both[:, c * 128:(c + 1) * 128]
+    give(OUTPUT, grads[4:5], 512)
+    rs.land(G_GATE, 2)
+    rs.land(G_QUERY, 2)
+    rs.land(G_VALUE, 2)
     swap(INPUT)
-    give(INPUT, grads[0:4])
-    for cp in ends:
+    give(INPUT, grads[0:4], 512)
+    for cp in ends.values():
         cp.wait_send()
     for k in range(1, 4):
         quarter(k).wait_send()
-    passed[1].wait_send()
-    passed[2].wait_send()
+    for cp in passed[1:]:
+        cp.wait_send()
     scan.drain()
     rs.drain()
 
@@ -927,11 +966,11 @@
             scratch.append(vm((3,) + live_dims(BACK_ORDERS[s][:stage + 1]) + tail, LOW))
     scratch += [vm(tail, F32) for tail in HELD] + [vm((8, tail[1]), F32) for tail in HELD[1:]]
     full = lambda width, kind=LOW: vm((ROWS, width), kind)
-    scratch += [vm((4, 24, 256), F32), vm((4, 24, 256), F32), vm((2, 256, FF), LOW), vm((2, FF, ROWS), LOW),
+    scratch += [vm((4, 24, 256), F32), vm((4, 24, 256), F32), vm((3, 256, FF), LOW), vm((2, FF, ROWS), LOW),
         vm((2, D, ROWS), LOW), vm((2, D, ROWS), LOW), vm((2, ROWS, D // 2), LOW), full(D), full(2 * FF), full(FF), full(D), full(D // 2),
-        full(2 * D), full(2 * FF), full(3 * D), full(2 * D), full(D), full(D, F32), full(D, F32), full(D), full(D, F32), full(D, F32), full(D)]
+        full(2 * D), full(2 * FF), full(3 * D), full(2 * D), full(D), full(D, F32), full(D, F32), full(D), full(D, F32), full(D)]
     scratch += [vm((N_SEQ, HD, HD), LOW)] * 5 + [vm((2, HD, HD), F32)] * 2
-    scratch += [DMA((16,)), DMA((2,)), DMA((n, 3, 4)), DMA((n, 3, 4))] + [DMA((N_SEQ,))] * 4 + [DMA((3,))] * 4 + [DMA((4,))] * 2
+    scratch += [DMA((16,)), DMA((3,)), DMA((n, 3, 6)), DMA((n, 3, 6))] + [DMA((N_SEQ,))] * 4 + [DMA((6,))] * 2 + [DMA((3,))] * 2 + [DMA((4,))] * 2
     return pl.pallas_call(
         backward_kernel,
         out_shape=[sds((ROWS, D), F32)] + [sds((64, 128), F32)] * 5 + [sds((176, 128), F32)] * 3,
@@ -943,6 +982,29 @@
     )(ids, tags_all, decays, *arrays)
 
 
+def copy_kernel(*refs):
+    n = len(refs) // 3
+    sems = refs[-1]
+    into = [pltpu.make_async_copy(refs[k], refs[2 * n + k], sems.at[0, k]) for k in range(n)]
+    out = [pltpu.make_async_copy(refs[2 * n + k], refs[n + k], sems.at[1, k]) for k in range(n)]
+    for cp in into:
+        cp.start()
+    for a, b in zip(into, out):
+        a.wait()
+        b.start()
+    for cp in out:
+        cp.wait()
+
+
+def hand_out(arrays):
+    anywhere = pl.BlockSpec(memory_space=pl.ANY)
+    return pl.pallas_call(
+        copy_kernel, out_shape=[jax.ShapeDtypeStruct(a.shape, a.dtype) for a in arrays],
+        in_specs=[anywhere] * len(arrays), out_specs=[anywhere] * len(arrays),
+        scratch_shapes=[pltpu.VMEM(a.shape, a.dtype) for a in arrays] + [DMA((2, len(arrays)))], name="hand_out",
+    )(*arrays)
+
+
 def on_device(hidden_in, seg_ids, decay_rates, grad_out, *weights):
     x, cot = hidden_in.reshape(ROWS, D), grad_out.reshape(ROWS, D)
     ids = seg_ids.reshape(2, HD).astype(F32)
@@ -951,6 +1013,7 @@
     input_grad, *grads = backward(ids, tags_all, decay_rates, [
         x, cot, qkv, slopes, gate, mixed, resid, up, carried, w_in.reshape(D, 4 * D), w_output.reshape(D, D),
         w_up.reshape(D, 2 * FF), w_down, t_first, t_gated, t_second, t_product, b_branch])
+    act, input_grad, *grads = hand_out([act, input_grad, *grads])
     return (act.reshape(hidden_in.shape), input_grad.reshape(hidden_in.shape), *(g.reshape(-1) for g in grads))
 
 

time: 249 us -> 220 us (0.88)
  Pallas kernels: 238 us -> 217 us
  local copies, waits for them, and re-layouts: 8.16 us -> 0 us
    pallas_call x1, Pallas kernels: 135 us -> 111 us  [backward(): pl.pallas_call(backward_kernel, out_shape=[sds((ROWS, D), F32)] + [sds((6...]
    unnamed x28 -> x0, local copies, waits for them, and re-layouts: 8.16 us -> none
    pallas_call x0 -> x1, Pallas kernels: none -> 2.67 us  [hand_out(): pl.pallas_call(copy_kernel, out_shape=[jax.ShapeDtypeStruct(a.shape, a.dt...]
where the time goes in v4:
time: 220 us; the launch traced here: 219 us
  Pallas kernels  217 us (99%)
    pallas_call x1, Pallas kernels, backward(): pl.pallas_call(backward_kernel, out_shape=[sds((ROWS, D), F32)] + [sds((6...  111 us
    pallas_call x1, Pallas kernels, forward(): pl.pallas_call(forward_kernel, out_shape=outs, in_specs=[v, v, v, pl.Bloc...  103 us

profile of v4, /device:TPU:1, one launch (start us, length us, event | category | flops | bytes accessed | tf_op | source)
XLA Modules:
  0.0 219.5 jit_solution(2996643947575405029)
XLA Ops:
  0.6 1.2 convert_bitcast_fusion.refs_2_.refs_0_
  1.9 103.5 %gather_and_forward.1 = (bf16[256,1024]{1,0:T(8,128)(2,1)}, f32[16,8,128]{2,1,0:T(8,128)}, bf16[256,3072]{1,0:T(8,128)(2,1)}, bf16[256,2048]{1,0:T(8,128)(2,1)},...) custom-call(bf16[256,1024]{1,0:T(8,128)(2,1)} %bitcast.32, ...), custom_call_target="tpu_custom_call" | custom-call | tf_op jit(solution)/shard_map/gather_and_forward/pallas_call | solution.py:484
  105.4 111.2 %backward_and_scatter.1 = (f32[256,1024]{1,0:T(8,128)}, f32[64,128]{1,0:T(8,128)}, f32[64,128]{1,0:T(8,128)}, f32[64,128]{1,0:T(8,128)}, f32[64,128]{1,0:T(8,128...) custom-call(f32[2,128]{1,0:T(2,128)} %convert_bitcast_fusion.refs_2_.refs_0_, ...), custom_call_target="tpu_custom_call" | custom-call | tf_op jit(solution)/shard_map/backward_and_scatter/pallas_call | solution.py:974
  216.6 2.7 %hand_out.1 = (bf16[256,1024]{1,0:T(8,128)(2,1)}, f32[256,1024]{1,0:T(8,128)}, f32[64,128]{1,0:T(8,128)}, f32[64,128]{1,0:T(8,128)}, f32[64,128]{1,0:T(8,128)}, ...) custom-call(bf16[256,1024]{1,0:T(8,128)(2,1)} %get-tuple-element.47., ...), custom_call_target="tpu_custom_call" | custom-call | tf_op jit(solution)/shard_map/hand_out/pallas_call | solution.py:1001

commit v5 on v4

--- a/solution.py
+++ b/solution.py
@@ -234,6 +234,14 @@
 
 def column_index():
     return lax.broadcasted_iota(jnp.int32, (HD, HD), 1).astype(F32)
+
+
+def each_pair(body, together=4):
+    def some(k, _):
+        for i in range(together):
+            body(k * together + i, 0)
+        return 0
+    lax.fori_loop(0, 2 * H // together, some, 0)
 
 
 def pair_at(p):
@@ -359,7 +367,7 @@
             slopes[rows, k * D:(k + 1) * D] = (s * (1.0 + u * (1.0 - s))).astype(LOW)
         qkv[rows, 2 * D:3 * D] = pre[rows, 2 * D:3 * D].astype(LOW)
         gate[rows, :] = pre[rows, 3 * D:4 * D].astype(LOW)
-    by_rows(ROWS, 16, rows_of_heads)
+    by_rows(ROWS, 32, rows_of_heads)
     keep(qkv, o_qkv)
     keep(slopes, o_slopes)
     keep(gate, o_gate)
@@ -370,7 +378,7 @@
         held = (qkv[rows, head_of(head, 1)].astype(F32) * keeping).astype(LOW)
         local[p] = dot(held, qkv[rows, head_of(head, 2)], ((0,), (0,))).astype(LOW)
         return 0
-    lax.fori_loop(0, 2 * H, states, 0)
+    each_pair(states)
     scan.start()
 
     def within(p, _):
@@ -379,7 +387,7 @@
         weighted = (dot(qkv[rows, head_of(head, 0)], qkv[rows, head_of(head, 1)], ((1,), (1,))) * mask).astype(LOW)
         mixed[rows, cols] = dot(weighted, qkv[rows, head_of(head, 2)])
         return 0
-    lax.fori_loop(0, 2 * H, within, 0)
+    each_pair(within)
     scan.each(lambda frm: pltpu.make_async_remote_copy(src_ref=tag, dst_ref=tags_all.at[frm], send_sem=tag_send.at[frm],
         recv_sem=tag_recv.at[frm], device_id=(dp, to(1)), device_id_type=MESH).wait_recv())
     scan.join(tags_all, decays, False)
@@ -396,13 +404,13 @@
         reaching = jnp.where(ids_down[micro] == boundary, jnp.exp(-(row_index() + 1.0) * decays[head]), 0.0)
         mixed[rows, cols] += dot(qkv[rows, head_of(head, 0)], carried[p]) * reaching
         return 0
-    lax.fori_loop(0, 2 * H, crossing, 0)
+    each_pair(crossing)
     keep(mixed, o_mixed)
 
     def gate_rows(rows):
         v = mixed[rows, :]
         gated[rows, :] = (v * rms_factor(v) * pre[rows, 3 * D:4 * D]).astype(LOW)
-    by_rows(ROWS, 16, gate_rows)
+    by_rows(ROWS, 32, gate_rows)
     m_output = w_output.reshape(D, D)
     def output(k, _):
         cols = columns_of(k, 512)
@@ -531,24 +539,40 @@
 
 def accumulate(dst, srcs, dims, out=None):
     target = dst if out is None else out
+    rows, width = dst.shape[-2:]
+    most = max(1, 64 // max(1, rows * width // 1024))
+    cut, inner = len(dims), 1
+    while cut > 0 and inner * dims[cut - 1] <= most:
+        cut -= 1
+        inner *= dims[cut]
+    near = [()]
+    for d in dims[cut:]:
+        near = [at + (i,) for at in near for i in range(d)]
+    def group(lead):
+        places = [lead + at if dims else ... for at in near]
+        totals = []
+        for at in places:
+            total = dst[at].astype(F32)
+            for s in srcs:
+                total = total + s[at].astype(F32)
+            totals.append(total.astype(target.dtype))
+        for at, total in zip(places, totals):
+            target[at] = total
+    count = 1
+    for d in dims[:cut]:
+        count *= d
     def one(k, _):
         idx, rest = [], k
-        for d in dims[::-1]:
-            idx.append(rest % d)
-            rest = rest // d
-        at = tuple(idx[::-1]) if dims else ...
-        total = dst[at].astype(F32)
-        for s in srcs:
-            total = total + s[at].astype(F32)
-        target[at] = total.astype(target.dtype)
-        return 0
-    n = 1
-    for d in dims:
-        n *= d
-    if n == 1:
-        one(0, 0)
+        for m, d in enumerate(dims[:cut][::-1]):
+            last = m == cut - 1
+            idx.append(rest if last else rest % d)
+            rest = rest if last else rest // d
+        group(tuple(idx[::-1]))
+        return 0
+    if count == 1:
+        group((0,) * cut)
     else:
-        lax.fori_loop(0, n, one, 0)
+        lax.fori_loop(0, count, one, 0)
 
 
 class Scatter:
@@ -581,7 +605,7 @@
             axis, fixed = order[stage], order[:stage + 1]
             above, below, across = (moved(self.me, axis, by) for by in (1, -1, 2))
             mine = lambda at, a, b: part_of(held, at, fixed, (), a, b, rows)
-            if stage == 2:
+            if stage > 0:
                 for k, at in enumerate((across, above, below)):
                     self.send(mine(at, lo, hi), self.slot(u, stage, k, lo, hi), u, stage, k, at)
                 continue
@@ -607,12 +631,16 @@
             held, order, rows, lo, mid, hi = self.spans(u)
             fixed = order[:stage + 1]
             mine = part_of(held, self.me, fixed, (), lo, hi, rows)
-            if stage == 2:
+            if stage > 0:
                 came = [self.slot(u, stage, k, lo, hi) for k in range(3)]
                 for k in range(3):
                     self.got(came[k], u, stage, k)
                 span = pl.ds(lo, hi - lo)
-                accumulate(mine, came, (), self.final[BACK_UNITS[u][0]].at[(span, slice(None)) if rows else (slice(None), span)])
+                if stage == 2:
+                    accumulate(mine, came, (), self.final[BACK_UNITS[u][0]].at[(span, slice(None)) if rows else (slice(None), span)])
+                else:
+                    accumulate(mine, came, live_dims(fixed))
+                    self.far((u,), 2)
                 continue
             for k, (a, b) in ((2, (mid, hi)), (3, (lo, mid)), (4, (lo, mid)), (5, (mid, hi))):
                 self.got(self.slot(u, stage, 1 + k % 2, a, b), u, stage, k)
@@ -629,10 +657,11 @@
 
 
 def backward_kernel(*refs):
-    (ids, tags_all, decays, h_x, h_cot, h_qkv, h_slopes, h_gate, h_mixed, h_resid, h_up, h_carried, w_in, w_output, w_up, w_down,
+    (h_ids, h_tags, decays, h_x, h_cot, h_qkv, h_slopes, h_gate, h_mixed, h_resid, h_up, h_carried, w_in, w_output, w_up, w_down,
      t_first, t_gated, t_second, t_product, b_branch) = refs[:21]
-    input_grad, grads = refs[21], refs[22:30]
+    o_input, o_grads = refs[21], refs[22:30]
     refs = refs[30:]
+    input_grad, grads, ids, tags_all, refs = refs[0], refs[1:9], refs[9], refs[10], refs[11:]
     n = len(BACK_UNITS)
     held, refs = refs[:4], refs[4:]
     slots = [refs[k * n:(k + 1) * n] for k in range(3)]
@@ -640,7 +669,7 @@
     final, theirs, refs = refs[:4], refs[4:7], refs[7:]
     (quarters, regroup, wbuf, product_t, lhs_a, lhs_b, branch, cot, d_up, up_sib, d_attn, attn_sib, pre_sib,
      up, qkv, slopes, gate, mixed, resid, x, work, d_mixed, carried, local, came, going, reverse, ids_down, allowed,
-     load_sem, wsem, send_sem, recv_sem, s1, r1, s2, r2, pass_send, pass_recv, end_send, end_recv, q_send, q_recv) = refs
+     load_sem, wsem, send_sem, recv_sem, s1, r1, s2, r2, pass_send, pass_recv, end_send, end_recv, q_send, q_recv, out_sem) = refs
     me = where_am_i()
     sib = moved(me, "c", 1)
     core, other_core = me["c"], sib["c"]
@@ -661,6 +690,8 @@
         cp = pltpu.make_async_copy(src, dst, load_sem.at[len(loads)])
         cp.start()
         loads[name] = cp
+    load("ids", h_ids, ids)
+    load("tags", h_tags, tags_all)
     load("product", t_product, product_t)
     load("branch", b_branch, branch)
     load("cot", h_cot, cot)
@@ -699,6 +730,13 @@
     load("carried", h_carried, carried)
     load("slopes", h_slopes, slopes)
     load("x", h_x, x)
+    kept = []
+    def keep(src, dst):
+        cp = pltpu.make_async_copy(src, dst, out_sem.at[len(kept)])
+        cp.start()
+        kept.append(cp)
+    loads["ids"].wait()
+    loads["tags"].wait()
     for m in range(2):
         below, across = spread(ids[m:m + 1, :])
         ids_down[m] = below
@@ -742,7 +780,6 @@
     def second_left(k, w):
         work[:, columns_of(k, 256)] = dot(d_up[:, 0:FF], w[...], ((1,), (1,)))
     stream(1, second_left)
-    rs.turn(G_DOWN, 0)
 
     def grad_half(i, lhs, own, base, shift, sibling, units):
         out = held[i].reshape(D, HELD[i][1])
@@ -761,10 +798,10 @@
     h_wide.wait_recv()
     grad_half(WIDE, lhs_a, d_up, core * FF, 0, up_sib, G_WIDE)
     load("first", t_first, lhs_a)
-    rs.land(G_DOWN, 0)
     def second_right(k, w):
         work[:, columns_of(k, 256)] += dot(d_up[:, FF:2 * FF], w[...], ((1,), (1,)))
     stream(2, second_right)
+    rs.turn(G_DOWN, 0)
 
     loads["resid"].wait()
     def resid_back(rows):
@@ -773,10 +810,8 @@
         total = cot[rows, :].astype(F32) + norm_back(work[rows, :], v * factor, factor)
         resid[rows, :] = total
         d_attn[rows, :] = total.astype(LOW)
-    by_rows(ROWS, 16, resid_back)
+    by_rows(ROWS, 32, resid_back)
     h_attn = hand(d_attn.at[:, side(other_core, D // 2)], attn_sib)
-    rs.turn(G_DOWN, 1)
-    rs.turn(G_WIDE, 0)
     def gated_back(k, w):
         work[:, columns_of(k, 256)] = dot(d_attn[...], w[...], ((1,), (1,)))
     stream(3, gated_back)
@@ -789,7 +824,7 @@
         g = work[rows, :]
         d_mixed[rows, :] = norm_back(g * gate[rows, :].astype(F32), normed, factor).astype(LOW)
         gate[rows, :] = (g * normed).astype(LOW)
-    by_rows(ROWS, 16, mixed_back)
+    by_rows(ROWS, 32, mixed_back)
     h_gate_out = hand(gate.at[:, side(other_core, D // 2)], pre_sib.at[:, pl.ds(1536, 512)])
     loads["qkv"].wait()
     def back_states(p, _):
@@ -799,16 +834,16 @@
         opened = (qkv[rows, head_of(head, 0)].astype(F32) * opening).astype(LOW)
         local[p] = dot(opened, d_mixed[rows, cols], ((0,), (0,))).astype(LOW)
         return 0
-    lax.fori_loop(0, 2 * H, back_states, 0)
+    each_pair(back_states)
     scan.start()
-    rs.land(G_DOWN, 1)
     loads["gated"].wait()
     h_attn.wait_recv()
     grad_half(OUTPUT, lhs_b, d_attn, core * (D // 2), 0, attn_sib, G_OUTPUT)
     loads["first"].wait()
     h_gate_out.wait_recv()
     grad_half(INPUT, lhs_a, gate, core * (D // 2), 1536, pre_sib, G_GATE)
-    rs.land(G_WIDE, 0)
+    rs.turn(G_WIDE, 0)
+    rs.land(G_DOWN, 0)
     scan.join(tags_all, decays, True)
 
     h_wide.wait_send()
@@ -829,12 +864,8 @@
         work[rows, cols] = dot(d_scores, q, ((0,), (0,)))
         mixed[rows, cols] = dot(weighted, dm, ((0,), (0,)))
         return 0
-    lax.fori_loop(0, 2 * H, pair_back, 0)
+    each_pair(pair_back)
     h_query = hand(d_pre.at[:, side(other_core, D // 2)], pre_sib.at[:, pl.ds(0, 512)])
-    rs.turn(G_OUTPUT, 0)
-    rs.turn(G_GATE, 0)
-    rs.land(G_DOWN, 2)
-    rs.turn(G_WIDE, 1)
     h_query.wait_recv()
     grad_half(INPUT, lhs_a, d_pre, core * (D // 2), 0, pre_sib, G_QUERY)
     scan.finish()
@@ -847,11 +878,11 @@
         d_pre[rows, head_of(head, 1)] = (d_k * slopes[rows, head_of(head, 1)].astype(F32)).astype(LOW)
         d_pre[rows, head_of(head, 2)] = d_v.astype(LOW)
         return 0
-    lax.fori_loop(0, 2 * H, pair_close, 0)
+    each_pair(pair_close)
     h_key = hand(d_pre.at[:, side(other_core, D // 2, D)], pre_sib.at[:, pl.ds(512, 512)])
     h_value = hand(d_pre.at[:, side(other_core, D // 2, 2 * D)], pre_sib.at[:, pl.ds(1024, 512)])
-    rs.land(G_OUTPUT, 0)
-    rs.land(G_GATE, 0)
+    rs.land(G_WIDE, 0)
+    rs.land(G_DOWN, 1)
     h_key.wait_recv()
     h_value.wait_recv()
     out = held[INPUT].reshape(D, 2 * D)
@@ -865,37 +896,39 @@
             out[:, a:a + wide] = (dot(lhs_a[core], mine) + dot(lhs_a[other_core], pre_sib[:, a:a + wide])).astype(LOW)
             a += wide
         rs.far((u,), 0)
+    rs.turn(G_OUTPUT, 0)
+    rs.turn(G_GATE, 0)
     rs.turn(G_QUERY, 0)
-    rs.land(G_WIDE, 1)
     def first_gate(k, w):
         work[:, columns_of(k, 256)] = dot(gate[...], w[...], ((1,), (1,)))
     stream(4, first_gate)
     rs.turn(G_VALUE, 0)
-    rs.turn(G_OUTPUT, 1)
-    rs.turn(G_GATE, 1)
+    rs.land(G_OUTPUT, 0)
+    rs.land(G_GATE, 0)
     rs.land(G_QUERY, 0)
+    rs.land(G_WIDE, 1)
+    rs.land(G_DOWN, 2)
     def first_keys(k, w):
         work[:, columns_of(k, 256)] += dot(d_pre[:, 0:2 * D], w[...], ((1,), (1,)))
     stream(5, first_keys)
     rs.land(G_VALUE, 0)
     rs.land(G_OUTPUT, 1)
     rs.land(G_GATE, 1)
-    rs.turn(G_QUERY, 1)
-    rs.land(G_WIDE, 2)
+    rs.land(G_QUERY, 1)
     def first_values(k, w):
         work[:, columns_of(k, 256)] += dot(d_pre[:, 2 * D:3 * D], w[...], ((1,), (1,)))
     stream(6, first_values)
-    rs.turn(G_VALUE, 1)
-    rs.land(G_QUERY, 1)
+    rs.land(G_VALUE, 1)
+    rs.land(G_WIDE, 2)
     loads["x"].wait()
     def input_back(rows):
         v = x[rows, :].astype(F32)
         factor = rms_factor(v)
         input_grad[rows, :] = resid[rows, :] + norm_back(work[rows, :], v * factor, factor)
-    by_rows(ROWS, 16, input_back)
+    by_rows(ROWS, 32, input_back)
+    keep(input_grad, o_input)
+
     rs.land(G_OUTPUT, 2)
-    rs.land(G_VALUE, 1)
-
     place = me["x"] // 2 * 2 + core
     def owner(j):
         return (dp, me["z"] * 4 + j)
@@ -932,17 +965,24 @@
         for k in range(2):
             t = (j % 2) * 4 + (j // 2) * 2 + k
             grads[7][pl.ds(t, 22, stride=8), :] = regroup[j, 0:22, k * 128:(k + 1) * 128]
+    keep(grads[7], o_grads[7])
     ends[WIDE].wait_recv()
     mine, came = final[WIDE][pl.ds(pl.multiple_of(core * 8, 8), 8), :], theirs[WIDE - 1][...]
     for k, both in enumerate((jnp.where(core == 0, mine, came), jnp.where(core == 0, came, mine))):
         for c in range(22):
             grads[5 + k][pl.ds(c, 8, stride=22), :] = both[:, c * 128:(c + 1) * 128]
+        keep(grads[5 + k], o_grads[5 + k])
     give(OUTPUT, grads[4:5], 512)
+    keep(grads[4], o_grads[4])
     rs.land(G_GATE, 2)
     rs.land(G_QUERY, 2)
     rs.land(G_VALUE, 2)
     swap(INPUT)
     give(INPUT, grads[0:4], 512)
+    for k in range(4):
+        keep(grads[k], o_grads[k])
+    for cp in kept:
+        cp.wait()
     for cp in ends.values():
         cp.wait_send()
     for k in range(1, 4):
@@ -954,12 +994,12 @@
 
 
 def backward(ids, tags_all, decays, arrays):
-    v = pl.BlockSpec(memory_space=pltpu.VMEM)
     anywhere = pl.BlockSpec(memory_space=pl.ANY)
     sds = jax.ShapeDtypeStruct
     vm = pltpu.VMEM
     n = len(BACK_UNITS)
-    scratch = [vm(live_dims(()) + tail, LOW) for tail in HELD]
+    scratch = [vm((ROWS, D), F32)] + [vm((64, 128), F32)] * 5 + [vm((176, 128), F32)] * 3 + [vm((2, HD), F32), vm((N_SEQ, 8, HD), F32)]
+    scratch += [vm(live_dims(()) + tail, LOW) for tail in HELD]
     for stage in range(3):
         for i, s, lo, hi in BACK_UNITS:
             tail = (hi - lo, 256) if i == DOWN else (HELD[i][0], hi - lo)
@@ -970,12 +1010,12 @@
         vm((2, D, ROWS), LOW), vm((2, D, ROWS), LOW), vm((2, ROWS, D // 2), LOW), full(D), full(2 * FF), full(FF), full(D), full(D // 2),
         full(2 * D), full(2 * FF), full(3 * D), full(2 * D), full(D), full(D, F32), full(D, F32), full(D), full(D, F32), full(D)]
     scratch += [vm((N_SEQ, HD, HD), LOW)] * 5 + [vm((2, HD, HD), F32)] * 2
-    scratch += [DMA((16,)), DMA((3,)), DMA((n, 3, 6)), DMA((n, 3, 6))] + [DMA((N_SEQ,))] * 4 + [DMA((6,))] * 2 + [DMA((3,))] * 2 + [DMA((4,))] * 2
+    scratch += [DMA((16,)), DMA((3,)), DMA((n, 3, 6)), DMA((n, 3, 6))] + [DMA((N_SEQ,))] * 4 + [DMA((6,))] * 2 + [DMA((3,))] * 2 + [DMA((4,))] * 2 + [DMA((9,))]
     return pl.pallas_call(
         backward_kernel,
         out_shape=[sds((ROWS, D), F32)] + [sds((64, 128), F32)] * 5 + [sds((176, 128), F32)] * 3,
-        in_specs=[v, v, pl.BlockSpec(memory_space=pltpu.SMEM)] + [anywhere] * len(arrays),
-        out_specs=[v] * 9,
+        in_specs=[anywhere] * 2 + [pl.BlockSpec(memory_space=pltpu.SMEM)] + [anywhere] * len(arrays),
+        out_specs=[anywhere] * 9,
         scratch_shapes=scratch,
         compiler_params=pltpu.CompilerParams(collective_id=1, has_side_effects=True, vmem_limit_bytes=60 << 20),
         name="backward_and_scatter",

time: 220 us -> 206 us (0.936)
  Pallas kernels: 217 us -> 203 us
    pallas_call x1, Pallas kernels: 111 us -> 99.6 us  [backward(): pl.pallas_call(backward_kernel, out_shape=[sds((ROWS, D), F32)] + [sds((6...]
    pallas_call x1, Pallas kernels: 103 us -> 101 us  [forward(): pl.pallas_call(forward_kernel, out_shape=outs, in_specs=[v, v, v, pl.Bloc...]
where the time goes in v5:
time: 206 us
  Pallas kernels  203 us (99%)
    pallas_call x1, Pallas kernels, forward(): pl.pallas_call(forward_kernel, out_shape=outs, in_specs=[v, v, v, pl.Bloc...  101 us
    pallas_call x1, Pallas kernels, backward(): pl.pallas_call(backward_kernel, out_shape=[sds((ROWS, D), F32)] + [sds((6...  99.6 us

profile of v5, /device:TPU:1, one launch (start us, length us, event | category | flops | bytes accessed | tf_op | source)
XLA Modules:
  0.0 205.5 jit_solution(13269146374848071263)
XLA Ops:
  0.6 1.2 convert_bitcast_fusion.refs_2_.refs_0_
  1.9 101.2 %gather_and_forward.1 = (bf16[256,1024]{1,0:T(8,128)(2,1)}, f32[16,8,128]{2,1,0:T(8,128)}, bf16[256,3072]{1,0:T(8,128)(2,1)}, bf16[256,2048]{1,0:T(8,128)(2,1)},...) custom-call(bf16[256,1024]{1,0:T(8,128)(2,1)} %bitcast.32, ...), custom_call_target="tpu_custom_call" | custom-call | tf_op jit(solution)/shard_map/gather_and_forward/pallas_call | solution.py:492
  103.1 99.6 %backward_and_scatter.1 = (f32[256,1024]{1,0:T(8,128)}, f32[64,128]{1,0:T(8,128)}, f32[64,128]{1,0:T(8,128)}, f32[64,128]{1,0:T(8,128)}, f32[64,128]{1,0:T(8,128...) custom-call(f32[2,128]{1,0:T(2,128)} %convert_bitcast_fusion.refs_2_.refs_0_, ...), custom_call_target="tpu_custom_call" | custom-call | tf_op jit(solution)/shard_map/backward_and_scatter/pallas_call | solution.py:1014
  202.7 2.7 %hand_out.1 = (bf16[256,1024]{1,0:T(8,128)(2,1)}, f32[256,1024]{1,0:T(8,128)}, f32[64,128]{1,0:T(8,128)}, f32[64,128]{1,0:T(8,128)}, f32[64,128]{1,0:T(8,128)}, ...) custom-call(bf16[256,1024]{1,0:T(8,128)(2,1)} %get-tuple-element.47., ...), custom_call_target="tpu_custom_call" | custom-call | tf_op jit(solution)/shard_map/hand_out/pallas_call | solution.py:1041

commit v6 on v5

--- a/solution.py
+++ b/solution.py
@@ -27,13 +27,13 @@
 
 
 CHUNKS = (
-    tuple(tiles(0, (0, 10, 20, 32))),
-    tuple(tiles(1, (0, 4, 8)) + tiles(2, (0, 15, 30, 44))),
-    tuple(tiles(3, (0, 7, 14, 22), 8)),
+    tuple(tiles(0, (0, 11, 22, 32))),
+    ((1, 2, 0, 1024),) + tuple(tiles(2, (0, 16, 32, 44))),
+    tuple(tiles(3, (0, 8, 16, 22), 8)),
 )
 UNITS = CHUNKS[0] + CHUNKS[1] + CHUNKS[2]
 C1, C2, C3 = (tuple(UNITS.index(u) for u in chunk) for chunk in CHUNKS)
-C2_FIRST = C2[:2]
+C2_FIRST = C2[:1]
 
 
 def where_am_i():
@@ -125,6 +125,10 @@
     def begin(self, units, stage):
         for u in units:
             a = self.axis(u, stage)
+            if stage == 0:
+                for k, by in enumerate((1, -1, 2)):
+                    self.go(self.copy(self.part(u, self.me, stage), u, k, moved(self.me, a, by)))
+                continue
             for k, (half, by) in enumerate(((0, 1), (1, -1), (1, 1), (0, -1))):
                 self.go(self.copy(self.part(u, self.me, stage, half), u, 6 * stage + k, moved(self.me, a, by)))
             if stage == 2:
@@ -141,6 +145,10 @@
     def finish(self, units, stage):
         for u in units:
             a = self.axis(u, stage)
+            if stage == 0:
+                for k, by in enumerate((-1, 1, 2)):
+                    self.copy(self.part(u, moved(self.me, a, by), stage), u, k, moved(self.me, a, 1)).wait_recv()
+                continue
             for k, by, half in ((2, -1, 1), (3, 1, 0), (4, 2, 0), (5, 2, 1)):
                 self.copy(self.part(u, moved(self.me, a, by), stage, half), u, 6 * stage + k, moved(self.me, a, 1)).wait_recv()
             if stage == 2:
@@ -258,18 +266,18 @@
 
 
 def forward_kernel(*refs):
-    (x, cot, ids, decays), small = refs[:4], refs[4:12]
+    (x, cot, whole_ids, decays), small = refs[:4], refs[4:12]
     (act, tags_all, o_qkv, o_slopes, o_gate, o_mixed, o_resid, o_up, o_carried, o_in, o_output, o_wide, o_down,
      t_first, t_gated, t_second, t_product, b_branch) = refs[12:30]
     (w_in, w_output, w_up, w_flat, w_down, pre, first_in, qkv, slopes, gate, mixed, resid, up, gated, second, product,
      first_t, gated_t, second_t, product_t, carried, local, came, going, spare, tag, allowed, kept_mask, ids_down,
-     send_sem, recv_sem, csend_sem, crecv_sem, tag_send, tag_recv, s1, r1, s2, r2, out_sem, pass_send, pass_recv) = refs[30:]
+     send_sem, recv_sem, csend_sem, crecv_sem, tag_send, tag_recv, s1, r1, s2, r2, out_sem, pass_send, pass_recv, ids) = refs[30:]
     me = where_am_i()
     sib = moved(me, "c", 1)
     seq, dp = lax.axis_index("seq"), lax.axis_index("dp")
     to = lambda k: (seq + k) % N_SEQ
     barrier = pltpu.get_barrier_semaphore()
-    close = neighbours(me)
+    close = neighbours(me) + [moved(me, a, 2) for a in "xyz"]
     for other in close:
         pl.semaphore_signal(barrier, inc=1, device_id=device(other), device_id_type=MESH)
 
@@ -290,6 +298,7 @@
     place(small[5], w_up, 0, FF)
     place(small[6], w_up, FF, FF)
     w_flat[here] = small[7][...]
+    ids[...] = whole_ids[...].astype(F32)
     tag[...] = jnp.zeros((8, HD), F32)
     for m in range(2):
         tag[2 * m:2 * m + 1, :] = jnp.broadcast_to(ids[m:m + 1, 0:1], (1, HD))
@@ -325,9 +334,6 @@
         v = x[rows, :].astype(F32)
         first_in[rows, :] = (v * rms_factor(v)).astype(LOW)
     by_rows(ROWS, 32, norm_in)
-    g.relay(C1, 0)
-    g.relay(C2, 0)
-    g.relay(C3, 0)
     g.advance(C1, 0)
     for m in range(2):
         down, across = spread(ids[m:m + 1, :])
@@ -351,26 +357,22 @@
     keep(w_in, o_in)
 
     m_in = w_in.reshape(D, 4 * D)
-    def project(k, _):
+    def project(k):
         cols = columns_of(k, 512)
         pre[:, cols] = dot(first_in[...], m_in[:, cols])
-        return 0
-    lax.fori_loop(0, 8, project, 0)
-    g.relay(C2, 2)
-    g.advance(C3, 1)
-
-    def rows_of_heads(rows):
-        for k in range(2):
-            u = pre[rows, k * D:(k + 1) * D]
-            s = sigmoid(u)
-            qkv[rows, k * D:(k + 1) * D] = (u * s).astype(LOW)
-            slopes[rows, k * D:(k + 1) * D] = (s * (1.0 + u * (1.0 - s))).astype(LOW)
+    def project_kv(k, _):
+        project(k + 2)
+        return 0
+    lax.fori_loop(0, 4, project_kv, 0)
+    def swish_rows(rows, k):
+        u = pre[rows, k * D:(k + 1) * D]
+        s = sigmoid(u)
+        qkv[rows, k * D:(k + 1) * D] = (u * s).astype(LOW)
+        slopes[rows, k * D:(k + 1) * D] = (s * (1.0 + u * (1.0 - s))).astype(LOW)
+    def rows_kv(rows):
+        swish_rows(rows, 1)
         qkv[rows, 2 * D:3 * D] = pre[rows, 2 * D:3 * D].astype(LOW)
-        gate[rows, :] = pre[rows, 3 * D:4 * D].astype(LOW)
-    by_rows(ROWS, 32, rows_of_heads)
-    keep(qkv, o_qkv)
-    keep(slopes, o_slopes)
-    keep(gate, o_gate)
+    by_rows(ROWS, 32, rows_kv)
 
     def states(p, _):
         micro, head, rows, _ = pair_at(p)
@@ -380,6 +382,19 @@
         return 0
     each_pair(states)
     scan.start()
+    g.relay(C2, 2)
+    g.advance(C3, 1)
+    def project_qg(k, _):
+        project(jnp.where(k < 2, k, k + 4))
+        return 0
+    lax.fori_loop(0, 4, project_qg, 0)
+    def rows_qg(rows):
+        swish_rows(rows, 0)
+        gate[rows, :] = pre[rows, 3 * D:4 * D].astype(LOW)
+    by_rows(ROWS, 32, rows_qg)
+    keep(qkv, o_qkv)
+    keep(slopes, o_slopes)
+    keep(gate, o_gate)
 
     def within(p, _):
         micro, head, rows, cols = pair_at(p)
@@ -427,7 +442,7 @@
     by_rows(ROWS, 32, norm_second)
     hand(gated_t, gated_t, t_gated)
     g.finish(C3, 2)
-    g.arrive(C2[2:])
+    g.arrive(C2[1:])
     keep(w_up, o_wide)
     m_up = w_up.reshape(D, 2 * FF)
     def widen(k, _):
@@ -450,8 +465,10 @@
         for c in range(8):
             w_down[pl.ds(pl.multiple_of(k * 176, 176), 176), c * 128:(c + 1) * 128] = spare[pl.ds(c, 176, stride=8), :].astype(LOW)
         return 0
-    lax.fori_loop(0, 16, arrange, 0)
-    keep(w_down, o_down)
+    for half_at in range(2):
+        lax.fori_loop(8 * half_at, 8 * half_at + 8, arrange, 0)
+        some = pl.ds(half_at * FF // 2, FF // 2)
+        keep(w_down.at[some, :], o_down.at[some, :])
     def last(k, _):
         cols = columns_of(k, 512)
         act[:, cols] = (resid[:, cols] + dot(product[...], w_down[:, cols])).astype(LOW)
@@ -488,7 +505,7 @@
         vm((ROWS, D), F32), vm((ROWS, D), F32), vm((ROWS, 2 * FF), LOW), vm((ROWS, D), LOW), vm((ROWS, D), LOW), vm((ROWS, FF), LOW),
         vm((D, ROWS), LOW), vm((D, ROWS), LOW), vm((D, ROWS), LOW), vm((FF, ROWS), LOW)] + [vm((N_SEQ, HD, HD), LOW)] * 4 + [
         vm((1408, 128), F32), vm((8, HD), F32)] + [vm((2, HD, HD), F32)] * 3 + [
-        DMA((n, 18)), DMA((n, 18)), DMA((n, 4)), DMA((n, 4))] + [DMA((N_SEQ,))] * 6 + [DMA((20,)), DMA((5,)), DMA((5,))]
+        DMA((n, 18)), DMA((n, 18)), DMA((n, 4)), DMA((n, 4))] + [DMA((N_SEQ,))] * 6 + [DMA((20,)), DMA((5,)), DMA((5,)), vm((2, HD), F32)]
     return pl.pallas_call(
         forward_kernel, out_shape=outs,
         in_specs=[v, v, v, pl.BlockSpec(memory_space=pltpu.SMEM)] + [v] * 8,
@@ -508,9 +525,9 @@
 GROUPS = (
     tiles(DOWN, (0, 3, 7, 11), 8),
     tiles(WIDE, (0, 7, 14, 22)),
-    [(OUTPUT, 0, 0, 256), (OUTPUT, 1, 256, 512)],
-    [(INPUT, 1, 1536, 1792), (INPUT, 2, 1792, 2048)],
-    [(INPUT, 2, 0, 256), (INPUT, 0, 256, 512)],
+    [(OUTPUT, 0, 0, 512)],
+    [(INPUT, 1, 1536, 2048)],
+    [(INPUT, 2, 0, 512)],
     [(INPUT, 0, 512, 896), (INPUT, 1, 896, 1280), (INPUT, 2, 1280, 1536)],
 )
 BACK_UNITS = tuple(unit for group in GROUPS for unit in group)
@@ -657,7 +674,7 @@
 
 
 def backward_kernel(*refs):
-    (h_ids, h_tags, decays, h_x, h_cot, h_qkv, h_slopes, h_gate, h_mixed, h_resid, h_up, h_carried, w_in, w_output, w_up, w_down,
+    (whole_ids, h_tags, decays, h_x, h_cot, h_qkv, h_slopes, h_gate, h_mixed, h_resid, h_up, h_carried, w_in, w_output, w_up, w_down,
      t_first, t_gated, t_second, t_product, b_branch) = refs[:21]
     o_input, o_grads = refs[21], refs[22:30]
     refs = refs[30:]
@@ -690,7 +707,7 @@
         cp = pltpu.make_async_copy(src, dst, load_sem.at[len(loads)])
         cp.start()
         loads[name] = cp
-    load("ids", h_ids, ids)
+    ids[...] = whole_ids[...].astype(F32)
     load("tags", h_tags, tags_all)
     load("product", t_product, product_t)
     load("branch", b_branch, branch)
@@ -721,28 +738,16 @@
     piece(0, 0).start()
     piece(0, 1).start()
     load("up", h_up, up)
-    load("resid", h_resid, resid)
-    load("mixed", h_mixed, mixed)
-    load("gate", h_gate, gate)
-    load("qkv", h_qkv, qkv)
-    load("second", t_second, lhs_a)
-    load("gated", t_gated, lhs_b)
-    load("carried", h_carried, carried)
-    load("slopes", h_slopes, slopes)
-    load("x", h_x, x)
     kept = []
     def keep(src, dst):
         cp = pltpu.make_async_copy(src, dst, out_sem.at[len(kept)])
         cp.start()
         kept.append(cp)
-    loads["ids"].wait()
     loads["tags"].wait()
     for m in range(2):
         below, across = spread(ids[m:m + 1, :])
         ids_down[m] = below
         allowed[m] = jnp.where((below == across) & (row_index() >= column_index()), 1.0, 0.0)
-    pl.semaphore_wait(barrier, len(close) + N_SEQ - 1)
-
     rs = Scatter(held, slots, final, me, send_sem, recv_sem)
     scan = Scan(local, came, going, reverse, (s1, r1, s2, r2))
     passed = []
@@ -765,7 +770,9 @@
                 held[DOWN][k // 2, k % 2, i, j] = total[i * 88:(i + 1) * 88].astype(LOW)
         return 0
     lax.fori_loop(0, 8, down_rows, 0)
+    pl.semaphore_wait(barrier, len(close) + N_SEQ - 1)
     rs.far(G_DOWN, 0)
+    load("second", t_second, lhs_a)
 
     loads["cot"].wait()
     loads["up"].wait()
@@ -777,10 +784,14 @@
     stream(0, up_back)
     side = lambda c, width, base=0: pl.ds(pl.multiple_of(c * width + base, 128), width)
     h_wide = hand(d_up.at[:, side(other_core, FF)], up_sib)
-    def second_left(k, w):
-        work[:, columns_of(k, 256)] = dot(d_up[:, 0:FF], w[...], ((1,), (1,)))
-    stream(1, second_left)
-
+    load("resid", h_resid, resid)
+    load("mixed", h_mixed, mixed)
+    load("gate", h_gate, gate)
+    load("qkv", h_qkv, qkv)
+    load("gated", t_gated, lhs_b)
+    load("carried", h_carried, carried)
+    load("slopes", h_slopes, slopes)
+    load("x", h_x, x)
     def grad_half(i, lhs, own, base, shift, sibling, units):
         out = held[i].reshape(D, HELD[i][1])
         for u in units:
@@ -798,6 +809,9 @@
     h_wide.wait_recv()
     grad_half(WIDE, lhs_a, d_up, core * FF, 0, up_sib, G_WIDE)
     load("first", t_first, lhs_a)
+    def second_left(k, w):
+        work[:, columns_of(k, 256)] = dot(d_up[:, 0:FF], w[...], ((1,), (1,)))
+    stream(1, second_left)
     def second_right(k, w):
         work[:, columns_of(k, 256)] += dot(d_up[:, FF:2 * FF], w[...], ((1,), (1,)))
     stream(2, second_right)
@@ -1014,7 +1028,7 @@
     return pl.pallas_call(
         backward_kernel,
         out_shape=[sds((ROWS, D), F32)] + [sds((64, 128), F32)] * 5 + [sds((176, 128), F32)] * 3,
-        in_specs=[anywhere] * 2 + [pl.BlockSpec(memory_space=pltpu.SMEM)] + [anywhere] * len(arrays),
+        in_specs=[pl.BlockSpec(memory_space=pltpu.VMEM), anywhere, pl.BlockSpec(memory_space=pltpu.SMEM)] + [anywhere] * len(arrays),
         out_specs=[anywhere] * 9,
         scratch_shapes=scratch,
         compiler_params=pltpu.CompilerParams(collective_id=1, has_side_effects=True, vmem_limit_bytes=60 << 20),
@@ -1025,15 +1039,21 @@
 def copy_kernel(*refs):
     n = len(refs) // 3
     sems = refs[-1]
-    into = [pltpu.make_async_copy(refs[k], refs[2 * n + k], sems.at[0, k]) for k in range(n)]
-    out = [pltpu.make_async_copy(refs[2 * n + k], refs[n + k], sems.at[1, k]) for k in range(n)]
-    for cp in into:
-        cp.start()
-    for a, b in zip(into, out):
-        a.wait()
-        b.start()
-    for cp in out:
-        cp.wait()
+    steps = []
+    for k in range(n):
+        src, dst, via = refs[k], refs[n + k], refs[2 * n + k]
+        pieces = [pl.ds(r, 64) for r in range(0, src.shape[0], 64)] if src.shape[0] == ROWS else [slice(None)]
+        for piece in pieces:
+            at = len(steps)
+            steps.append((pltpu.make_async_copy(src.at[piece], via.at[piece], sems.at[0, at]),
+                pltpu.make_async_copy(via.at[piece], dst.at[piece], sems.at[1, at])))
+    for into, _ in steps:
+        into.start()
+    for into, out in steps:
+        into.wait()
+        out.start()
+    for _, out in steps:
+        out.wait()
 
 
 def hand_out(arrays):
@@ -1041,13 +1061,13 @@
     return pl.pallas_call(
         copy_kernel, out_shape=[jax.ShapeDtypeStruct(a.shape, a.dtype) for a in arrays],
         in_specs=[anywhere] * len(arrays), out_specs=[anywhere] * len(arrays),
-        scratch_shapes=[pltpu.VMEM(a.shape, a.dtype) for a in arrays] + [DMA((2, len(arrays)))], name="hand_out",
+        scratch_shapes=[pltpu.VMEM(a.shape, a.dtype) for a in arrays] + [DMA((2, 16))], name="hand_out",
     )(*arrays)
 
 
 def on_device(hidden_in, seg_ids, decay_rates, grad_out, *weights):
     x, cot = hidden_in.reshape(ROWS, D), grad_out.reshape(ROWS, D)
-    ids = seg_ids.reshape(2, HD).astype(F32)
+    ids = seg_ids.reshape(2, HD)
     (act, tags_all, qkv, slopes, gate, mixed, resid, up, carried, w_in, w_output, w_up, w_down, t_first, t_gated, t_second,
      t_product, b_branch) = forward(x, cot, ids, decay_rates, [w.reshape(-1, 128) for w in weights])
     input_grad, *grads = backward(ids, tags_all, decay_rates, [

time: 206 us -> 198 us (0.961)
  Pallas kernels: 203 us -> 197 us
    pallas_call x1, Pallas kernels: 101 us -> 95.2 us  [forward(): pl.pallas_call(forward_kernel, out_shape=outs, in_specs=[v, v, v, pl.Bloc...]
where the time goes in v6:
time: 198 us; the launch traced here: 197 us
  Pallas kernels  197 us (99%)
    pallas_call x1, Pallas kernels, backward(): pl.pallas_call(backward_kernel, out_shape=[sds((ROWS, D), F32)] + [sds((6...  98.7 us
    pallas_call x1, Pallas kernels, forward(): pl.pallas_call(forward_kernel, out_shape=outs, in_specs=[v, v, v, pl.Bloc...  95.2 us

profile of v6, /device:TPU:1, one launch (start us, length us, event | category | flops | bytes accessed | tf_op | source)
XLA Modules:
  0.0 197.3 jit_solution(16175343260530183808)
XLA Ops:
  0.6 95.2 %gather_and_forward.1 = (bf16[256,1024]{1,0:T(8,128)(2,1)}, f32[16,8,128]{2,1,0:T(8,128)}, bf16[256,3072]{1,0:T(8,128)(2,1)}, bf16[256,2048]{1,0:T(8,128)(2,1)},...) custom-call(bf16[256,1024]{1,0:T(8,128)(2,1)} %bitcast.30, ...), custom_call_target="tpu_custom_call" | custom-call | tf_op jit(solution)/shard_map/gather_and_forward/pallas_call | solution.py:509
  95.9 98.7 %backward_and_scatter.1 = (f32[256,1024]{1,0:T(8,128)}, f32[64,128]{1,0:T(8,128)}, f32[64,128]{1,0:T(8,128)}, f32[64,128]{1,0:T(8,128)}, f32[64,128]{1,0:T(8,128...) custom-call(s32[2,128]{1,0:T(2,128)} %bitcast.44, ...), custom_call_target="tpu_custom_call" | custom-call | tf_op jit(solution)/shard_map/backward_and_scatter/pallas_call | solution.py:1028
  194.6 2.6 %hand_out.1 = (bf16[256,1024]{1,0:T(8,128)(2,1)}, f32[256,1024]{1,0:T(8,128)}, f32[64,128]{1,0:T(8,128)}, f32[64,128]{1,0:T(8,128)}, f32[64,128]{1,0:T(8,128)}, ...) custom-call(bf16[256,1024]{1,0:T(8,128)(2,1)} %get-tuple-element.47., ...), custom_call_target="tpu_custom_call" | custom-call | tf_op jit(solution)/shard_map/hand_out/pallas_call | solution.py:1061

commit v7 on v6

--- a/solution.py
+++ b/solution.py
@@ -622,7 +622,7 @@
             axis, fixed = order[stage], order[:stage + 1]
             above, below, across = (moved(self.me, axis, by) for by in (1, -1, 2))
             mine = lambda at, a, b: part_of(held, at, fixed, (), a, b, rows)
-            if stage > 0:
+            if stage == 2 or stage == 1 and u not in G_WIDE:
                 for k, at in enumerate((across, above, below)):
                     self.send(mine(at, lo, hi), self.slot(u, stage, k, lo, hi), u, stage, k, at)
                 continue
@@ -648,7 +648,7 @@
             held, order, rows, lo, mid, hi = self.spans(u)
             fixed = order[:stage + 1]
             mine = part_of(held, self.me, fixed, (), lo, hi, rows)
-            if stage > 0:
+            if stage == 2 or stage == 1 and u not in G_WIDE:
                 came = [self.slot(u, stage, k, lo, hi) for k in range(3)]
                 for k in range(3):
                     self.got(came[k], u, stage, k)
@@ -916,6 +916,7 @@
     def first_gate(k, w):
         work[:, columns_of(k, 256)] = dot(gate[...], w[...], ((1,), (1,)))
     stream(4, first_gate)
+    rs.turn(G_WIDE, 1)
     rs.turn(G_VALUE, 0)
     rs.land(G_OUTPUT, 0)
     rs.land(G_GATE, 0)

time: 198 us -> 195 us (0.985)
  Pallas kernels: 197 us -> 194 us
    pallas_call x1, Pallas kernels: 98.7 us -> 95.8 us  [backward(): pl.pallas_call(backward_kernel, out_shape=[sds((ROWS, D), F32)] + [sds((6...]
where the time goes in v7:
time: 195 us; the launch traced here: 194 us
  Pallas kernels  194 us (99%)
    pallas_call x1, Pallas kernels, backward(): pl.pallas_call(backward_kernel, out_shape=[sds((ROWS, D), F32)] + [sds((6...  95.8 us
    pallas_call x1, Pallas kernels, forward(): pl.pallas_call(forward_kernel, out_shape=outs, in_specs=[v, v, v, pl.Bloc...  95.2 us

profile of v7, /device:TPU:1, one launch (start us, length us, event | category | flops | bytes accessed | tf_op | source)
XLA Modules:
  0.0 194.4 jit_solution(7391146219155262232)
XLA Ops:
  0.6 95.2 %gather_and_forward.1 = (bf16[256,1024]{1,0:T(8,128)(2,1)}, f32[16,8,128]{2,1,0:T(8,128)}, bf16[256,3072]{1,0:T(8,128)(2,1)}, bf16[256,2048]{1,0:T(8,128)(2,1)},...) custom-call(bf16[256,1024]{1,0:T(8,128)(2,1)} %bitcast.30, ...), custom_call_target="tpu_custom_call" | custom-call | tf_op jit(solution)/shard_map/gather_and_forward/pallas_call | solution.py:509
  95.9 95.8 %backward_and_scatter.1 = (f32[256,1024]{1,0:T(8,128)}, f32[64,128]{1,0:T(8,128)}, f32[64,128]{1,0:T(8,128)}, f32[64,128]{1,0:T(8,128)}, f32[64,128]{1,0:T(8,128...) custom-call(s32[2,128]{1,0:T(2,128)} %bitcast.44, ...), custom_call_target="tpu_custom_call" | custom-call | tf_op jit(solution)/shard_map/backward_and_scatter/pallas_call | solution.py:1029
  191.7 2.6 %hand_out.1 = (bf16[256,1024]{1,0:T(8,128)(2,1)}, f32[256,1024]{1,0:T(8,128)}, f32[64,128]{1,0:T(8,128)}, f32[64,128]{1,0:T(8,128)}, f32[64,128]{1,0:T(8,128)}, ...) custom-call(bf16[256,1024]{1,0:T(8,128)(2,1)} %get-tuple-element.47., ...), custom_call_target="tpu_custom_call" | custom-call | tf_op jit(solution)/shard_map/hand_out/pallas_call | solution.py:1062
